TPU v7x, 32 devices: a whole 2x2x4 slice. The times are simulated.
32 devices in a mesh: seq: 16 (over z, x, core), head: 2 (over y).
Axes of the slice: x: 2, y: 2, z: 4, core: 2. Of those that a mesh axis runs over, the one named last changes fastest.
Arguments:
- tokens: bfloat16 [8192, 4096], P('seq'), may hold values from -18 to 18
- norm_gain: float32 [4096], replicated, may hold values from 0.5 to 1.5
- w_query: bfloat16 [4096, 2048], P(None, 'head'), may hold values from -0.0625 to 0.0625
- w_key: bfloat16 [4096, 512], P(None, 'head'), may hold values from -1.90625 to 1.90625
- w_value: bfloat16 [4096, 512], P(None, 'head'), may hold values from -0.09375 to 0.09375
- w_out: bfloat16 [2048, 4096], P('head'), may hold values from -0.125 to 0.125
- window: int32 [16], P('head'), may hold values from 256 to 4096, as said below
- sink_count: int32 [16], P('head'), may hold values from 1 to 4, as said below
- sink_bias: float32 [16], P('head'), may hold values from 4 to 8
Outputs:
- mixed: bfloat16 [8192, 4096], P('seq', 'head')
Inputs may be any that keep to these rules, and one draw needn't show every extreme that they name: Some head's window is exactly 4096. `sink_count`: some head's count is exactly 4.
All inputs are finite; a program needn't handle non-finite values.
Results may differ from a plain program's by a relative error of at most 0.0071.
Values may be sent and summed in bfloat16 or wider, within the bound.
No kernel may reach another device: no remote copies, remote signals or barrier semaphores. Data moves between devices by JAX's collectives and lax.ppermute only.
A program may use at most 128 MiB of HBM per device.

v0:
```python
import jax
import jax.numpy as jnp
from jax import lax
from jax.sharding import PartitionSpec as P

HEAD_DIM = 128
SINK = 4
SPAN = 9


EPSILON = 1e-05


def from_root(block, axis, holder):
    block = jnp.where(lax.axis_index(axis) == holder, block, jnp.zeros_like(block))
    return lax.psum(block, axis)


def shifted(shard, axis, by):
    peers = lax.axis_size(axis)
    pairs = [(i, i + by) for i in range(peers) if 0 <= i + by < peers]
    return lax.ppermute(shard, axis, pairs)


def normalize(tokens, norm_gain):
    widened = tokens.astype(jnp.float32)
    row_scale = lax.rsqrt(jnp.mean(widened * widened, axis=1, keepdims=True) + EPSILON)
    return (widened, (widened * row_scale * norm_gain).astype(jnp.bfloat16))


def attend(
    queries,
    block_keys,
    block_values,
    anchor_key_rows,
    anchor_value_rows,
    query_start,
    key_start,
    window,
    sink_count,
    sink_bias,
):
    tok_rows, heads_here, head_width = queries.shape
    key_rows, groups_here, _ = block_keys.shape
    per_group = heads_here // groups_here
    softmax_scale = head_width ** (-0.5)
    query_pos = (query_start + jnp.arange(tok_rows, dtype=jnp.int32))[:, None]
    key_pos = (key_start + jnp.arange(key_rows, dtype=jnp.int32))[None, :]
    sink_pos = jnp.arange(anchor_key_rows.shape[0], dtype=jnp.int32)[None, :]

    def one_head(index):
        group = index // per_group
        head_queries = lax.dynamic_index_in_dim(queries, index, 1, keepdims=False)
        head_keys = lax.dynamic_index_in_dim(block_keys, group, 1, keepdims=False)
        head_values = lax.dynamic_index_in_dim(block_values, group, 1, keepdims=False)
        head_sink_keys = lax.dynamic_index_in_dim(anchor_key_rows, group, 1, keepdims=False)
        head_sink_values = lax.dynamic_index_in_dim(anchor_value_rows, group, 1, keepdims=False)
        reach_rows = window[index]
        open_sinks = sink_count[index]
        scores = (
            jnp.einsum("te,le->tl", head_queries, head_keys, preferred_element_type=jnp.float32)
            * softmax_scale
        )
        anchor_score_rows = (
            jnp.einsum(
                "te,se->ts", head_queries, head_sink_keys, preferred_element_type=jnp.float32
            )
            * softmax_scale
        )
        anchor_score_rows = anchor_score_rows + sink_bias[index]
        visible = (key_pos <= query_pos) & (key_pos > query_pos - reach_rows) & (key_pos >= 0)
        sink_open = (sink_pos < open_sinks) & (sink_pos <= query_pos - reach_rows)
        scores = jnp.where(visible, scores, -1e30)
        anchor_score_rows = jnp.where(sink_open, anchor_score_rows, -1e30)
        peak_score = jnp.maximum(
            jnp.max(scores, axis=1, keepdims=True),
            jnp.max(anchor_score_rows, axis=1, keepdims=True),
        )
        weights = jnp.exp(scores - peak_score)
        anchor_weight_rows = jnp.exp(anchor_score_rows - peak_score)
        denominator = jnp.sum(weights, axis=1, keepdims=True) + jnp.sum(
            anchor_weight_rows, axis=1, keepdims=True
        )
        weights = (weights / denominator).astype(jnp.bfloat16)
        anchor_weight_rows = (anchor_weight_rows / denominator).astype(jnp.bfloat16)
        merged_scores = jnp.einsum(
            "tl,le->te", weights, head_values, preferred_element_type=jnp.float32
        )
        merged_scores = merged_scores + jnp.einsum(
            "ts,se->te", anchor_weight_rows, head_sink_values, preferred_element_type=jnp.float32
        )
        return merged_scores.astype(jnp.bfloat16)

    per_head = lax.map(one_head, jnp.arange(heads_here, dtype=jnp.int32))
    return jnp.transpose(per_head, (1, 0, 2)).reshape(tok_rows, heads_here * head_width)


def local(tokens, norm_gain, w_query, w_key, w_value, w_out, window, sink_count, sink_bias):
    widened, normed = normalize(tokens, norm_gain)
    tok_rows = tokens.shape[0]
    heads_here = w_query.shape[1] // HEAD_DIM
    groups_here = w_key.shape[1] // HEAD_DIM
    queries = (
        jnp.dot(normed, w_query, preferred_element_type=jnp.float32)
        .astype(jnp.bfloat16)
        .reshape(tok_rows, heads_here, HEAD_DIM)
    )
    key_value = jnp.stack(
        [
            jnp.dot(normed, w_key, preferred_element_type=jnp.float32).astype(jnp.bfloat16),
            jnp.dot(normed, w_value, preferred_element_type=jnp.float32).astype(jnp.bfloat16),
        ]
    )
    sink_pair = from_root(key_value[:, :SINK], "seq", 0)
    buffer = jnp.zeros((2, SPAN * tok_rows, key_value.shape[2]), jnp.bfloat16)
    buffer = lax.dynamic_update_slice_in_dim(buffer, key_value, (SPAN - 1) * tok_rows, 1)

    def advance(offset, loop_state):
        gathered, moving = loop_state
        moving = shifted(moving, "seq", 1)
        gathered = lax.dynamic_update_slice_in_dim(
            gathered, moving, (SPAN - 2 - offset) * tok_rows, 1
        )
        return (gathered, moving)

    buffer, _ = lax.fori_loop(0, SPAN - 1, advance, (buffer, key_value))
    block_index = lax.axis_index("seq")
    query_start = block_index * tok_rows
    key_start = query_start - (SPAN - 1) * tok_rows
    key_rows = SPAN * tok_rows
    attended = attend(
        queries,
        buffer[0].reshape(key_rows, groups_here, HEAD_DIM),
        buffer[1].reshape(key_rows, groups_here, HEAD_DIM),
        sink_pair[0].reshape(SINK, groups_here, HEAD_DIM),
        sink_pair[1].reshape(SINK, groups_here, HEAD_DIM),
        query_start,
        key_start,
        window,
        sink_count,
        sink_bias,
    )
    partial_value = (
        jnp.dot(attended, w_out, preferred_element_type=jnp.float32)
        .astype(jnp.bfloat16)
        .astype(jnp.float32)
    )
    summed = lax.psum_scatter(
        partial_value.astype(jnp.bfloat16), "head", scatter_dimension=1, tiled=True
    ).astype(jnp.float32)
    share_width = summed.shape[1]
    residual = lax.dynamic_slice_in_dim(
        widened, lax.axis_index("head") * share_width, share_width, 1
    )
    return (residual + summed).astype(jnp.bfloat16)


def solution(mesh):
    in_specs = (
        P("seq", None),
        P(),
        P(None, "head"),
        P(None, "head"),
        P(None, "head"),
        P("head", None),
        P("head"),
        P("head"),
        P("head"),
    )
    out_specs = P("seq", "head")
    return jax.shard_map(local, mesh=mesh, in_specs=in_specs, out_specs=out_specs, check_vma=False)
```

profile of v0, /device:TPU:18, one launch (start us, length us, event | category | flops | bytes accessed | tf_op | source)
XLA Modules:
  0.0 369.7 jit_solution(8411604665070656211)
XLA Ops:
  6.5 3.2 multiply_reduce_fusion
  9.8 3.7 fusion.32
  15.3 2.4 dynamic_update_slice.17
  17.8 91.0 %while.29 = (s32[]{:T(128)}, bf16[2,4608,256]{2,1,0:T(8,128)(2,1)}, bf16[2,512,256]{2,1,0:T(8,128)(2,1)S(1)}, s32[]{:T(128)}, s32[]{:T(128)}, /*index=5*/s32[]{:T(128)}, s32[]{:T(128)}, s32[]{:T(128)}) while((s32[]{:T(128)}, bf16[2,4608,256]{2,1,0:T(8,128)(2,1)}, bf16[2,512,256]{2,1,0:T(8,128)(2,1)S(1)}, s32[]{:T(128)}, s32[]{:T(128)}, ...), condition=%wide.region_2.3_spmd, body=%wide.region_1.2_spmd.sunk | while | flops 7 | bytes 4194491 | solution.py:126
  17.8 1.9 collective-permute-start
  19.7 8.6 %collective-permute-done = bf16[2,512,256]{2,1,0:T(8,128)(2,1)S(1)} collective-permute-done((bf16[2,512,256]{2,1,0:T(8,128)(2,1)S(1)}, bf16[2,512,256]{2,1,0:T(8,128)(2,1)S(1)}, u32[]{:S(2)}, u32[]{:S(2)}) %collective-permute-start) | collective-permute-done | bytes 524320 | tf_op jit(solution)/shard_map/while/body/eval_jaxpr/ppermute | solution.py:22
  29.1 1.9 collective-permute-start
  31.1 8.6 %collective-permute-done = bf16[2,512,256]{2,1,0:T(8,128)(2,1)S(1)} collective-permute-done((bf16[2,512,256]{2,1,0:T(8,128)(2,1)S(1)}, bf16[2,512,256]{2,1,0:T(8,128)(2,1)S(1)}, u32[]{:S(2)}, u32[]{:S(2)}) %collective-permute-start) | collective-permute-done | bytes 524320 | tf_op jit(solution)/shard_map/while/body/eval_jaxpr/ppermute | solution.py:22
  40.5 2.0 collective-permute-start
  42.5 8.5 %collective-permute-done = bf16[2,512,256]{2,1,0:T(8,128)(2,1)S(1)} collective-permute-done((bf16[2,512,256]{2,1,0:T(8,128)(2,1)S(1)}, bf16[2,512,256]{2,1,0:T(8,128)(2,1)S(1)}, u32[]{:S(2)}, u32[]{:S(2)}) %collective-permute-start) | collective-permute-done | bytes 524320 | tf_op jit(solution)/shard_map/while/body/eval_jaxpr/ppermute | solution.py:22
  51.9 2.9 collective-permute-start
  54.8 7.6 %collective-permute-done = bf16[2,512,256]{2,1,0:T(8,128)(2,1)S(1)} collective-permute-done((bf16[2,512,256]{2,1,0:T(8,128)(2,1)S(1)}, bf16[2,512,256]{2,1,0:T(8,128)(2,1)S(1)}, u32[]{:S(2)}, u32[]{:S(2)}) %collective-permute-start) | collective-permute-done | bytes 524320 | tf_op jit(solution)/shard_map/while/body/eval_jaxpr/ppermute | solution.py:22
  63.2 3.8 %collective-permute-start = (bf16[2,512,256]{2,1,0:T(8,128)(2,1)S(1)}, bf16[2,512,256]{2,1,0:T(8,128)(2,1)S(1)}, u32[]{:S(2)}, u32[]{:S(2)}) collective-permute-start(bf16[2,512,256]{2,1,0:T(8,128)(2,1)S(1)} %get-tuple-element.494), channel_id=1, source_target_pairs={{0,2},{2,4},{4,6},{6,8},{8,10},{10,12},{12,14},{14,16},{16,18},{18... | collective-permute-start | bytes 1572872 | tf_op jit(solution)/shard_map/while/body/eval_jaxpr/ppermute | solution.py:22
  67.0 6.7 %collective-permute-done = bf16[2,512,256]{2,1,0:T(8,128)(2,1)S(1)} collective-permute-done((bf16[2,512,256]{2,1,0:T(8,128)(2,1)S(1)}, bf16[2,512,256]{2,1,0:T(8,128)(2,1)S(1)}, u32[]{:S(2)}, u32[]{:S(2)}) %collective-permute-start) | collective-permute-done | bytes 524320 | tf_op jit(solution)/shard_map/while/body/eval_jaxpr/ppermute | solution.py:22
  74.6 4.7 %collective-permute-start = (bf16[2,512,256]{2,1,0:T(8,128)(2,1)S(1)}, bf16[2,512,256]{2,1,0:T(8,128)(2,1)S(1)}, u32[]{:S(2)}, u32[]{:S(2)}) collective-permute-start(bf16[2,512,256]{2,1,0:T(8,128)(2,1)S(1)} %get-tuple-element.494), channel_id=1, source_target_pairs={{0,2},{2,4},{4,6},{6,8},{8,10},{10,12},{12,14},{14,16},{16,18},{18... | collective-permute-start | bytes 1572872 | tf_op jit(solution)/shard_map/while/body/eval_jaxpr/ppermute | solution.py:22
  79.3 5.8 %collective-permute-done = bf16[2,512,256]{2,1,0:T(8,128)(2,1)S(1)} collective-permute-done((bf16[2,512,256]{2,1,0:T(8,128)(2,1)S(1)}, bf16[2,512,256]{2,1,0:T(8,128)(2,1)S(1)}, u32[]{:S(2)}, u32[]{:S(2)}) %collective-permute-start) | collective-permute-done | bytes 524320 | tf_op jit(solution)/shard_map/while/body/eval_jaxpr/ppermute | solution.py:22
  86.0 5.6 %collective-permute-start = (bf16[2,512,256]{2,1,0:T(8,128)(2,1)S(1)}, bf16[2,512,256]{2,1,0:T(8,128)(2,1)S(1)}, u32[]{:S(2)}, u32[]{:S(2)}) collective-permute-start(bf16[2,512,256]{2,1,0:T(8,128)(2,1)S(1)} %get-tuple-element.494), channel_id=1, source_target_pairs={{0,2},{2,4},{4,6},{6,8},{8,10},{10,12},{12,14},{14,16},{16,18},{18... | collective-permute-start | bytes 1572872 | tf_op jit(solution)/shard_map/while/body/eval_jaxpr/ppermute | solution.py:22
  91.6 4.9 %collective-permute-done = bf16[2,512,256]{2,1,0:T(8,128)(2,1)S(1)} collective-permute-done((bf16[2,512,256]{2,1,0:T(8,128)(2,1)S(1)}, bf16[2,512,256]{2,1,0:T(8,128)(2,1)S(1)}, u32[]{:S(2)}, u32[]{:S(2)}) %collective-permute-start) | collective-permute-done | bytes 524320 | tf_op jit(solution)/shard_map/while/body/eval_jaxpr/ppermute | solution.py:22
  97.3 6.5 %collective-permute-start = (bf16[2,512,256]{2,1,0:T(8,128)(2,1)S(1)}, bf16[2,512,256]{2,1,0:T(8,128)(2,1)S(1)}, u32[]{:S(2)}, u32[]{:S(2)}) collective-permute-start(bf16[2,512,256]{2,1,0:T(8,128)(2,1)S(1)} %get-tuple-element.494), channel_id=1, source_target_pairs={{0,2},{2,4},{4,6},{6,8},{8,10},{10,12},{12,14},{14,16},{16,18},{18... | collective-permute-start | bytes 1572872 | tf_op jit(solution)/shard_map/while/body/eval_jaxpr/ppermute | solution.py:22
  103.8 4.0 %collective-permute-done = bf16[2,512,256]{2,1,0:T(8,128)(2,1)S(1)} collective-permute-done((bf16[2,512,256]{2,1,0:T(8,128)(2,1)S(1)}, bf16[2,512,256]{2,1,0:T(8,128)(2,1)S(1)}, u32[]{:S(2)}, u32[]{:S(2)}) %collective-permute-start) | collective-permute-done | bytes 524320 | tf_op jit(solution)/shard_map/while/body/eval_jaxpr/ppermute | solution.py:22
  108.7 6.7 %copy.14 = bf16[2,4608,256]{1,2,0:T(8,128)(2,1)} copy(bf16[2,4608,256]{2,1,0:T(8,128)(2,1)} %get-tuple-element.246) | data formatting | bytes 9437184 | tf_op jit(solution)/shard_map/while | solution.py:126
  115.4 4.8 %fusion.38 = (bf16[1,4608,256]{1,2,0:T(8,128)(2,1)}, bf16[1,4608,256]{1,2,0:T(8,128)(2,1)}) fusion(bf16[2,4608,256]{1,2,0:T(8,128)(2,1)} %copy.14), kind=kLoop, calls=%fused_computation.64 | loop fusion | bytes 9437184 | tf_op jit(solution)/shard_map/slice | solution.py:134
  120.2 27.4 %psum.7 = bf16[2,4,256]{2,1,0:T(4,128)(2,1)S(1)} all-reduce(bf16[2,4,256]{2,1,0:T(4,128)(2,1)S(1)} %fusion.35), channel_id=1, replica_groups=mesh['seq'=16,'head'=2] {'seq'}, use_global_device_ids=true, to_apply=%region_3.4 | all-reduce | flops 2048 | bytes 8192 | tf_op jit(solution)/shard_map/psum | solution.py:16
  147.7 9.2 %fusion.31 = bf16[64,8,8,128]{3,2,1,0:T(8,128)(2,1)S(1)} fusion(bf16[4096,1024]{1,0:T(8,128)(2,1)} %param.15, f32[4096]{0:T(1024)S(1)} %copy-done.5, f32[512]{0:T(512)S(1)} %add_rsqrt_fusion, bf16[512,4096]{1,0:T(8,128)(2,1)} %param.13), kind=kOutput, calls=%fused_computation.48 | convolution fusion | flops 4303880192 | bytes 13649920 | tf_op jit(solution)/shard_map/dot_general | solution.py:104
  157.2 134.6 %while.30 = (s32[]{:T(128)}, bf16[8,512,128]{1,2,0:T(8,128)(2,1)S(1)}, s32[8]{0:T(128)S(1)}, s32[8]{0:T(128)S(1)}, bf16[512,8,128]{2,0,1:T(8,128)(2,1)S(1)}, /*i...) while((s32[]{:T(128)}, ...), condition=%wide.region_9.10_spmd.clone.clone, body=%wide.region_4.9_spmd.clone.clone.sunk | while | flops 1237482496 | bytes 41689596 | solution.py:94
  163.2 4.4 %fusion.54 = (f32[512]{0:T(512)S(1)}, f32[512,4608]{1,0:T(8,128)S(1)}) fusion(bf16[4608,2,128]{0,2,1:T(8,128)(2,1)} %get-tuple-element.551, s32[]{:T(128)S(6)} %select_n.84, bf16[512,8,128]{2,0,1:T(8,128)(2,1)S(1)} %get-tuple-element.550, s32[]{:T(128)S(6)} %select_n.85, pred[4608]{0:T(1024)(128)(4,1)S(1)} %broadcast_compare_fusion.2, ...), kind=kOutput, calls=%fused_computation.62.clone.1 | convolution fusion | flops 620494336 | bytes 10779656 | tf_op jit(solution)/shard_map/while/body/eval_jaxpr/te,le->tl/dot_general | solution.py:61
  170.5 1.4 fusion.56
  172.1 1.6 fusion.58
  180.0 4.5 %fusion.54 = (f32[512]{0:T(512)S(1)}, f32[512,4608]{1,0:T(8,128)S(1)}) fusion(bf16[4608,2,128]{0,2,1:T(8,128)(2,1)} %get-tuple-element.551, s32[]{:T(128)S(6)} %select_n.84, bf16[512,8,128]{2,0,1:T(8,128)(2,1)S(1)} %get-tuple-element.550, s32[]{:T(128)S(6)} %select_n.85, pred[4608]{0:T(1024)(128)(4,1)S(1)} %broadcast_compare_fusion.2, ...), kind=kOutput, calls=%fused_computation.62.clone.1 | convolution fusion | flops 620494336 | bytes 10779656 | tf_op jit(solution)/shard_map/while/body/eval_jaxpr/te,le->tl/dot_general | solution.py:61
  187.3 1.4 fusion.56
  188.9 1.6 fusion.58
  196.8 4.5 %fusion.54 = (f32[512]{0:T(512)S(1)}, f32[512,4608]{1,0:T(8,128)S(1)}) fusion(bf16[4608,2,128]{0,2,1:T(8,128)(2,1)} %get-tuple-element.551, s32[]{:T(128)S(6)} %select_n.84, bf16[512,8,128]{2,0,1:T(8,128)(2,1)S(1)} %get-tuple-element.550, s32[]{:T(128)S(6)} %select_n.85, pred[4608]{0:T(1024)(128)(4,1)S(1)} %broadcast_compare_fusion.2, ...), kind=kOutput, calls=%fused_computation.62.clone.1 | convolution fusion | flops 620494336 | bytes 10779656 | tf_op jit(solution)/shard_map/while/body/eval_jaxpr/te,le->tl/dot_general | solution.py:61
  204.1 1.4 fusion.56
  205.7 1.6 fusion.58
  213.6 4.5 %fusion.54 = (f32[512]{0:T(512)S(1)}, f32[512,4608]{1,0:T(8,128)S(1)}) fusion(bf16[4608,2,128]{0,2,1:T(8,128)(2,1)} %get-tuple-element.551, s32[]{:T(128)S(6)} %select_n.84, bf16[512,8,128]{2,0,1:T(8,128)(2,1)S(1)} %get-tuple-element.550, s32[]{:T(128)S(6)} %select_n.85, pred[4608]{0:T(1024)(128)(4,1)S(1)} %broadcast_compare_fusion.2, ...), kind=kOutput, calls=%fused_computation.62.clone.1 | convolution fusion | flops 620494336 | bytes 10779656 | tf_op jit(solution)/shard_map/while/body/eval_jaxpr/te,le->tl/dot_general | solution.py:61
  222.5 1.6 fusion.58
  230.4 4.5 %fusion.54 = (f32[512]{0:T(512)S(1)}, f32[512,4608]{1,0:T(8,128)S(1)}) fusion(bf16[4608,2,128]{0,2,1:T(8,128)(2,1)} %get-tuple-element.551, s32[]{:T(128)S(6)} %select_n.84, bf16[512,8,128]{2,0,1:T(8,128)(2,1)S(1)} %get-tuple-element.550, s32[]{:T(128)S(6)} %select_n.85, pred[4608]{0:T(1024)(128)(4,1)S(1)} %broadcast_compare_fusion.2, ...), kind=kOutput, calls=%fused_computation.62.clone.1 | convolution fusion | flops 620494336 | bytes 10779656 | tf_op jit(solution)/shard_map/while/body/eval_jaxpr/te,le->tl/dot_general | solution.py:61
  239.3 1.6 fusion.58
  247.2 4.5 %fusion.54 = (f32[512]{0:T(512)S(1)}, f32[512,4608]{1,0:T(8,128)S(1)}) fusion(bf16[4608,2,128]{0,2,1:T(8,128)(2,1)} %get-tuple-element.551, s32[]{:T(128)S(6)} %select_n.84, bf16[512,8,128]{2,0,1:T(8,128)(2,1)S(1)} %get-tuple-element.550, s32[]{:T(128)S(6)} %select_n.85, pred[4608]{0:T(1024)(128)(4,1)S(1)} %broadcast_compare_fusion.2, ...), kind=kOutput, calls=%fused_computation.62.clone.1 | convolution fusion | flops 620494336 | bytes 10779656 | tf_op jit(solution)/shard_map/while/body/eval_jaxpr/te,le->tl/dot_general | solution.py:61
  256.1 1.6 fusion.58
  264.0 4.5 %fusion.54 = (f32[512]{0:T(512)S(1)}, f32[512,4608]{1,0:T(8,128)S(1)}) fusion(bf16[4608,2,128]{0,2,1:T(8,128)(2,1)} %get-tuple-element.551, s32[]{:T(128)S(6)} %select_n.84, bf16[512,8,128]{2,0,1:T(8,128)(2,1)S(1)} %get-tuple-element.550, s32[]{:T(128)S(6)} %select_n.85, pred[4608]{0:T(1024)(128)(4,1)S(1)} %broadcast_compare_fusion.2, ...), kind=kOutput, calls=%fused_computation.62.clone.1 | convolution fusion | flops 620494336 | bytes 10779656 | tf_op jit(solution)/shard_map/while/body/eval_jaxpr/te,le->tl/dot_general | solution.py:61
  272.9 1.6 fusion.58
  280.8 4.5 %fusion.54 = (f32[512]{0:T(512)S(1)}, f32[512,4608]{1,0:T(8,128)S(1)}) fusion(bf16[4608,2,128]{0,2,1:T(8,128)(2,1)} %get-tuple-element.551, s32[]{:T(128)S(6)} %select_n.84, bf16[512,8,128]{2,0,1:T(8,128)(2,1)S(1)} %get-tuple-element.550, s32[]{:T(128)S(6)} %select_n.85, pred[4608]{0:T(1024)(128)(4,1)S(1)} %broadcast_compare_fusion.2, ...), kind=kOutput, calls=%fused_computation.62.clone.1 | convolution fusion | flops 620494336 | bytes 10779656 | tf_op jit(solution)/shard_map/while/body/eval_jaxpr/te,le->tl/dot_general | solution.py:61
  289.7 1.6 fusion.58
  291.7 9.5 %convolution_convert_fusion = bf16[512,4096]{1,0:T(8,128)(2,1)} fusion(bf16[512,1024]{0,1:T(8,128)(2,1)S(1)} %bitcast.86, bf16[1024,4096]{1,0:T(8,128)(2,1)} %param.18), kind=kOutput, calls=%fused_computation.45 | convolution fusion | flops 4297064448 | bytes 13631488 | tf_op jit(solution)/shard_map/dot_general | solution.py:144
  301.3 6.6 %convert_element_type.44 = f32[512,4096]{1,0:T(8,128)} convert(bf16[512,4096]{1,0:T(8,128)(2,1)} %param.13) | non-fusion elementwise | flops 2097152 | bytes 12582912 | tf_op jit(solution)/shard_map/convert_element_type | solution.py:26
  307.9 50.1 %reduce-scatter.2.cloned.1.call-done = bf16[512,2048]{1,0:T(8,128)(2,1)} async-done(((bf16[512,4096]{1,0:T(8,128)(2,1)}), bf16[512,2048]{1,0:T(8,128)(2,1)}) %reduce-scatter.2.cloned.1.call-update) | async-done | bytes 2097168 | tf_op jit(solution)/shard_map/reduce_scatter | solution.py:148
  358.0 4.8 %add_convert_fusion = bf16[512,2048]{1,0:T(8,128)(2,1)} fusion(bf16[512,2048]{1,0:T(8,128)(2,1)} %reduce-scatter.2.cloned.1.call-done, f32[512,4096]{1,0:T(8,128)} %convert_element_type.44, s32[]{:T(128)S(6)} %select_n.61), kind=kLoop, calls=%fused_computation.46 | loop fusion | flops 3145728 | bytes 8388612 | tf_op jit(solution)/shard_map/convert_element_type | solution.py:155
  (191 shorter events, 59.5 us)
Async XLA Ops:
  6.5 3.2 copy-start
  6.5 351.5 %reduce-scatter.2.cloned.1.call-start = ((), (), s32[]{:S(2)}) async-start(), calls=%async_computation.1 | async-start | bytes 6291456 | tf_op jit(solution)/shard_map/reduce_scatter | solution.py:148
  9.8 3.7 %copy-start.2 = (bf16[512,4096]{1,0:T(8,128)(2,1)S(1)}, bf16[512,4096]{1,0:T(8,128)(2,1)}, u32[]{:S(2)}) copy-start(bf16[512,4096]{1,0:T(8,128)(2,1)} %param.13) | copy-start | bytes 12582916
  9.8 4.1 %copy-start.4 = (bf16[4096,256]{1,0:T(8,128)(2,1)S(1)}, bf16[4096,256]{1,0:T(8,128)(2,1)}, u32[]{:S(2)}) copy-start(bf16[4096,256]{1,0:T(8,128)(2,1)} %param.17) | copy-start | bytes 6291460
  9.8 4.1 %copy-start.5 = (f32[4096]{0:T(1024)S(1)}, f32[4096]{0:T(1024)}, u32[]{:S(2)}) copy-start(f32[4096]{0:T(1024)} %param.14) | copy-start | bytes 49156
  17.8 10.5 %collective-permute-start = (bf16[2,512,256]{2,1,0:T(8,128)(2,1)S(1)}, bf16[2,512,256]{2,1,0:T(8,128)(2,1)S(1)}, u32[]{:S(2)}, u32[]{:S(2)}) collective-permute-start(bf16[2,512,256]{2,1,0:T(8,128)(2,1)S(1)} %get-tuple-element.494), channel_id=1, source_target_pairs={{0,2},{2,4},{4,6},{6,8},{8,10},{10,12},{12,14},{14,16},{16,18},{18... | collective-permute-start | bytes 1572872 | tf_op jit(solution)/shard_map/while/body/eval_jaxpr/ppermute | solution.py:22
  29.1 10.5 %collective-permute-start = (bf16[2,512,256]{2,1,0:T(8,128)(2,1)S(1)}, bf16[2,512,256]{2,1,0:T(8,128)(2,1)S(1)}, u32[]{:S(2)}, u32[]{:S(2)}) collective-permute-start(bf16[2,512,256]{2,1,0:T(8,128)(2,1)S(1)} %get-tuple-element.494), channel_id=1, source_target_pairs={{0,2},{2,4},{4,6},{6,8},{8,10},{10,12},{12,14},{14,16},{16,18},{18... | collective-permute-start | bytes 1572872 | tf_op jit(solution)/shard_map/while/body/eval_jaxpr/ppermute | solution.py:22
  40.5 10.5 %collective-permute-start = (bf16[2,512,256]{2,1,0:T(8,128)(2,1)S(1)}, bf16[2,512,256]{2,1,0:T(8,128)(2,1)S(1)}, u32[]{:S(2)}, u32[]{:S(2)}) collective-permute-start(bf16[2,512,256]{2,1,0:T(8,128)(2,1)S(1)} %get-tuple-element.494), channel_id=1, source_target_pairs={{0,2},{2,4},{4,6},{6,8},{8,10},{10,12},{12,14},{14,16},{16,18},{18... | collective-permute-start | bytes 1572872 | tf_op jit(solution)/shard_map/while/body/eval_jaxpr/ppermute | solution.py:22
  51.9 10.5 %collective-permute-start = (bf16[2,512,256]{2,1,0:T(8,128)(2,1)S(1)}, bf16[2,512,256]{2,1,0:T(8,128)(2,1)S(1)}, u32[]{:S(2)}, u32[]{:S(2)}) collective-permute-start(bf16[2,512,256]{2,1,0:T(8,128)(2,1)S(1)} %get-tuple-element.494), channel_id=1, source_target_pairs={{0,2},{2,4},{4,6},{6,8},{8,10},{10,12},{12,14},{14,16},{16,18},{18... | collective-permute-start | bytes 1572872 | tf_op jit(solution)/shard_map/while/body/eval_jaxpr/ppermute | solution.py:22
  63.2 10.5 %collective-permute-start = (bf16[2,512,256]{2,1,0:T(8,128)(2,1)S(1)}, bf16[2,512,256]{2,1,0:T(8,128)(2,1)S(1)}, u32[]{:S(2)}, u32[]{:S(2)}) collective-permute-start(bf16[2,512,256]{2,1,0:T(8,128)(2,1)S(1)} %get-tuple-element.494), channel_id=1, source_target_pairs={{0,2},{2,4},{4,6},{6,8},{8,10},{10,12},{12,14},{14,16},{16,18},{18... | collective-permute-start | bytes 1572872 | tf_op jit(solution)/shard_map/while/body/eval_jaxpr/ppermute | solution.py:22
  74.6 10.5 %collective-permute-start = (bf16[2,512,256]{2,1,0:T(8,128)(2,1)S(1)}, bf16[2,512,256]{2,1,0:T(8,128)(2,1)S(1)}, u32[]{:S(2)}, u32[]{:S(2)}) collective-permute-start(bf16[2,512,256]{2,1,0:T(8,128)(2,1)S(1)} %get-tuple-element.494), channel_id=1, source_target_pairs={{0,2},{2,4},{4,6},{6,8},{8,10},{10,12},{12,14},{14,16},{16,18},{18... | collective-permute-start | bytes 1572872 | tf_op jit(solution)/shard_map/while/body/eval_jaxpr/ppermute | solution.py:22
  86.0 10.5 %collective-permute-start = (bf16[2,512,256]{2,1,0:T(8,128)(2,1)S(1)}, bf16[2,512,256]{2,1,0:T(8,128)(2,1)S(1)}, u32[]{:S(2)}, u32[]{:S(2)}) collective-permute-start(bf16[2,512,256]{2,1,0:T(8,128)(2,1)S(1)} %get-tuple-element.494), channel_id=1, source_target_pairs={{0,2},{2,4},{4,6},{6,8},{8,10},{10,12},{12,14},{14,16},{16,18},{18... | collective-permute-start | bytes 1572872 | tf_op jit(solution)/shard_map/while/body/eval_jaxpr/ppermute | solution.py:22
  97.3 10.5 %collective-permute-start = (bf16[2,512,256]{2,1,0:T(8,128)(2,1)S(1)}, bf16[2,512,256]{2,1,0:T(8,128)(2,1)S(1)}, u32[]{:S(2)}, u32[]{:S(2)}) collective-permute-start(bf16[2,512,256]{2,1,0:T(8,128)(2,1)S(1)} %get-tuple-element.494), channel_id=1, source_target_pairs={{0,2},{2,4},{4,6},{6,8},{8,10},{10,12},{12,14},{14,16},{16,18},{18... | collective-permute-start | bytes 1572872 | tf_op jit(solution)/shard_map/while/body/eval_jaxpr/ppermute | solution.py:22
  147.7 9.5 %copy-start.6 = (s32[8]{0:T(128)S(1)}, s32[8]{0:T(128)}, u32[]{:S(2)}) copy-start(s32[8]{0:T(128)} %param.19) | copy-start | bytes 100
  147.7 9.5 %copy-start.7 = (s32[8]{0:T(128)S(1)}, s32[8]{0:T(128)}, u32[]{:S(2)}) copy-start(s32[8]{0:T(128)} %param.20) | copy-start | bytes 100
  147.7 9.5 %copy-start.8 = (f32[8]{0:T(128)S(1)}, f32[8]{0:T(128)}, u32[]{:S(2)}) copy-start(f32[8]{0:T(128)} %param.21) | copy-start | bytes 100
  170.5 1.7 copy-start.3
  187.3 1.7 copy-start.3
  204.1 1.7 copy-start.3
  220.9 1.7 copy-start.3
  237.7 1.7 copy-start.3
  254.5 1.7 copy-start.3
  271.3 1.7 copy-start.3
  288.1 1.7 copy-start.3
  301.3 61.6 %copy-start.1 = (bf16[4096,256]{1,0:T(8,128)(2,1)S(1)}, bf16[4096,256]{1,0:T(8,128)(2,1)}, u32[]{:S(2)}) copy-start(bf16[4096,256]{1,0:T(8,128)(2,1)} %param.16) | copy-start | bytes 6291460
Sparse Core Ops, SparseCore 0:
  301.4 56.5 reduce-scatter.1
where the time goes:
time: 373 us; the launch traced here: 370 us
  waiting for transfers between devices  105 us (28%)
  matrix products  80.5 us (22%)
  local copies, waits for them, and re-layouts  45.5 us (12%)
  other arithmetic  37 us (10%)
  loops' own time  31.7 us (8%)
  starting transfers between devices  29.1 us (8%)
  blocking collectives  27.4 us (7%)
  between operations  13.6 us (4%)
    ppermute x8, waiting for transfers between devices, shifted(): return lax.ppermute(shard, axis, pairs)  54.6 us
    reduce_scatter x1, waiting for transfers between devices, local(): lax.psum_scatter(partial_value.astype(jnp.bfloat16), 'head', scatter_dime...  50.1 us
    dot_general x8, matrix products, one_head(): jnp.einsum('te,le->tl', head_queries, head_keys, preferred_element_type=j...  35.6 us
    another operation x1, loops' own time, attend(): per_head = lax.map(one_head, jnp.arange(heads_here, dtype=jnp.int32))  31.6 us
    ppermute x8, starting transfers between devices, shifted(): return lax.ppermute(shard, axis, pairs)  29.1 us
    psum x1, blocking collectives, from_root(): return lax.psum(block, axis)  27.4 us
    dot_general x8, matrix products, one_head(): jnp.einsum('tl,le->te', weights, head_values, preferred_element_type=jnp....  12.7 us
    reduce_sum x8, other arithmetic, one_head(): jnp.sum(weights, axis=1, keepdims=True)  11.2 us
  transfers between devices with their start and end apart: 9, of which 9 were waited for; matrix products, arithmetic and copies ran while one was open for 2% of the time, Pallas kernels for 0%

commit v1 on v0

v1 whole, which is shorter than its diff:
```python
import functools

import jax
import jax.numpy as jnp
from jax import lax
from jax.experimental import pallas as pl
from jax.experimental.pallas import tpu as pltpu
from jax.sharding import PartitionSpec as P

HEAD_DIM = 128
SINK = 4
SINK_ROWS = 16
SPAN = 9
QUAD = (SPAN - 1) // 2
EPSILON = 1e-05
LOG2E = 1.4426950408889634
LOW = -1e30
VMEM_LIMIT = 60 * 1024 * 1024
ANY = pl.BlockSpec(memory_space=pl.ANY)
SMEM = pl.BlockSpec(memory_space=pltpu.SMEM)
VMEM = pl.BlockSpec(memory_space=pltpu.VMEM)


def norm_kv_kernel(tok_ref, gain_ref, wk_ref, wv_ref, normed_ref, kv_ref):
    widened = tok_ref[...].astype(jnp.float32)
    row_scale = lax.rsqrt(jnp.mean(widened * widened, axis=1, keepdims=True) + EPSILON)
    normed = (widened * row_scale * gain_ref[...]).astype(jnp.bfloat16)
    normed_ref[...] = normed
    keys = jnp.dot(normed, wk_ref[...], preferred_element_type=jnp.float32).astype(jnp.bfloat16)
    values = jnp.dot(normed, wv_ref[...], preferred_element_type=jnp.float32).astype(jnp.bfloat16)
    for g in range(keys.shape[1] // HEAD_DIM):
        lo = 2 * g * HEAD_DIM
        kv_ref[:, lo : lo + HEAD_DIM] = keys[:, g * HEAD_DIM : (g + 1) * HEAD_DIM]
        kv_ref[:, lo + HEAD_DIM : lo + 2 * HEAD_DIM] = values[:, g * HEAD_DIM : (g + 1) * HEAD_DIM]


def norm_kv(tokens, gain, w_key, w_value):
    rows, width = tokens.shape
    kv_width = w_key.shape[1] + w_value.shape[1]
    tile = rows // 2
    return pl.pallas_call(
        norm_kv_kernel,
        grid=(rows // tile,),
        in_specs=[
            pl.BlockSpec((tile, width), lambda i: (i, 0)),
            pl.BlockSpec((1, width), lambda i: (0, 0)),
            pl.BlockSpec(w_key.shape, lambda i: (0, 0)),
            pl.BlockSpec(w_value.shape, lambda i: (0, 0)),
        ],
        out_specs=[
            pl.BlockSpec((tile, width), lambda i: (i, 0)),
            pl.BlockSpec((tile, kv_width), lambda i: (i, 0)),
        ],
        out_shape=[
            jax.ShapeDtypeStruct((rows, width), jnp.bfloat16),
            jax.ShapeDtypeStruct((rows, kv_width), jnp.bfloat16),
        ],
        compiler_params=pltpu.CompilerParams(vmem_limit_bytes=VMEM_LIMIT),
        cost_estimate=pl.CostEstimate(
            flops=2 * rows * width * kv_width, bytes_accessed=4 * rows * width + 2 * width * kv_width, transcendentals=rows
        ),
        name="norm_kv",
    )(tokens, gain.reshape(1, width), w_key, w_value)


def attend_kernel(group, slots, meta, window, sinks, bias, q_ref, *refs):
    kv_refs, sink_ref, out_ref = refs[:slots], refs[slots], refs[slots + 1]
    kvbuf, m_ref, acc_ref, sems = refs[slots + 2 :]
    rows = q_ref.shape[0]
    key_rows = kvbuf.shape[1]
    heads = q_ref.shape[1] // HEAD_DIM
    cols = pl.ds(2 * group * HEAD_DIM, 2 * HEAD_DIM)
    copies = [
        pltpu.make_async_copy(ref.at[:, cols], kvbuf.at[s, :, pl.ds(0, 2 * HEAD_DIM)], sems.at[s])
        for s, ref in enumerate(kv_refs)
    ]
    for copy in copies:
        copy.start()
    kvbuf[:, :, 2 * HEAD_DIM :] = jnp.ones((slots, key_rows, HEAD_DIM), jnp.bfloat16)
    for copy in copies:
        copy.wait()
    own = meta[0]
    query_start = own * rows
    tile = 256
    diff = lax.broadcasted_iota(jnp.int32, (tile, key_rows), 0) - lax.broadcasted_iota(jnp.int32, (tile, key_rows), 1)

    def update(t, scores, vaug):
        at = pl.ds(t * tile, tile)
        m_prev = m_ref[at, :]
        m_new = jnp.maximum(m_prev, jnp.max(scores, axis=1, keepdims=True))
        alpha = jnp.exp2(m_prev - m_new)
        reps = scores.shape[1] // HEAD_DIM
        weights = jnp.exp2(scores - jnp.concatenate([m_new] * reps, axis=1)).astype(jnp.bfloat16)
        m_ref[at, :] = m_new
        add = jnp.dot(weights, vaug, preferred_element_type=jnp.float32)
        acc_ref[at, :] = acc_ref[at, :] * jnp.concatenate([alpha, alpha], axis=1) + add

    def one_head(index, carry):
        head = pl.ds(pl.multiple_of(index * HEAD_DIM, HEAD_DIM), HEAD_DIM)
        reach = window[group * heads + index]
        m_ref[...] = jnp.full(m_ref.shape, LOW, jnp.float32)
        acc_ref[...] = jnp.zeros(acc_ref.shape, jnp.float32)

        def scores_of(t, keys):
            return lax.dot_general(
                q_ref[pl.ds(t * tile, tile), head], keys, (((1,), (1,)), ((), ())), preferred_element_type=jnp.float32
            )

        def one_slot(s, carry):
            block = meta[1 + s]
            ahead = (own - block) * rows
            some = (block >= 0) & (ahead - (rows - 1) < reach)
            whole = (ahead > 0) & (ahead + rows - 1 < reach)

            @pl.when(some & whole)
            def _():
                keys, vaug = kvbuf[s, :, :HEAD_DIM], kvbuf[s, :, HEAD_DIM:]
                for t in range(rows // tile):
                    update(t, scores_of(t, keys), vaug)

            @pl.when(some & jnp.logical_not(whole))
            def _():
                keys, vaug = kvbuf[s, :, :HEAD_DIM], kvbuf[s, :, HEAD_DIM:]
                for t in range(rows // tile):
                    gap = diff + (ahead + t * tile)
                    scores = jnp.where((gap >= 0) & (gap < reach), scores_of(t, keys), LOW)
                    update(t, scores, vaug)

            return carry

        lax.fori_loop(0, slots, one_slot, 0)

        @pl.when(query_start + rows - 1 - reach >= 0)
        def _():
            base = 2 * group * HEAD_DIM
            pad = jnp.zeros((HEAD_DIM - SINK_ROWS, HEAD_DIM), jnp.bfloat16)
            keys = jnp.concatenate([sink_ref[:, base : base + HEAD_DIM], pad], axis=0)
            values = jnp.concatenate([sink_ref[:, base + HEAD_DIM : base + 2 * HEAD_DIM], pad], axis=0)
            vaug = jnp.concatenate([values, jnp.ones((HEAD_DIM, HEAD_DIM), jnp.bfloat16)], axis=1)
            column = lax.broadcasted_iota(jnp.int32, (tile, HEAD_DIM), 1)
            row = lax.broadcasted_iota(jnp.int32, (tile, HEAD_DIM), 0)
            shift = bias[group * heads + index] * LOG2E
            count = jnp.minimum(sinks[group * heads + index], SINK)
            for t in range(rows // tile):
                latest = row + (query_start + t * tile - reach)
                open_ = (column < count) & (column <= latest)
                update(t, jnp.where(open_, scores_of(t, keys) + shift, LOW), vaug)

        out_ref[:, head] = (acc_ref[:, :HEAD_DIM] / acc_ref[:, HEAD_DIM:]).astype(jnp.bfloat16)
        return carry

    lax.fori_loop(0, heads, one_head, 0)


def attend(group, groups, meta, window, sink_count, sink_bias, queries, blocks, sink_rows):
    rows, width = queries.shape
    share = width // groups
    slots = len(blocks)
    key_rows = blocks[0].shape[0]
    return pl.pallas_call(
        functools.partial(attend_kernel, group, slots),
        grid=(1,),
        in_specs=[SMEM] * 4
        + [pl.BlockSpec((rows, share), lambda i: (0, group))]
        + [ANY] * slots
        + [pl.BlockSpec(sink_rows.shape, lambda i: (0, 0))],
        out_specs=pl.BlockSpec((rows, share), lambda i: (0, 0)),
        out_shape=jax.ShapeDtypeStruct((rows, share), jnp.bfloat16),
        scratch_shapes=[
            pltpu.VMEM((slots, key_rows, 3 * HEAD_DIM), jnp.bfloat16),
            pltpu.VMEM((rows, HEAD_DIM), jnp.float32),
            pltpu.VMEM((rows, 2 * HEAD_DIM), jnp.float32),
            pltpu.SemaphoreType.DMA((slots,)),
        ],
        compiler_params=pltpu.CompilerParams(vmem_limit_bytes=32 * 1024 * 1024),
        cost_estimate=pl.CostEstimate(
            flops=4 * rows * slots * key_rows * share,
            bytes_accessed=2 * slots * key_rows * 2 * HEAD_DIM,
            transcendentals=rows * slots * key_rows * (share // HEAD_DIM),
        ),
        name="attend",
    )(meta, window, sink_count, sink_bias, queries, *blocks, sink_rows)


def project_kernel(where, tok_ref, own0, own1, far0, far1, w_ref, wa_ref, wb_ref, out_ref):
    step = pl.program_id(0)
    half = own0.shape[1]
    total = tok_ref[...].astype(jnp.float32)
    total += jnp.dot(own0[...], w_ref[:half, :], preferred_element_type=jnp.float32)
    total += jnp.dot(own1[...], w_ref[half:, :], preferred_element_type=jnp.float32)

    def finish(w):
        more = jnp.dot(far0[...], w[:half, :], preferred_element_type=jnp.float32)
        more += jnp.dot(far1[...], w[half:, :], preferred_element_type=jnp.float32)
        out_ref[...] = (total + more).astype(jnp.bfloat16)

    @pl.when(step < pl.num_programs(0) // 2)
    def _():
        finish(wa_ref)

    @pl.when(step >= pl.num_programs(0) // 2)
    def _():
        finish(wb_ref)


def project(where, tokens, own, far, w_out, w_near, w_swap):
    rows = tokens.shape[0]
    depth, piece = w_near.shape
    share = 2 * piece
    tile = 512
    steps = share // tile
    part = steps // 2

    def column(j, where):
        return jnp.where(where[1] == 0, j, lax.rem(j + part, steps))

    full = lambda a: pl.BlockSpec(a.shape, lambda j, where: (0, 0))
    shifted_column = lambda j, where: (0, where[0] * steps + column(j, where))
    return pl.pallas_call(
        project_kernel,
        grid_spec=pltpu.PrefetchScalarGridSpec(
            num_scalar_prefetch=1,
            grid=(steps,),
            in_specs=[
                pl.BlockSpec((rows, tile), shifted_column),
                full(own[0]),
                full(own[1]),
                full(far[0]),
                full(far[1]),
                pl.BlockSpec((depth, tile), shifted_column),
                pl.BlockSpec((depth, tile), lambda j, where: (0, jnp.minimum(j, part - 1))),
                pl.BlockSpec((depth, tile), lambda j, where: (0, jnp.maximum(j - part, 0))),
            ],
            out_specs=pl.BlockSpec((rows, tile), lambda j, where: (0, column(j, where))),
        ),
        out_shape=jax.ShapeDtypeStruct((rows, share), jnp.bfloat16),
        compiler_params=pltpu.CompilerParams(vmem_limit_bytes=VMEM_LIMIT),
        cost_estimate=pl.CostEstimate(
            flops=4 * rows * depth * share, bytes_accessed=4 * depth * share + 4 * rows * share, transcendentals=0
        ),
        name="project",
    )(where, tokens, own[0], own[1], far[0], far[1], w_out, w_near, w_swap)


def local(tokens, norm_gain, w_query, w_key, w_value, w_out, window, sink_count, sink_bias):
    peers = lax.axis_size("seq")
    head_peers = lax.axis_size("head")
    me = lax.axis_index("seq")
    my_head = lax.axis_index("head")
    core, side = me % 2, (me // 2) % 2
    groups = w_key.shape[1] // HEAD_DIM
    share = w_out.shape[1] // head_peers
    piece = share // 2

    ahead = [(i, i + QUAD) for i in range(peers - QUAD)]
    core_swap = [(i, i ^ 1) for i in range(peers)]
    side_swap = [(i, i ^ 2) for i in range(peers)]
    head_swap = [(i, i ^ 1) for i in range(head_peers)]

    w_send = lax.dynamic_slice_in_dim(w_out, (1 - my_head) * share + core * piece, piece, 1)
    normed, kv = norm_kv(tokens, norm_gain, w_key, w_value)

    back4 = lax.ppermute(kv, "seq", ahead)
    w_near = lax.ppermute(w_send, "head", head_swap)

    sink_rows = kv[:SINK_ROWS]
    have = peers
    while have > 1:
        step = have // 2
        arrived = lax.ppermute(sink_rows, "seq", [(i, i + step) for i in range(0, peers, have)])
        sink_rows = jnp.where(me % have == step, arrived, sink_rows)
        have = step

    queries = (
        jnp.dot(normed, w_query, preferred_element_type=jnp.float32) * (HEAD_DIM**-0.5 * LOG2E)
    ).astype(jnp.bfloat16)

    back8 = lax.ppermute(back4, "seq", ahead)
    side_a = lax.ppermute(back4, "seq", side_swap)
    side_b = lax.ppermute(jnp.where(side == 0, kv, back8), "seq", side_swap)
    core_a = lax.ppermute(back4, "seq", core_swap)
    core_b = lax.ppermute(jnp.where(core == 0, kv, back8), "seq", core_swap)
    cross_a = lax.ppermute(side_a, "seq", core_swap)
    cross_b = lax.ppermute(side_b, "seq", core_swap)
    w_swap = lax.ppermute(w_near, "seq", core_swap)

    mate = me ^ 1
    across = jnp.where(side == 0, 2, -2)
    twin = jnp.where(core == 0, 1, -1)
    far_b = jnp.where(side == 0, 8, 0)
    blocks = [kv, back4, core_a, core_b, side_a, cross_a, side_b, cross_b, back8]
    index = [
        me,
        me - 4,
        me + twin - 4,
        me + twin - jnp.where(core == 0, 8, 0),
        me + across - 4,
        mate + across - 4,
        me + across - far_b,
        mate + across - far_b,
        me - 8,
    ]
    meta = jnp.stack([me] + index).astype(jnp.int32)
    own, far = [], []
    for g in range(groups):
        att = attend(g, groups, meta, window, sink_count, sink_bias, queries, blocks, sink_rows)
        own.append(att)
        far.append(lax.ppermute(att, "head", head_swap))
    where = jnp.stack([my_head, core]).astype(jnp.int32)
    return project(where, tokens, own, far, w_out, w_near, w_swap)


def solution(mesh):
    in_specs = (
        P("seq", None),
        P(),
        P(None, "head"),
        P(None, "head"),
        P(None, "head"),
        P("head", None),
        P("head"),
        P("head"),
        P("head"),
    )
    out_specs = P("seq", "head")
    return jax.shard_map(local, mesh=mesh, in_specs=in_specs, out_specs=out_specs, check_vma=False)
```

time: 373 us -> 148 us (0.40)
  matrix products: 80.5 us -> 10.2 us
  Pallas kernels: 0 us -> 63.8 us
  waiting for transfers between devices: 105 us -> 41.5 us
  local copies, waits for them, and re-layouts: 45.5 us -> 7.17 us
  other arithmetic: 37 us -> 3.26 us
  loops' own time: 31.7 us -> 0 us
  blocking collectives: 27.4 us -> 0 us
  between operations: 13.6 us -> 0.32 us
  starting transfers between devices: 29.1 us -> 21.7 us
    dot_general x35 -> x0, matrix products: 71.3 us -> none  [the longest x8 35.6 us: one_head(): jnp.einsum('te,le->tl', head_queries, head_keys, preferred_element_type=j...]
    pallas_call x0 -> x4, Pallas kernels: none -> 63.8 us  [the longest x2 45.9 us: attend(): pl.pallas_call(functools.partial(attend_kernel, group, slots), grid=(1,),...]
    reduce_scatter x1 -> x0, waiting for transfers between devices: 50.1 us -> none  [local(): lax.psum_scatter(partial_value.astype(jnp.bfloat16), 'head', scatter_dime...]
    another operation x2 -> x0, loops' own time: 31.7 us -> none  [the longest x1 31.6 us: attend(): per_head = lax.map(one_head, jnp.arange(heads_here, dtype=jnp.int32))]
    psum x1 -> x0, blocking collectives: 27.4 us -> none  [from_root(): return lax.psum(block, axis)]
    dynamic_slice x32 -> x1, local copies, waits for them, and re-layouts: 20.9 us -> 3.08 us  [local(): lax.dynamic_slice_in_dim(w_out, (1 - my_head) * share + core * piece, pie...]
    reduce_sum x17 -> x0, other arithmetic: 14.7 us -> none  [the longest x8 11.2 us: one_head(): jnp.sum(weights, axis=1, keepdims=True)]
    ppermute x8 -> x16, waiting for transfers between devices: 54.6 us -> 41.5 us  [the longest x1 12 us: local(): back4 = lax.ppermute(kv, 'seq', ahead)]
  transfers between devices with their start and end apart: 9 -> 16, of which waited for: 9 -> 5; matrix products, arithmetic and copies ran while one was open for 2% -> 10% of each run, Pallas kernels for 0% -> 36%
where the time goes in v1:
time: 148 us
  Pallas kernels  63.8 us (43%)
  waiting for transfers between devices  41.5 us (28%)
  starting transfers between devices  21.7 us (15%)
  matrix products  10.2 us (7%)
  local copies, waits for them, and re-layouts  7.17 us (5%)
  other arithmetic  3.26 us (2%)
    pallas_call x2, Pallas kernels, attend(): pl.pallas_call(functools.partial(attend_kernel, group, slots), grid=(1,),...  45.9 us
    ppermute x1, waiting for transfers between devices, local(): back4 = lax.ppermute(kv, 'seq', ahead)  12 us
    ppermute x2, waiting for transfers between devices, local(): far.append(lax.ppermute(att, 'head', head_swap))  11.6 us
    pallas_call x1, Pallas kernels, project(): pl.pallas_call(project_kernel, grid_spec=pltpu.PrefetchScalarGridSpec(num...  10.7 us
    dot_general x1, matrix products, local(): jnp.dot(normed, w_query, preferred_element_type=jnp.float32)  10.2 us
    ppermute x4, waiting for transfers between devices, local(): lax.ppermute(sink_rows, 'seq', [(i, i + step) for i in range(0, peers, ha...  9.59 us
    ppermute x1, waiting for transfers between devices, local(): back8 = lax.ppermute(back4, 'seq', ahead)  8.36 us
    pallas_call x1, Pallas kernels, norm_kv(): pl.pallas_call(norm_kv_kernel, grid=(rows // tile,), in_specs=[pl.BlockSp...  7.18 us
  transfers between devices with their start and end apart: 16, of which 5 were waited for; matrix products, arithmetic and copies ran while one was open for 10% of the time, Pallas kernels for 36%

profile of v1, /device:TPU:18, one launch (start us, length us, event | category | flops | bytes accessed | tf_op | source)
XLA Modules:
  0.0 147.9 jit_solution(6864516354850665645)
XLA Ops:
  0.0 3.1 %constant_dynamic-slice_fusion = bf16[1024,1024]{1,0:T(8,128)(2,1)} fusion(bf16[1024,4096]{1,0:T(8,128)(2,1)} %w_ref.1, s32[]{:T(128)S(6)} %select_n.107), kind=kLoop, calls=%fused_computation.8 | loop fusion | bytes 4194308 | tf_op jit(solution)/shard_map/dynamic_slice | solution.py:260
  3.1 1.5 %collective-permute-start.14 = (bf16[1024,1024]{1,0:T(8,128)(2,1)}, bf16[1024,1024]{1,0:T(8,128)(2,1)}, u32[]{:S(2)}, u32[]{:S(2)}) collective-permute-start(bf16[1024,1024]{1,0:T(8,128)(2,1)} %constant_dynamic-slice_fusion), channel_id=1, source_target_pairs={{0,1},{1,0},{2,3},{3,2},{4,5},{5,4},{6,7},{7,6},{8,9},{9,8},{10,11... | collective-permute-start | bytes 6291464 | tf_op jit(solution)/shard_map/ppermute | solution.py:264
  4.6 7.2 %norm_kv.1 = (bf16[512,4096]{1,0:T(8,128)(2,1)}, bf16[512,512]{1,0:T(8,128)(2,1)}) custom-call(bf16[512,4096]{1,0:T(8,128)(2,1)} %tok_ref.3, f32[1,4096]{1,0:T(1,128)} %bitcast.14, bf16[4096,256]{1,0:T(8,128)(2,1)} %wk_ref.1, bf16[4096,256]{1,0:T(8,128)(2,1)} %wv_ref.1), custom_call_target="tpu_custom_call" | custom-call | flops 2147483648 | bytes 12582912 | tf_op jit(solution)/shard_map/norm_kv/pallas_call | solution.py:41
  11.8 3.5 %collective-permute-start = (bf16[512,512]{1,0:T(8,128)(2,1)}, bf16[512,512]{1,0:T(8,128)(2,1)S(1)}, u32[]{:S(2)}, u32[]{:S(2)}) collective-permute-start(bf16[512,512]{1,0:T(8,128)(2,1)} %get-tuple-element.8.refs_0_), channel_id=1, source_target_pairs={{0,8},{2,10},{4,12},{6,14},{8,16},{10,18},{12,20},{14,22},{16,24},... | collective-permute-start | bytes 1572872 | tf_op jit(solution)/shard_map/ppermute | solution.py:263
  15.2 12.0 %collective-permute-done.refs_1_ = bf16[512,512]{1,0:T(8,128)(2,1)S(1)} collective-permute-done((bf16[512,512]{1,0:T(8,128)(2,1)}, bf16[512,512]{1,0:T(8,128)(2,1)S(1)}, u32[]{:S(2)}, u32[]{:S(2)}) %collective-permute-start) | collective-permute-done | bytes 524320 | tf_op jit(solution)/shard_map/ppermute | solution.py:263
  27.2 3.5 %collective-permute-start.2 = (bf16[512,512]{1,0:T(8,128)(2,1)S(1)}, bf16[512,512]{1,0:T(8,128)(2,1)S(1)}, u32[]{:S(2)}, u32[]{:S(2)}) collective-permute-start(bf16[512,512]{1,0:T(8,128)(2,1)S(1)} %collective-permute-done.refs_1_), channel_id=1, source_target_pairs={{0,8},{2,10},{4,12},{6,14},{8,16},{10,18},{12,20},{14,22},{16,24},... | collective-permute-start | bytes 1572872 | tf_op jit(solution)/shard_map/ppermute | solution.py:278
  30.7 0.7 slice.3
  31.4 0.7 collective-permute-start.8
  32.2 1.2 collective-permute-start.4
  33.4 8.4 %collective-permute-done.2.refs_8_ = bf16[512,512]{1,0:T(8,128)(2,1)S(1)} collective-permute-done((bf16[512,512]{1,0:T(8,128)(2,1)S(1)}, bf16[512,512]{1,0:T(8,128)(2,1)S(1)}, u32[]{:S(2)}, u32[]{:S(2)}) %collective-permute-start.2) | collective-permute-done | bytes 524320 | tf_op jit(solution)/shard_map/ppermute | solution.py:278
  41.8 1.9 %broadcast_select_fusion = (bf16[512,512]{1,0:T(8,128)(2,1)S(1)}, bf16[512,512]{1,0:T(8,128)(2,1)}) fusion(bf16[512,512]{1,0:T(8,128)(2,1)} %get-tuple-element.8.refs_0_, bf16[512,512]{1,0:T(8,128)(2,1)S(1)} %collective-permute-done.2.refs_8_, pred[]{:T(512)S(6)} %eq.30, pred[]{:T(512)S(6)} %eq.29), kind=kLoop, calls=%fused_computation.1 | loop fusion | flops 524288 | bytes 2097154 | tf_op jit(solution)/shard_map/jit(_where)/select_n | solution.py:280
  43.7 0.7 collective-permute-start.6
  44.4 0.0 collective-permute-done.8
  44.4 0.7 broadcast_select_fusion.2
  45.1 0.7 collective-permute-start.9
  45.8 0.0 collective-permute-done.9
  45.8 1.3 collective-permute-start.10
  47.1 8.8 %collective-permute-done.10 = bf16[16,512]{1,0:T(8,128)(2,1)S(1)} collective-permute-done((bf16[16,512]{1,0:T(8,128)(2,1)S(1)}, bf16[16,512]{1,0:T(8,128)(2,1)S(1)}, u32[]{:S(2)}, u32[]{:S(2)}) %collective-permute-start.10) | collective-permute-done | bytes 16416 | tf_op jit(solution)/shard_map/ppermute | solution.py:270
  56.0 1.3 collective-permute-start.11
  57.3 0.1 collective-permute-start.1
  57.4 0.7 collective-permute-done.11
  58.1 0.3 collective-permute-start.3
  58.4 0.0 collective-permute-done.4.refs_4_
  58.4 0.2 collective-permute-start.5
  58.6 0.0 collective-permute-done.6.refs_6_
  58.6 0.3 collective-permute-start.7
  59.0 0.0 collective-permute-done.14.wa_ref
  59.0 0.2 collective-permute-start.15
  59.1 10.2 %multiply_convert_fusion.q_ref = bf16[512,1024]{1,0:T(8,128)(2,1)} fusion(bf16[512,4096]{1,0:T(8,128)(2,1)} %get-tuple-element.7, bf16[4096,1024]{1,0:T(8,128)(2,1)} %param.11), kind=kOutput, calls=%fused_computation | convolution fusion | flops 4296015872 | bytes 13631488 | tf_op jit(solution)/shard_map/dot_general | solution.py:275
  69.3 0.1 stack.52.meta
  69.4 0.0 collective-permute-done.1.refs_2_
  69.4 0.0 collective-permute-done.3.refs_3_
  69.4 0.0 collective-permute-done.5.refs_5_
  69.4 0.0 collective-permute-done.7.refs_7_
  69.5 0.0 copy-start.8
  69.5 1.3 copy-done.8
  70.8 27.5 %attend.2.own0 = bf16[512,512]{1,0:T(8,128)(2,1)S(1)} custom-call(s32[10]{0:T(128)S(1)} %stack.52.meta, s32[8]{0:T(128)S(1)} %copy-done.5, s32[8]{0:T(128)S(1)} %copy-done.6, f32[8]{0:T(128)S(1)} %copy-done.7, bf16[512,1024]{1,0:T(8,128)(2,1)S(1)} %copy-done.8, bf16[512,512]{1,0:T(8,128)(2,1)S(1)} %copy-done, ...), custom_call_target="tpu_custom_call" | custom-call | flops 4831838208 | bytes 2359296 | tf_op jit(solution)/shard_map/attend/pallas_call | solution.py:160
  98.4 0.1 collective-permute-start.12
  98.5 1.1 copy-done.4
  99.6 18.4 %attend.3.own1 = bf16[512,512]{1,0:T(8,128)(2,1)S(1)} custom-call(s32[10]{0:T(128)S(1)} %stack.52.meta, s32[8]{0:T(128)S(1)} %copy-done.5, s32[8]{0:T(128)S(1)} %copy-done.6, f32[8]{0:T(128)S(1)} %copy-done.7, bf16[512,1024]{1,0:T(8,128)(2,1)S(1)} %copy-done.8, bf16[512,512]{1,0:T(8,128)(2,1)S(1)} %copy-done, ...), custom_call_target="tpu_custom_call" | custom-call | flops 4831838208 | bytes 2359296 | tf_op jit(solution)/shard_map/attend/pallas_call | solution.py:160
  118.0 6.2 %collective-permute-start.13 = (bf16[512,512]{1,0:T(8,128)(2,1)S(1)}, bf16[512,512]{1,0:T(8,128)(2,1)S(1)}, u32[]{:S(2)}, u32[]{:S(2)}) collective-permute-start(bf16[512,512]{1,0:T(8,128)(2,1)S(1)} %attend.3.own1), channel_id=1, source_target_pairs={{0,1},{1,0},{2,3},{3,2},{4,5},{5,4},{6,7},{7,6},{8,9},{9,8},{10,11... | collective-permute-start | bytes 1572872 | tf_op jit(solution)/shard_map/ppermute | solution.py:308
  124.3 0.6 pad_add_fusion.where
  124.9 0.0 collective-permute-done.12.far0
  124.9 11.6 %collective-permute-done.13.far1 = bf16[512,512]{1,0:T(8,128)(2,1)S(1)} collective-permute-done((bf16[512,512]{1,0:T(8,128)(2,1)S(1)}, bf16[512,512]{1,0:T(8,128)(2,1)S(1)}, u32[]{:S(2)}, u32[]{:S(2)}) %collective-permute-start.13) | collective-permute-done | bytes 524320 | tf_op jit(solution)/shard_map/ppermute | solution.py:308
  136.4 0.0 collective-permute-done.15.wb_ref
  136.4 0.0 copy-done.2
  136.4 0.8 copy-done.10
  137.2 10.7 %project.1 = bf16[512,2048]{1,0:T(8,128)(2,1)} custom-call(s32[2]{0:T(128)} %pad_add_fusion.where, bf16[512,4096]{1,0:T(8,128)(2,1)} %tok_ref.3, bf16[512,512]{1,0:T(8,128)(2,1)} %copy-done.1, bf16[512,512]{1,0:T(8,128)(2,1)} %copy-done.2, bf16[512,512]{1,0:T(8,128)(2,1)} %copy-done.9, bf16[512,512]{1,0:T(8,128)(2,1)} %copy-done.10, ...), custom_call_target="tpu_custom_call" | custom-call | flops 4294967296 | bytes 12582912 | tf_op jit(solution)/shard_map/project/pallas_call | solution.py:219
  (20 shorter events, 0.1 us)
Async XLA Ops:
  3.1 55.9 %collective-permute-start.14 = (bf16[1024,1024]{1,0:T(8,128)(2,1)}, bf16[1024,1024]{1,0:T(8,128)(2,1)}, u32[]{:S(2)}, u32[]{:S(2)}) collective-permute-start(bf16[1024,1024]{1,0:T(8,128)(2,1)} %constant_dynamic-slice_fusion), channel_id=1, source_target_pairs={{0,1},{1,0},{2,3},{3,2},{4,5},{5,4},{6,7},{7,6},{8,9},{9,8},{10,11... | collective-permute-start | bytes 6291464 | tf_op jit(solution)/shard_map/ppermute | solution.py:264
  11.8 15.5 %collective-permute-start = (bf16[512,512]{1,0:T(8,128)(2,1)}, bf16[512,512]{1,0:T(8,128)(2,1)S(1)}, u32[]{:S(2)}, u32[]{:S(2)}) collective-permute-start(bf16[512,512]{1,0:T(8,128)(2,1)} %get-tuple-element.8.refs_0_), channel_id=1, source_target_pairs={{0,8},{2,10},{4,12},{6,14},{8,16},{10,18},{12,20},{14,22},{16,24},... | collective-permute-start | bytes 1572872 | tf_op jit(solution)/shard_map/ppermute | solution.py:263
  27.2 14.5 %collective-permute-start.2 = (bf16[512,512]{1,0:T(8,128)(2,1)S(1)}, bf16[512,512]{1,0:T(8,128)(2,1)S(1)}, u32[]{:S(2)}, u32[]{:S(2)}) collective-permute-start(bf16[512,512]{1,0:T(8,128)(2,1)S(1)} %collective-permute-done.refs_1_), channel_id=1, source_target_pairs={{0,8},{2,10},{4,12},{6,14},{8,16},{10,18},{12,20},{14,22},{16,24},... | collective-permute-start | bytes 1572872 | tf_op jit(solution)/shard_map/ppermute | solution.py:278
  31.4 13.0 %collective-permute-start.8 = (bf16[16,512]{1,0:T(8,128)(2,1)S(1)}, bf16[16,512]{1,0:T(8,128)(2,1)S(1)}, u32[]{:S(2)}, u32[]{:S(2)}) collective-permute-start(bf16[16,512]{1,0:T(8,128)(2,1)S(1)} %slice.3), channel_id=1, source_target_pairs={{0,16},{1,17}} | collective-permute-start | bytes 49160 | tf_op jit(solution)/shard_map/ppermute | solution.py:270
  32.2 26.3 %collective-permute-start.4 = (bf16[512,512]{1,0:T(8,128)(2,1)S(1)}, bf16[512,512]{1,0:T(8,128)(2,1)S(1)}, u32[]{:S(2)}, u32[]{:S(2)}) collective-permute-start(bf16[512,512]{1,0:T(8,128)(2,1)S(1)} %collective-permute-done.refs_1_), channel_id=1, source_target_pairs={{0,4},{2,6},{4,0},{6,2},{8,12},{10,14},{12,8},{14,10},{16,20},{18,... | collective-permute-start | bytes 1572872 | tf_op jit(solution)/shard_map/ppermute | solution.py:279
  43.7 14.9 %collective-permute-start.6 = (bf16[512,512]{1,0:T(8,128)(2,1)S(1)}, bf16[512,512]{1,0:T(8,128)(2,1)S(1)}, u32[]{:S(2)}, u32[]{:S(2)}) collective-permute-start(bf16[512,512]{1,0:T(8,128)(2,1)S(1)} %get-tuple-element.9), channel_id=1, source_target_pairs={{0,4},{2,6},{4,0},{6,2},{8,12},{10,14},{12,8},{14,10},{16,20},{18,... | collective-permute-start | bytes 1572872 | tf_op jit(solution)/shard_map/ppermute | solution.py:280
  45.1 0.7 collective-permute-start.9
  45.8 10.2 %collective-permute-start.10 = (bf16[16,512]{1,0:T(8,128)(2,1)S(1)}, bf16[16,512]{1,0:T(8,128)(2,1)S(1)}, u32[]{:S(2)}, u32[]{:S(2)}) collective-permute-start(bf16[16,512]{1,0:T(8,128)(2,1)S(1)} %broadcast_select_fusion.3), channel_id=1, source_target_pairs={{0,4},{8,12},{16,20},{24,28},{1,5},{9,13},{17,21},{25,29}} | collective-permute-start | bytes 49160 | tf_op jit(solution)/shard_map/ppermute | solution.py:270
  56.0 2.1 %collective-permute-start.11 = (bf16[16,512]{1,0:T(8,128)(2,1)S(1)}, bf16[16,512]{1,0:T(8,128)(2,1)S(1)}, u32[]{:S(2)}, u32[]{:S(2)}) collective-permute-start(bf16[16,512]{1,0:T(8,128)(2,1)S(1)} %broadcast_select_fusion.4), channel_id=1, source_target_pairs={{0,2},{4,6},{8,10},{12,14},{16,18},{20,22},{24,26},{28,30},{1,3},{... | collective-permute-start | bytes 49160 | tf_op jit(solution)/shard_map/ppermute | solution.py:270
  57.3 12.1 %collective-permute-start.1 = (bf16[512,512]{1,0:T(8,128)(2,1)S(1)}, bf16[512,512]{1,0:T(8,128)(2,1)S(1)}, u32[]{:S(2)}, u32[]{:S(2)}) collective-permute-start(bf16[512,512]{1,0:T(8,128)(2,1)S(1)} %collective-permute-done.refs_1_), channel_id=1, source_target_pairs={{0,2},{2,0},{4,6},{6,4},{8,10},{10,8},{12,14},{14,12},{16,18},{18,... | collective-permute-start | bytes 1572872 | tf_op jit(solution)/shard_map/ppermute | solution.py:281
  58.1 11.3 %collective-permute-start.3 = (bf16[512,512]{1,0:T(8,128)(2,1)}, bf16[512,512]{1,0:T(8,128)(2,1)}, u32[]{:S(2)}, u32[]{:S(2)}) collective-permute-start(bf16[512,512]{1,0:T(8,128)(2,1)} %get-tuple-element.10), channel_id=1, source_target_pairs={{0,2},{2,0},{4,6},{6,4},{8,10},{10,8},{12,14},{14,12},{16,18},{18,... | collective-permute-start | bytes 1572872 | tf_op jit(solution)/shard_map/ppermute | solution.py:282
  58.4 11.0 %collective-permute-start.5 = (bf16[512,512]{1,0:T(8,128)(2,1)S(1)}, bf16[512,512]{1,0:T(8,128)(2,1)}, u32[]{:S(2)}, u32[]{:S(2)}) collective-permute-start(bf16[512,512]{1,0:T(8,128)(2,1)S(1)} %collective-permute-done.4.refs_4_), channel_id=1, source_target_pairs={{0,2},{2,0},{4,6},{6,4},{8,10},{10,8},{12,14},{14,12},{16,18},{18,... | collective-permute-start | bytes 1572872 | tf_op jit(solution)/shard_map/ppermute | solution.py:283
  58.6 10.8 %collective-permute-start.7 = (bf16[512,512]{1,0:T(8,128)(2,1)S(1)}, bf16[512,512]{1,0:T(8,128)(2,1)}, u32[]{:S(2)}, u32[]{:S(2)}) collective-permute-start(bf16[512,512]{1,0:T(8,128)(2,1)S(1)} %collective-permute-done.6.refs_6_), channel_id=1, source_target_pairs={{0,2},{2,0},{4,6},{6,4},{8,10},{10,8},{12,14},{14,12},{16,18},{18,... | collective-permute-start | bytes 1572872 | tf_op jit(solution)/shard_map/ppermute | solution.py:284
  59.0 77.5 %collective-permute-start.15 = (bf16[1024,1024]{1,0:T(8,128)(2,1)}, bf16[1024,1024]{1,0:T(8,128)(2,1)}, u32[]{:S(2)}, u32[]{:S(2)}) collective-permute-start(bf16[1024,1024]{1,0:T(8,128)(2,1)} %collective-permute-done.14.wa_ref), channel_id=1, source_target_pairs={{0,2},{2,0},{4,6},{6,4},{8,10},{10,8},{12,14},{14,12},{16,18},{18,... | collective-permute-start | bytes 6291464 | tf_op jit(solution)/shard_map/ppermute | solution.py:285
  59.1 10.3 %copy-start = (bf16[512,512]{1,0:T(8,128)(2,1)S(1)}, bf16[512,512]{1,0:T(8,128)(2,1)}, u32[]{:S(2)}) copy-start(bf16[512,512]{1,0:T(8,128)(2,1)} %get-tuple-element.8.refs_0_) | copy-start | bytes 1572868
  59.1 10.3 %copy-start.5 = (s32[8]{0:T(128)S(1)}, s32[8]{0:T(128)}, u32[]{:S(2)}) copy-start(s32[8]{0:T(128)} %window.3) | copy-start | bytes 100
  59.1 10.3 %copy-start.6 = (s32[8]{0:T(128)S(1)}, s32[8]{0:T(128)}, u32[]{:S(2)}) copy-start(s32[8]{0:T(128)} %sinks.3) | copy-start | bytes 100
  59.1 10.3 %copy-start.7 = (f32[8]{0:T(128)S(1)}, f32[8]{0:T(128)}, u32[]{:S(2)}) copy-start(f32[8]{0:T(128)} %bias.3) | copy-start | bytes 100
  69.4 29.0 %copy-start.3 = (bf16[512,512]{1,0:T(8,128)(2,1)}, bf16[512,512]{1,0:T(8,128)(2,1)S(1)}, u32[]{:S(2)}) copy-start(bf16[512,512]{1,0:T(8,128)(2,1)S(1)} %collective-permute-done.1.refs_2_) | copy-start | bytes 1572868
  69.5 1.3 copy-start.8
  98.4 19.7 %copy-start.1 = (bf16[512,512]{1,0:T(8,128)(2,1)}, bf16[512,512]{1,0:T(8,128)(2,1)S(1)}, u32[]{:S(2)}) copy-start(bf16[512,512]{1,0:T(8,128)(2,1)S(1)} %attend.2.own0) | copy-start | bytes 1572868
  98.4 26.5 %collective-permute-start.12 = (bf16[512,512]{1,0:T(8,128)(2,1)S(1)}, bf16[512,512]{1,0:T(8,128)(2,1)S(1)}, u32[]{:S(2)}, u32[]{:S(2)}) collective-permute-start(bf16[512,512]{1,0:T(8,128)(2,1)S(1)} %attend.2.own0), channel_id=1, source_target_pairs={{0,1},{1,0},{2,3},{3,2},{4,5},{5,4},{6,7},{7,6},{8,9},{9,8},{10,11... | collective-permute-start | bytes 1572872 | tf_op jit(solution)/shard_map/ppermute | solution.py:308
  98.5 1.2 copy-start.4
  118.0 18.4 %copy-start.2 = (bf16[512,512]{1,0:T(8,128)(2,1)}, bf16[512,512]{1,0:T(8,128)(2,1)S(1)}, u32[]{:S(2)}) copy-start(bf16[512,512]{1,0:T(8,128)(2,1)S(1)} %attend.3.own1) | copy-start | bytes 1572868
  118.0 18.4 %collective-permute-start.13 = (bf16[512,512]{1,0:T(8,128)(2,1)S(1)}, bf16[512,512]{1,0:T(8,128)(2,1)S(1)}, u32[]{:S(2)}, u32[]{:S(2)}) collective-permute-start(bf16[512,512]{1,0:T(8,128)(2,1)S(1)} %attend.3.own1), channel_id=1, source_target_pairs={{0,1},{1,0},{2,3},{3,2},{4,5},{5,4},{6,7},{7,6},{8,9},{9,8},{10,11... | collective-permute-start | bytes 1572872 | tf_op jit(solution)/shard_map/ppermute | solution.py:308
  124.9 11.6 %copy-start.9 = (bf16[512,512]{1,0:T(8,128)(2,1)}, bf16[512,512]{1,0:T(8,128)(2,1)S(1)}, u32[]{:S(2)}) copy-start(bf16[512,512]{1,0:T(8,128)(2,1)S(1)} %collective-permute-done.12.far0) | copy-start | bytes 1572868
  136.4 0.8 copy-start.10

commit v2 on v1

v2 whole, which is shorter than its diff:
```python
import functools

import jax
import jax.numpy as jnp
from jax import lax
from jax.experimental import pallas as pl
from jax.experimental.pallas import tpu as pltpu
from jax.sharding import PartitionSpec as P


HEAD_DIM = 128
PAIR = 2 * HEAD_DIM
SINK = 4
SINK_ROWS = 16
SPAN = 9
QUAD = (SPAN - 1) // 2
EPSILON = 1e-05
LOG2E = 1.4426950408889634
LOW = -1e30
UNROLL = 2
MIB = 1024 * 1024
ANY = pl.BlockSpec(memory_space=pl.ANY)
SMEM = pl.BlockSpec(memory_space=pltpu.SMEM)


def keys_values_kernel(place, tok_ref, gain_ref, wk_ref, wv_ref, w_hbm, *refs):
    groups = wk_ref.shape[1] // HEAD_DIM
    kv_refs, (sink_ref, scale_ref, send_hbm) = refs[:groups], refs[groups : groups + 3]
    k_acc, v_acc, squares, w_vmem, sem_in, sem_out = refs[groups + 3 :]
    step, steps = pl.program_id(0), pl.num_programs(0)
    piece = send_hbm.shape[1]
    columns = pl.ds(pl.multiple_of(place[0], HEAD_DIM), piece)
    fetch = pltpu.make_async_copy(w_hbm.at[:, columns], w_vmem, sem_in)
    store = pltpu.make_async_copy(w_vmem, send_hbm, sem_out)

    @pl.when(step == 0)
    def _():
        fetch.start()
        k_acc[...] = jnp.zeros(k_acc.shape, jnp.float32)
        v_acc[...] = jnp.zeros(v_acc.shape, jnp.float32)
        squares[...] = jnp.zeros(squares.shape, jnp.float32)

    @pl.when(step == steps // 2)
    def _():
        fetch.wait()
        store.start()

    widened = tok_ref[...].astype(jnp.float32)
    scaled = (widened * gain_ref[...]).astype(jnp.bfloat16)
    k_acc[...] += jnp.dot(scaled, wk_ref[...], preferred_element_type=jnp.float32)
    v_acc[...] += jnp.dot(scaled, wv_ref[...], preferred_element_type=jnp.float32)
    square = widened * widened
    total = square[:, :HEAD_DIM]
    for lo in range(HEAD_DIM, square.shape[1], HEAD_DIM):
        total += square[:, lo : lo + HEAD_DIM]
    squares[...] += total

    @pl.when(step == steps - 1)
    def _():
        mean = jnp.sum(squares[...], axis=1, keepdims=True) / (steps * tok_ref.shape[1])
        scale = jnp.broadcast_to(lax.rsqrt(mean + EPSILON), scale_ref.shape)
        scale_ref[...] = scale
        for g in range(groups):
            at = slice(g * HEAD_DIM, (g + 1) * HEAD_DIM)
            pair = jnp.concatenate([k_acc[:, at] * scale, v_acc[:, at] * scale], axis=1).astype(jnp.bfloat16)
            kv_refs[g][...] = pair
            sink_ref[:, g * PAIR : (g + 1) * PAIR] = pair[:SINK_ROWS]
        store.wait()


def keys_values(place, tokens, gain, w_key, w_value, w_out, piece):
    rows, width = tokens.shape
    narrow = w_key.shape[1]
    groups = narrow // HEAD_DIM
    chunk = width // 4
    fixed = lambda shape: pl.BlockSpec(shape, lambda i, place: (0, 0))
    return pl.pallas_call(
        keys_values_kernel,
        grid_spec=pltpu.PrefetchScalarGridSpec(
            num_scalar_prefetch=1,
            grid=(width // chunk,),
            in_specs=[
                pl.BlockSpec((rows, chunk), lambda i, place: (0, i)),
                pl.BlockSpec((1, chunk), lambda i, place: (0, i)),
                pl.BlockSpec((chunk, narrow), lambda i, place: (i, 0)),
                pl.BlockSpec((chunk, narrow), lambda i, place: (i, 0)),
                ANY,
            ],
            out_specs=[fixed((rows, PAIR))] * groups
            + [fixed((SINK_ROWS, groups * PAIR)), fixed((rows, HEAD_DIM)), ANY],
            scratch_shapes=[
                pltpu.VMEM((rows, narrow), jnp.float32),
                pltpu.VMEM((rows, narrow), jnp.float32),
                pltpu.VMEM((rows, HEAD_DIM), jnp.float32),
                pltpu.VMEM((w_out.shape[0], piece), jnp.bfloat16),
                pltpu.SemaphoreType.DMA,
                pltpu.SemaphoreType.DMA,
            ],
        ),
        out_shape=[jax.ShapeDtypeStruct((rows, PAIR), jnp.bfloat16)] * groups
        + [
            jax.ShapeDtypeStruct((SINK_ROWS, groups * PAIR), jnp.bfloat16),
            jax.ShapeDtypeStruct((rows, HEAD_DIM), jnp.float32),
            jax.ShapeDtypeStruct((w_out.shape[0], piece), jnp.bfloat16),
        ],
        compiler_params=pltpu.CompilerParams(vmem_limit_bytes=60 * MIB),
        cost_estimate=pl.CostEstimate(
            flops=4 * rows * width * narrow, bytes_accessed=2 * width * (rows + 2 * narrow), transcendentals=rows
        ),
        name="keys_values",
    )(place, tokens, gain, w_key, w_value, w_out)


def query_kernel(tok_ref, gain_ref, w_ref, scale_ref, q_ref, acc):
    step = pl.program_id(0)
    scaled = (tok_ref[...].astype(jnp.float32) * gain_ref[...]).astype(jnp.bfloat16)
    add = jnp.dot(scaled, w_ref[...], preferred_element_type=jnp.float32)

    @pl.when(step == 0)
    def _():
        acc[...] = add

    @pl.when(step > 0)
    def _():
        acc[...] += add

    @pl.when(step == pl.num_programs(0) - 1)
    def _():
        scale = scale_ref[...] * (HEAD_DIM**-0.5 * LOG2E)
        scale = jnp.concatenate([scale] * (acc.shape[1] // HEAD_DIM), axis=1)
        q_ref[...] = (acc[...] * scale).astype(jnp.bfloat16)


def query_group(group, groups, tokens, gain, w_query, scale):
    rows, width = tokens.shape
    share = w_query.shape[1] // groups
    chunk = width // 4
    return pl.pallas_call(
        query_kernel,
        grid=(width // chunk,),
        in_specs=[
            pl.BlockSpec((rows, chunk), lambda i: (0, i)),
            pl.BlockSpec((1, chunk), lambda i: (0, i)),
            pl.BlockSpec((chunk, share), lambda i: (i, group)),
            pl.BlockSpec(scale.shape, lambda i: (0, 0)),
        ],
        out_specs=pl.BlockSpec((rows, share), lambda i: (0, 0)),
        out_shape=jax.ShapeDtypeStruct((rows, share), jnp.bfloat16),
        scratch_shapes=[pltpu.VMEM((rows, share), jnp.float32)],
        compiler_params=pltpu.CompilerParams(vmem_limit_bytes=58 * MIB),
        cost_estimate=pl.CostEstimate(
            flops=2 * rows * width * share, bytes_accessed=2 * width * (rows + share), transcendentals=0
        ),
        name="query_group",
    )(tokens, gain, w_query, scale)


def attend_kernel(group, slots, meta, window, sinks, bias, q_ref, *refs):
    kv_refs, sink_ref, out_ref = refs[:slots], refs[slots], refs[slots + 1]
    kvbuf, sems, masked_items, whole_items, s_even, s_odd, x_even, x_odd, m_ref, acc_ref = refs[slots + 2 :]
    bufs = ((s_even, x_even), (s_odd, x_odd))
    rows = q_ref.shape[0]
    key_rows = kvbuf.shape[1]
    heads = q_ref.shape[1] // HEAD_DIM
    lanes = key_rows // HEAD_DIM
    copies = [
        pltpu.make_async_copy(ref, kvbuf.at[s, :, pl.ds(0, PAIR)], sems.at[s]) for s, ref in enumerate(kv_refs)
    ]
    for copy in copies:
        copy.start()
    kvbuf[:, :, PAIR:] = jnp.ones((slots, key_rows, HEAD_DIM), jnp.bfloat16)
    m_ref[...] = jnp.full(m_ref.shape, LOW, jnp.float32)
    acc_ref[...] = jnp.zeros(acc_ref.shape, jnp.float32)
    own = meta[0]
    query_start = own * rows

    def put(items, n, head, slot, gap):
        items[0, n] = head
        items[1, n] = slot
        items[2, n] = gap

    def scan(s, counts):
        block = meta[1 + s]
        gap = (own - block) * rows

        def add(head, counts):
            masked, whole = counts
            reach = window[group * heads + head]
            put(masked_items, masked, head, s, gap)
            put(whole_items, whole, head, s, gap)
            some = gap - (rows - 1) < reach
            full = (gap > 0) & (gap + rows - 1 < reach)
            return (
                masked + (some & jnp.logical_not(full)).astype(jnp.int32),
                whole + full.astype(jnp.int32),
            )

        return lax.fori_loop(0, jnp.where(block >= 0, heads, 0), add, counts)

    masked, whole = lax.fori_loop(0, slots, scan, (jnp.int32(0), jnp.int32(0)))
    for extra in range(UNROLL):
        put(masked_items, masked + extra, 0, 0, -rows)
        put(whole_items, whole + extra, 0, 0, -rows)
    diff = lax.broadcasted_iota(jnp.int32, (rows, key_rows), 0) - lax.broadcasted_iota(
        jnp.int32, (rows, key_rows), 1
    )
    for copy in copies:
        copy.wait()

    def queries_of(head):
        return q_ref[:, pl.ds(pl.multiple_of(head * HEAD_DIM, HEAD_DIM), HEAD_DIM)]

    def scores_of(head, keys):
        return lax.dot_general(
            queries_of(head), keys, (((1,), (1,)), ((), ())), preferred_element_type=jnp.float32
        )

    def score(items, i, buf, mask):
        head, slot = items[0, i], items[1, i]
        scores = scores_of(head, kvbuf[slot, :, :HEAD_DIM])
        if mask:
            gap = diff + items[2, i]
            scores = jnp.where((gap >= 0) & (gap < window[group * heads + head]), scores, LOW)
        buf[0][...] = scores
        top = scores[:, :HEAD_DIM]
        for part in range(1, lanes):
            top = jnp.maximum(top, scores[:, part * HEAD_DIM : (part + 1) * HEAD_DIM])
        buf[1][...] = top

    def fold(head, scores, top, vaug):
        m_prev = m_ref[head]
        m_new = jnp.maximum(m_prev, jnp.max(top, axis=1, keepdims=True))
        alpha = jnp.exp2(m_prev - m_new)
        m_ref[head] = m_new
        shift = jnp.concatenate([m_new] * (scores.shape[1] // HEAD_DIM), axis=1)
        weights = jnp.exp2(scores - shift).astype(jnp.bfloat16)
        add = jnp.dot(weights, vaug, preferred_element_type=jnp.float32)
        acc_ref[head] = acc_ref[head] * jnp.concatenate([alpha, alpha], axis=1) + add

    def consume(items, i, buf):
        fold(items[0, i], buf[0][...], buf[1][...], kvbuf[items[1, i], :, HEAD_DIM:])

    def turns(items, first, count, mask):
        score(items, first, bufs[0], mask)

        def turn(j, carry):
            for u in range(UNROLL):
                i = first + UNROLL * j + u
                score(items, i + 1, bufs[(u + 1) % 2], mask)
                consume(items, i, bufs[u % 2])
            return carry

        lax.fori_loop(0, count, turn, 0)

    turns(masked_items, 0, (masked + UNROLL - 1) // UNROLL, True)
    rest = lax.rem(whole, UNROLL)

    def single(i, carry):
        score(whole_items, i, bufs[0], False)
        consume(whole_items, i, bufs[0])
        return carry

    lax.fori_loop(0, rest, single, 0)
    turns(whole_items, rest, whole // UNROLL, False)

    def finish(head, carry):
        reach = window[group * heads + head]

        @pl.when(query_start + rows - 1 - reach >= 0)
        def _():
            base = group * PAIR
            pad = jnp.zeros((HEAD_DIM - SINK_ROWS, HEAD_DIM), jnp.bfloat16)
            keys = jnp.concatenate([sink_ref[:, base : base + HEAD_DIM], pad], axis=0)
            values = jnp.concatenate([sink_ref[:, base + HEAD_DIM : base + PAIR], pad], axis=0)
            vaug = jnp.concatenate([values, jnp.ones((HEAD_DIM, HEAD_DIM), jnp.bfloat16)], axis=1)
            column = lax.broadcasted_iota(jnp.int32, (rows, HEAD_DIM), 1)
            latest = lax.broadcasted_iota(jnp.int32, (rows, HEAD_DIM), 0) + (query_start - reach)
            count = jnp.minimum(sinks[group * heads + head], SINK)
            allowed = (column < count) & (column <= latest)
            scores = scores_of(head, keys) + bias[group * heads + head] * LOG2E
            scores = jnp.where(allowed, scores, LOW)
            fold(head, scores, scores, vaug)

        out_ref[:, pl.ds(pl.multiple_of(head * HEAD_DIM, HEAD_DIM), HEAD_DIM)] = (
            acc_ref[head, :, :HEAD_DIM] / acc_ref[head, :, HEAD_DIM:]
        ).astype(jnp.bfloat16)
        return carry

    lax.fori_loop(0, heads, finish, 0)


def attend(group, meta, window, sink_count, sink_bias, queries, blocks, sink_rows):
    rows, share = queries.shape
    heads = share // HEAD_DIM
    slots = len(blocks)
    key_rows = blocks[0].shape[0]
    items = heads * slots + 2 * UNROLL
    f32 = jnp.float32
    return pl.pallas_call(
        functools.partial(attend_kernel, group, slots),
        grid=(1,),
        in_specs=[SMEM] * 4
        + [pl.BlockSpec((rows, share), lambda i: (0, 0))]
        + [ANY] * slots
        + [pl.BlockSpec(sink_rows.shape, lambda i: (0, 0))],
        out_specs=pl.BlockSpec((rows, share), lambda i: (0, 0)),
        out_shape=jax.ShapeDtypeStruct((rows, share), jnp.bfloat16),
        scratch_shapes=[
            pltpu.VMEM((slots, key_rows, 3 * HEAD_DIM), jnp.bfloat16),
            pltpu.SemaphoreType.DMA((slots,)),
            pltpu.SMEM((3, items), jnp.int32),
            pltpu.SMEM((3, items), jnp.int32),
            pltpu.VMEM((rows, key_rows), f32),
            pltpu.VMEM((rows, key_rows), f32),
            pltpu.VMEM((rows, HEAD_DIM), f32),
            pltpu.VMEM((rows, HEAD_DIM), f32),
            pltpu.VMEM((heads, rows, HEAD_DIM), f32),
            pltpu.VMEM((heads, rows, PAIR), f32),
        ],
        compiler_params=pltpu.CompilerParams(vmem_limit_bytes=60 * MIB),
        cost_estimate=pl.CostEstimate(
            flops=8 * rows * SPAN * key_rows * share,
            bytes_accessed=2 * slots * key_rows * PAIR,
            transcendentals=rows * SPAN * key_rows * heads,
        ),
        name="attend",
    )(meta, window, sink_count, sink_bias, queries, *blocks, sink_rows)


def project_kernel(where, tok_ref, own0, own1, w_ref, out_ref):
    half = own0.shape[1]
    total = jnp.dot(own0[...], w_ref[:half, :], preferred_element_type=jnp.float32)
    total += jnp.dot(own1[...], w_ref[half:, :], preferred_element_type=jnp.float32)
    out_ref[...] = tok_ref[...].astype(jnp.float32) + total


def project_last_kernel(where, part_ref, far0, far1, wa_ref, wb_ref, out_ref):
    step = pl.program_id(0)
    half = far0.shape[1]

    def finish(w):
        more = jnp.dot(far0[...], w[:half, :], preferred_element_type=jnp.float32)
        more += jnp.dot(far1[...], w[half:, :], preferred_element_type=jnp.float32)
        out_ref[...] = (part_ref[...] + more).astype(jnp.bfloat16)

    @pl.when(step < pl.num_programs(0) // 2)
    def _():
        finish(wa_ref)

    @pl.when(step >= pl.num_programs(0) // 2)
    def _():
        finish(wb_ref)


def project(where, tokens, own, w_out, share):
    rows = tokens.shape[0]
    depth = w_out.shape[0]
    tile = 512
    steps = share // tile
    shifted = lambda j, where: (0, where[0] * steps + j)
    fixed = lambda a: pl.BlockSpec(a.shape, lambda j, where: (0, 0))
    return pl.pallas_call(
        project_kernel,
        grid_spec=pltpu.PrefetchScalarGridSpec(
            num_scalar_prefetch=1,
            grid=(steps,),
            in_specs=[pl.BlockSpec((rows, tile), shifted), fixed(own[0]), fixed(own[1])]
            + [pl.BlockSpec((depth, tile), shifted)],
            out_specs=pl.BlockSpec((rows, tile), lambda j, where: (0, j)),
        ),
        out_shape=jax.ShapeDtypeStruct((rows, share), jnp.float32),
        compiler_params=pltpu.CompilerParams(vmem_limit_bytes=40 * MIB),
        cost_estimate=pl.CostEstimate(
            flops=2 * rows * depth * share, bytes_accessed=2 * depth * share + 6 * rows * share, transcendentals=0
        ),
        name="project",
    )(where, tokens, own[0], own[1], w_out)


def project_last(where, partial, far, w_near, w_swap):
    rows, share = partial.shape
    depth, _ = w_near.shape
    tile = 512
    steps = share // tile
    part = steps // 2

    def here(j, where):
        return (0, jnp.where(where[1] == 0, j, lax.rem(j + part, steps)))

    fixed = lambda a: pl.BlockSpec(a.shape, lambda j, where: (0, 0))
    return pl.pallas_call(
        project_last_kernel,
        grid_spec=pltpu.PrefetchScalarGridSpec(
            num_scalar_prefetch=1,
            grid=(steps,),
            in_specs=[
                pl.BlockSpec((rows, tile), here),
                fixed(far[0]),
                fixed(far[1]),
                pl.BlockSpec((depth, tile), lambda j, where: (0, jnp.minimum(j, part - 1))),
                pl.BlockSpec((depth, tile), lambda j, where: (0, jnp.maximum(j - part, 0))),
            ],
            out_specs=pl.BlockSpec((rows, tile), here),
        ),
        out_shape=jax.ShapeDtypeStruct((rows, share), jnp.bfloat16),
        compiler_params=pltpu.CompilerParams(vmem_limit_bytes=40 * MIB),
        cost_estimate=pl.CostEstimate(
            flops=2 * rows * depth * share, bytes_accessed=2 * depth * share + 6 * rows * share, transcendentals=0
        ),
        name="project_last",
    )(where, partial, far[0], far[1], w_near, w_swap)


def local(tokens, norm_gain, w_query, w_key, w_value, w_out, window, sink_count, sink_bias):
    peers = lax.axis_size("seq")
    head_peers = lax.axis_size("head")
    me = lax.axis_index("seq")
    my_head = lax.axis_index("head")
    core, side = me % 2, (me // 2) % 2
    groups = w_key.shape[1] // HEAD_DIM
    share = w_out.shape[1] // head_peers
    piece = share // 2
    gain = norm_gain.reshape(1, -1)
    everyone = range(peers)

    def send(x, pairs, axis="seq"):
        return lax.ppermute(x, axis, pairs)

    ahead = [(i, i + QUAD) for i in range(peers - QUAD)]
    core_swap = [(i, i ^ 1) for i in everyone]
    core_up = [(i, i + 1) for i in everyone if i % 2 == 0]
    core_down = [(i, i - 1) for i in everyone if i % 2 == 1]
    side_swap = [(i, i ^ 2) for i in everyone]
    side_up = [(i, i + 2) for i in everyone if (i // 2) % 2 == 0]
    side_down = [(i, i - 2) for i in everyone if (i // 2) % 2 == 1]
    cross_up = [(i, i ^ 1) for i in everyone if (i // 2) % 2 == 1]
    cross_down = [(i, i ^ 1) for i in everyone if (i // 2) % 2 == 0]
    head_swap = [(i, i ^ 1) for i in range(head_peers)]

    twin, across, mirror = me ^ 1, me ^ 2, me ^ 3
    index = [
        me,
        me - 4,
        twin - 4,
        jnp.where(core == 1, me - 1, -1),
        jnp.where(core == 0, me - 7, -1),
        across - 4,
        mirror - 4,
        jnp.where(side == 1, me - 2, -1),
        jnp.where(side == 0, me - 6, -1),
        jnp.where(side == 1, twin - 2, -1),
        jnp.where(side == 0, twin - 6, -1),
        me - 8,
    ]
    meta = jnp.stack([me] + index).astype(jnp.int32)
    place = ((1 - my_head) * share + core * piece).astype(jnp.int32).reshape(1)

    *kv, sink_rows, scale, w_send = keys_values(place, tokens, gain, w_key, w_value, w_out, piece)

    back4 = [send(x, ahead) for x in kv]
    near_side = [send(x, side_up) for x in kv]
    near_core = [send(x, core_up) for x in kv]
    w_near = send(w_send, head_swap, "head")

    def spread(rows, have):
        step = have // 2
        arrived = send(rows, [(i, i + step) for i in range(0, peers, have)])
        return jnp.where(me % have == step, arrived, rows), step

    have = peers
    queries, blocks = [], []
    for g in range(groups):
        queries.append(query_group(g, groups, tokens, gain, w_query, scale))
        b4, ns = back4[g], near_side[g]
        b8 = send(b4, ahead)
        across4 = send(b4, side_swap)
        far_side = send(b8, side_down)
        blocks.append(
            [
                kv[g],
                b4,
                send(b4, core_swap),
                near_core[g],
                send(b8, core_down),
                across4,
                send(across4, core_swap),
                ns,
                far_side,
                send(ns, cross_up),
                send(far_side, cross_down),
                b8,
            ]
        )
    while have > 1:
        sink_rows, have = spread(sink_rows, have)
    w_swap = send(w_near, core_swap)

    own, far = [], []
    for g in range(groups):
        att = attend(g, meta, window, sink_count, sink_bias, queries[g], blocks[g], sink_rows)
        own.append(att)
        far.append(send(att, head_swap, "head"))
    where = jnp.stack([my_head, core]).astype(jnp.int32)
    partial = project(where, tokens, own, w_out, share)
    return project_last(where, partial, far, w_near, w_swap)


def solution(mesh):
    in_specs = (
        P("seq", None),
        P(),
        P(None, "head"),
        P(None, "head"),
        P(None, "head"),
        P("head", None),
        P("head"),
        P("head"),
        P("head"),
    )
    out_specs = P("seq", "head")
    return jax.shard_map(local, mesh=mesh, in_specs=in_specs, out_specs=out_specs, check_vma=False)
```

time: 148 us -> 133 us (0.90)
  waiting for transfers between devices: 41.5 us -> 18.7 us
  starting transfers between devices: 21.7 us -> 44 us
  matrix products: 10.2 us -> 0 us
  local copies, waits for them, and re-layouts: 7.17 us -> 3.91 us
  other arithmetic: 3.26 us -> 1.42 us
    ppermute x16 -> x30, waiting for transfers between devices: 41.5 us -> 18.7 us  [send(): return lax.ppermute(x, axis, pairs)]
    ppermute x16 -> x30, starting transfers between devices: 21.7 us -> 44 us  [send(): return lax.ppermute(x, axis, pairs)]
    pallas_call x1 -> x4, Pallas kernels: 7.18 us -> 26.3 us  [the longest x2 13.3 us: query_group(): pl.pallas_call(query_kernel, grid=(width // chunk,), in_specs=[pl.BlockSp...]
    pallas_call x2, Pallas kernels: 45.9 us -> 31.7 us  [attend(): pl.pallas_call(functools.partial(attend_kernel, group, slots), grid=(1,),...]
    dot_general x1 -> x0, matrix products: 10.2 us -> none  [local(): jnp.dot(normed, w_query, preferred_element_type=jnp.float32)]
    pallas_call x1, Pallas kernels: 10.7 us -> 5.58 us  [project(): pl.pallas_call(project_kernel, grid_spec=pltpu.PrefetchScalarGridSpec(num...]
    dynamic_slice x1 -> x0, local copies, waits for them, and re-layouts: 3.08 us -> none  [local(): lax.dynamic_slice_in_dim(w_out, (1 - my_head) * share + core * piece, pie...]
    unnamed x22 -> x32, local copies, waits for them, and re-layouts: 3.29 us -> 3.29 us
  transfers between devices with their start and end apart: 16 -> 30, of which waited for: 5 -> 6; matrix products, arithmetic and copies ran while one was open for 10% -> 2% of each run, Pallas kernels for 36% -> 38%
where the time goes in v2:
time: 133 us; the launch traced here: 132 us
  Pallas kernels  63.6 us (48%)
  starting transfers between devices  44 us (33%)
  waiting for transfers between devices  18.7 us (14%)
  local copies, waits for them, and re-layouts  3.91 us (3%)
  other arithmetic  1.42 us (1%)
    ppermute x30, starting transfers between devices, send(): return lax.ppermute(x, axis, pairs)  44 us
    pallas_call x2, Pallas kernels, attend(): pl.pallas_call(functools.partial(attend_kernel, group, slots), grid=(1,),...  31.7 us
    ppermute x30, waiting for transfers between devices, send(): return lax.ppermute(x, axis, pairs)  18.7 us
    pallas_call x2, Pallas kernels, query_group(): pl.pallas_call(query_kernel, grid=(width // chunk,), in_specs=[pl.BlockSp...  13.3 us
    pallas_call x1, Pallas kernels, keys_values(): pl.pallas_call(keys_values_kernel, grid_spec=pltpu.PrefetchScalarGridSpec...  6.62 us
    pallas_call x1, Pallas kernels, project_last(): pl.pallas_call(project_last_kernel, grid_spec=pltpu.PrefetchScalarGridSpe...  6.41 us
    pallas_call x1, Pallas kernels, project(): pl.pallas_call(project_kernel, grid_spec=pltpu.PrefetchScalarGridSpec(num...  5.58 us
    unnamed x32, local copies, waits for them, and re-layouts  3.29 us
  transfers between devices with their start and end apart: 30, of which 6 were waited for; matrix products, arithmetic and copies ran while one was open for 2% of the time, Pallas kernels for 38%

profile of v2, /device:TPU:18, one launch (start us, length us, event | category | flops | bytes accessed | tf_op | source)
XLA Modules:
  0.0 132.2 jit_solution(5090174870048562382)
XLA Ops:
  0.0 6.6 %keys_values.1 = (bf16[512,256]{1,0:T(8,128)(2,1)}, bf16[512,256]{1,0:T(8,128)(2,1)}, bf16[16,512]{1,0:T(8,128)(2,1)}, f32[512,128]{1,0:T(8,128)}, bf16[1024,1024]{1,0:T(8,128)(2,1)}) custom-call(s32[1]{0:T(128)} %bitcast.15.place, bf16[512,4096]{1,0:T(8,128)(2,1)} %tok_ref.7, f32[1,4096]{1,0:T(1,128)} %bitcast.16, bf16[4096,256]{1,0:T(8,128)(2,1)} %wk_ref.1, ...), custom_call_target="tpu_custom_call" | custom-call | flops 2147483648 | bytes 8388608 | tf_op jit(solution)/shard_map/keys_values/pallas_call | solution.py:77
  6.6 1.6 %collective-permute-start.28 = (bf16[1024,1024]{1,0:T(8,128)(2,1)}, bf16[1024,1024]{1,0:T(8,128)(2,1)S(1)}, u32[]{:S(2)}, u32[]{:S(2)}) collective-permute-start(bf16[1024,1024]{1,0:T(8,128)(2,1)} %get-tuple-element.14), channel_id=1, source_target_pairs={{0,1},{1,0},{2,3},{3,2},{4,5},{5,4},{6,7},{7,6},{8,9},{9,8},{10,11... | collective-permute-start | bytes 6291464 | tf_op jit(solution)/shard_map/ppermute | solution.py:427
  8.2 0.7 collective-permute-start.11
  8.9 0.7 broadcast_select_fusion
  9.6 0.7 collective-permute-start.12
  10.3 1.3 collective-permute-start.7
  11.6 1.5 %collective-permute-start.2 = (bf16[512,256]{1,0:T(8,128)(2,1)}, bf16[512,256]{1,0:T(8,128)(2,1)S(1)}, u32[]{:S(2)}, u32[]{:S(2)}) collective-permute-start(bf16[512,256]{1,0:T(8,128)(2,1)} %get-tuple-element.11.refs_0_), channel_id=1, source_target_pairs={{0,2},{4,6},{8,10},{12,14},{16,18},{20,22},{24,26},{28,30},{1,3},{... | collective-permute-start | bytes 786440 | tf_op jit(solution)/shard_map/ppermute | solution.py:427
  13.1 1.3 collective-permute-start.13
  14.4 8.4 %collective-permute-done.13 = bf16[16,512]{1,0:T(8,128)(2,1)S(1)} collective-permute-done((bf16[16,512]{1,0:T(8,128)(2,1)S(1)}, bf16[16,512]{1,0:T(8,128)(2,1)S(1)}, u32[]{:S(2)}, u32[]{:S(2)}) %collective-permute-start.13) | collective-permute-done | bytes 16416 | tf_op jit(solution)/shard_map/ppermute | solution.py:427
  22.8 1.3 collective-permute-start.14
  24.1 2.6 %collective-permute-start = (bf16[512,256]{1,0:T(8,128)(2,1)}, bf16[512,256]{1,0:T(8,128)(2,1)S(1)}, u32[]{:S(2)}, u32[]{:S(2)}) collective-permute-start(bf16[512,256]{1,0:T(8,128)(2,1)} %get-tuple-element.11.refs_0_), channel_id=1, source_target_pairs={{0,8},{2,10},{4,12},{6,14},{8,16},{10,18},{12,20},{14,22},{16,24},... | collective-permute-start | bytes 786440 | tf_op jit(solution)/shard_map/ppermute | solution.py:427
  26.7 1.3 collective-permute-start.22
  28.0 1.3 collective-permute-start.17
  29.4 1.9 %collective-permute-start.15 = (bf16[512,256]{1,0:T(8,128)(2,1)}, bf16[512,256]{1,0:T(8,128)(2,1)S(1)}, u32[]{:S(2)}, u32[]{:S(2)}) collective-permute-start(bf16[512,256]{1,0:T(8,128)(2,1)} %get-tuple-element.13.refs_0_), channel_id=1, source_target_pairs={{0,8},{2,10},{4,12},{6,14},{8,16},{10,18},{12,20},{14,22},{16,24},... | collective-permute-start | bytes 786440 | tf_op jit(solution)/shard_map/ppermute | solution.py:427
  31.3 1.3 collective-permute-done.refs_1_
  32.6 1.9 %collective-permute-start.9 = (bf16[512,256]{1,0:T(8,128)(2,1)S(1)}, bf16[512,256]{1,0:T(8,128)(2,1)S(1)}, u32[]{:S(2)}, u32[]{:S(2)}) collective-permute-start(bf16[512,256]{1,0:T(8,128)(2,1)S(1)} %collective-permute-done.7.refs_7_), channel_id=1, source_target_pairs={{4,6},{6,4},{12,14},{14,12},{20,22},{22,20},{28,30},{30,28},{5,7},... | collective-permute-start | bytes 786440 | tf_op jit(solution)/shard_map/ppermute | solution.py:427
  34.5 1.1 collective-permute-done.22.refs_7_
  35.6 2.6 %collective-permute-start.3 = (bf16[512,256]{1,0:T(8,128)(2,1)S(1)}, bf16[512,256]{1,0:T(8,128)(2,1)}, u32[]{:S(2)}, u32[]{:S(2)}) collective-permute-start(bf16[512,256]{1,0:T(8,128)(2,1)S(1)} %collective-permute-done.refs_1_), channel_id=1, source_target_pairs={{0,8},{2,10},{4,12},{6,14},{8,16},{10,18},{12,20},{14,22},{16,24},... | collective-permute-start | bytes 786440 | tf_op jit(solution)/shard_map/ppermute | solution.py:427
  38.2 0.1 collective-permute-start.1
  38.3 2.4 %collective-permute-start.24 = (bf16[512,256]{1,0:T(8,128)(2,1)S(1)}, bf16[512,256]{1,0:T(8,128)(2,1)S(1)}, u32[]{:S(2)}, u32[]{:S(2)}) collective-permute-start(bf16[512,256]{1,0:T(8,128)(2,1)S(1)} %collective-permute-done.22.refs_7_), channel_id=1, source_target_pairs={{4,6},{6,4},{12,14},{14,12},{20,22},{22,20},{28,30},{30,28},{5,7},... | collective-permute-start | bytes 786440 | tf_op jit(solution)/shard_map/ppermute | solution.py:427
  40.7 2.7 %collective-permute-done.5.refs_5_ = bf16[512,256]{1,0:T(8,128)(2,1)} collective-permute-done((bf16[512,256]{1,0:T(8,128)(2,1)S(1)}, bf16[512,256]{1,0:T(8,128)(2,1)}, u32[]{:S(2)}, u32[]{:S(2)}) %collective-permute-start.5) | collective-permute-done | bytes 262176 | tf_op jit(solution)/shard_map/ppermute | solution.py:427
  43.4 0.3 collective-permute-start.20
  43.7 1.6 %collective-permute-done.3.refs_11_ = bf16[512,256]{1,0:T(8,128)(2,1)} collective-permute-done((bf16[512,256]{1,0:T(8,128)(2,1)S(1)}, bf16[512,256]{1,0:T(8,128)(2,1)}, u32[]{:S(2)}, u32[]{:S(2)}) %collective-permute-start.3) | collective-permute-done | bytes 262176 | tf_op jit(solution)/shard_map/ppermute | solution.py:427
  45.3 2.6 %collective-permute-start.18 = (bf16[512,256]{1,0:T(8,128)(2,1)S(1)}, bf16[512,256]{1,0:T(8,128)(2,1)}, u32[]{:S(2)}, u32[]{:S(2)}) collective-permute-start(bf16[512,256]{1,0:T(8,128)(2,1)S(1)} %collective-permute-done.15.refs_1_), channel_id=1, source_target_pairs={{0,8},{2,10},{4,12},{6,14},{8,16},{10,18},{12,20},{14,22},{16,24},... | collective-permute-start | bytes 786440 | tf_op jit(solution)/shard_map/ppermute | solution.py:427
  48.0 4.3 %collective-permute-start.8 = (bf16[512,256]{1,0:T(8,128)(2,1)}, bf16[512,256]{1,0:T(8,128)(2,1)}, u32[]{:S(2)}, u32[]{:S(2)}) collective-permute-start(bf16[512,256]{1,0:T(8,128)(2,1)} %collective-permute-done.3.refs_11_), channel_id=1, source_target_pairs={{4,0},{6,2},{12,8},{14,10},{20,16},{22,18},{28,24},{30,26},{5,1},{... | collective-permute-start | bytes 786440 | tf_op jit(solution)/shard_map/ppermute | solution.py:427
  52.3 6.6 %query_group.3.q_ref = bf16[512,512]{1,0:T(8,128)(2,1)} custom-call(bf16[512,4096]{1,0:T(8,128)(2,1)} %tok_ref.7, f32[1,4096]{1,0:T(1,128)} %bitcast.17, bf16[4096,1024]{1,0:T(8,128)(2,1)} %w_ref.4, f32[512,128]{1,0:T(8,128)} %get-tuple-element.10.scale_ref), custom_call_target="tpu_custom_call" | custom-call | flops 2147483648 | bytes 8388608 | tf_op jit(solution)/shard_map/query_group/pallas_call | solution.py:138
  59.0 1.3 collective-permute-start.4
  60.3 1.2 collective-permute-start.6
  61.5 1.3 collective-permute-start.23
  62.8 1.5 %collective-permute-start.10 = (bf16[512,256]{1,0:T(8,128)(2,1)}, bf16[512,256]{1,0:T(8,128)(2,1)}, u32[]{:S(2)}, u32[]{:S(2)}) collective-permute-start(bf16[512,256]{1,0:T(8,128)(2,1)} %collective-permute-done.8.refs_8_), channel_id=1, source_target_pairs={{0,2},{2,0},{8,10},{10,8},{16,18},{18,16},{24,26},{26,24},{1,3},{3... | collective-permute-start | bytes 786440 | tf_op jit(solution)/shard_map/ppermute | solution.py:427
  64.4 6.6 %query_group.2.q_ref = bf16[512,512]{1,0:T(8,128)(2,1)} custom-call(bf16[512,4096]{1,0:T(8,128)(2,1)} %tok_ref.7, f32[1,4096]{1,0:T(1,128)} %bitcast.18, bf16[4096,1024]{1,0:T(8,128)(2,1)} %w_ref.4, f32[512,128]{1,0:T(8,128)} %get-tuple-element.10.scale_ref), custom_call_target="tpu_custom_call" | custom-call | flops 2147483648 | bytes 8388608 | tf_op jit(solution)/shard_map/query_group/pallas_call | solution.py:138
  71.0 0.6 stack.64.meta
  71.6 0.6 broadcast_select_fusion.3.refs_12_
  72.2 0.0 collective-permute-start.16
  72.3 1.3 collective-permute-start.19
  73.6 1.8 %collective-permute-start.21 = (bf16[512,256]{1,0:T(8,128)(2,1)S(1)}, bf16[512,256]{1,0:T(8,128)(2,1)}, u32[]{:S(2)}, u32[]{:S(2)}) collective-permute-start(bf16[512,256]{1,0:T(8,128)(2,1)S(1)} %copy-done.12), channel_id=1, source_target_pairs={{0,2},{2,0},{4,6},{6,4},{8,10},{10,8},{12,14},{14,12},{16,18},{18,... | collective-permute-start | bytes 786440 | tf_op jit(solution)/shard_map/ppermute | solution.py:427
  75.4 1.4 %collective-permute-start.25 = (bf16[512,256]{1,0:T(8,128)(2,1)S(1)}, bf16[512,256]{1,0:T(8,128)(2,1)}, u32[]{:S(2)}, u32[]{:S(2)}) collective-permute-start(bf16[512,256]{1,0:T(8,128)(2,1)S(1)} %collective-permute-done.23.refs_8_), channel_id=1, source_target_pairs={{0,2},{2,0},{8,10},{10,8},{16,18},{18,16},{24,26},{26,24},{1,3},{3... | collective-permute-start | bytes 786440 | tf_op jit(solution)/shard_map/ppermute | solution.py:427
  76.8 0.0 collective-permute-start.29
  76.8 16.6 %attend.2.own0 = bf16[512,512]{1,0:T(8,128)(2,1)} custom-call(s32[13]{0:T(128)} %stack.64.meta, s32[8]{0:T(128)} %window.3, s32[8]{0:T(128)} %sinks.3, f32[8]{0:T(128)} %bias.3, bf16[512,512]{1,0:T(8,128)(2,1)} %query_group.2.q_ref, bf16[512,256]{1,0:T(8,128)(2,1)} %get-tuple-element.11.refs_0_, bf16[512,256]{1,0:T(8,128)(2,1)} %copy-done.8, ...), custom_call_target="tpu_custom_call" | custom-call | flops 9663676416 | bytes 3145728 | tf_op jit(solution)/shard_map/attend/pallas_call | solution.py:299
  93.5 0.1 collective-permute-start.26
  93.6 15.1 %attend.3.own1 = bf16[512,512]{1,0:T(8,128)(2,1)} custom-call(s32[13]{0:T(128)} %stack.64.meta, s32[8]{0:T(128)} %window.3, s32[8]{0:T(128)} %sinks.3, f32[8]{0:T(128)} %bias.3, bf16[512,512]{1,0:T(8,128)(2,1)} %query_group.3.q_ref, bf16[512,256]{1,0:T(8,128)(2,1)} %get-tuple-element.13.refs_0_, bf16[512,256]{1,0:T(8,128)(2,1)} %copy-done.7, ...), custom_call_target="tpu_custom_call" | custom-call | flops 9663676416 | bytes 3145728 | tf_op jit(solution)/shard_map/attend/pallas_call | solution.py:299
  108.7 4.6 %collective-permute-start.27 = (bf16[512,512]{1,0:T(8,128)(2,1)}, bf16[512,512]{1,0:T(8,128)(2,1)S(1)}, u32[]{:S(2)}, u32[]{:S(2)}) collective-permute-start(bf16[512,512]{1,0:T(8,128)(2,1)} %attend.3.own1), channel_id=1, source_target_pairs={{0,1},{1,0},{2,3},{3,2},{4,5},{5,4},{6,7},{7,6},{8,9},{9,8},{10,11... | collective-permute-start | bytes 1572872 | tf_op jit(solution)/shard_map/ppermute | solution.py:427
  113.3 0.1 pad_add_fusion.where
  113.4 2.2 %copy-done = bf16[512,4096]{1,0:T(8,128)(2,1)S(1)} copy-done((bf16[512,4096]{1,0:T(8,128)(2,1)S(1)}, bf16[512,4096]{1,0:T(8,128)(2,1)}, u32[]{:S(2)}) %copy-start) | copy-done | bytes 4194328
  115.6 1.0 copy-done.2
  116.6 5.6 %project.1.part_ref = f32[512,2048]{1,0:T(8,128)S(1)} custom-call(s32[2]{0:T(128)S(1)} %pad_add_fusion.where, bf16[512,4096]{1,0:T(8,128)(2,1)S(1)} %copy-done, bf16[512,512]{1,0:T(8,128)(2,1)S(1)} %copy-done.1, bf16[512,512]{1,0:T(8,128)(2,1)S(1)} %copy-done.2, bf16[1024,4096]{1,0:T(8,128)(2,1)} %w_ref.5), custom_call_target="tpu_custom_call" | custom-call | flops 2147483648 | bytes 10485760 | tf_op jit(solution)/shard_map/project/pallas_call | solution.py:362
  122.2 3.6 %collective-permute-done.27.far1 = bf16[512,512]{1,0:T(8,128)(2,1)S(1)} collective-permute-done((bf16[512,512]{1,0:T(8,128)(2,1)}, bf16[512,512]{1,0:T(8,128)(2,1)S(1)}, u32[]{:S(2)}, u32[]{:S(2)}) %collective-permute-start.27) | collective-permute-done | bytes 524320 | tf_op jit(solution)/shard_map/ppermute | solution.py:427
  125.8 6.4 %project_last.1 = bf16[512,2048]{1,0:T(8,128)(2,1)} custom-call(s32[2]{0:T(128)S(1)} %pad_add_fusion.where, f32[512,2048]{1,0:T(8,128)S(1)} %project.1.part_ref, bf16[512,512]{1,0:T(8,128)(2,1)S(1)} %collective-permute-done.26.far0, bf16[512,512]{1,0:T(8,128)(2,1)S(1)} %collective-permute-done.27.far1, ...), custom_call_target="tpu_custom_call" | custom-call | flops 2147483648 | bytes 10485760 | tf_op jit(solution)/shard_map/project_last/pallas_call | solution.py:391
  (57 shorter events, 0.1 us)
Async XLA Ops:
  6.6 70.2 %collective-permute-start.28 = (bf16[1024,1024]{1,0:T(8,128)(2,1)}, bf16[1024,1024]{1,0:T(8,128)(2,1)S(1)}, u32[]{:S(2)}, u32[]{:S(2)}) collective-permute-start(bf16[1024,1024]{1,0:T(8,128)(2,1)} %get-tuple-element.14), channel_id=1, source_target_pairs={{0,1},{1,0},{2,3},{3,2},{4,5},{5,4},{6,7},{7,6},{8,9},{9,8},{10,11... | collective-permute-start | bytes 6291464 | tf_op jit(solution)/shard_map/ppermute | solution.py:427
  8.2 0.7 collective-permute-start.11
  9.6 3.5 %collective-permute-start.12 = (bf16[16,512]{1,0:T(8,128)(2,1)S(1)}, bf16[16,512]{1,0:T(8,128)(2,1)S(1)}, u32[]{:S(2)}, u32[]{:S(2)}) collective-permute-start(bf16[16,512]{1,0:T(8,128)(2,1)S(1)} %broadcast_select_fusion), channel_id=1, source_target_pairs={{0,8},{16,24},{1,9},{17,25}} | collective-permute-start | bytes 49160 | tf_op jit(solution)/shard_map/ppermute | solution.py:427
  10.3 17.7 %collective-permute-start.7 = (bf16[512,256]{1,0:T(8,128)(2,1)}, bf16[512,256]{1,0:T(8,128)(2,1)S(1)}, u32[]{:S(2)}, u32[]{:S(2)}) collective-permute-start(bf16[512,256]{1,0:T(8,128)(2,1)} %get-tuple-element.11.refs_0_), channel_id=1, source_target_pairs={{0,4},{2,6},{8,12},{10,14},{16,20},{18,22},{24,28},{26,30},{1,5},{... | collective-permute-start | bytes 786440 | tf_op jit(solution)/shard_map/ppermute | solution.py:427
  11.6 17.8 %collective-permute-start.2 = (bf16[512,256]{1,0:T(8,128)(2,1)}, bf16[512,256]{1,0:T(8,128)(2,1)S(1)}, u32[]{:S(2)}, u32[]{:S(2)}) collective-permute-start(bf16[512,256]{1,0:T(8,128)(2,1)} %get-tuple-element.11.refs_0_), channel_id=1, source_target_pairs={{0,2},{4,6},{8,10},{12,14},{16,18},{20,22},{24,26},{28,30},{1,3},{... | collective-permute-start | bytes 786440 | tf_op jit(solution)/shard_map/ppermute | solution.py:427
  13.1 9.7 %collective-permute-start.13 = (bf16[16,512]{1,0:T(8,128)(2,1)S(1)}, bf16[16,512]{1,0:T(8,128)(2,1)S(1)}, u32[]{:S(2)}, u32[]{:S(2)}) collective-permute-start(bf16[16,512]{1,0:T(8,128)(2,1)S(1)} %broadcast_select_fusion.1), channel_id=1, source_target_pairs={{0,4},{8,12},{16,20},{24,28},{1,5},{9,13},{17,21},{25,29}} | collective-permute-start | bytes 49160 | tf_op jit(solution)/shard_map/ppermute | solution.py:427
  22.8 3.9 %collective-permute-start.14 = (bf16[16,512]{1,0:T(8,128)(2,1)S(1)}, bf16[16,512]{1,0:T(8,128)(2,1)S(1)}, u32[]{:S(2)}, u32[]{:S(2)}) collective-permute-start(bf16[16,512]{1,0:T(8,128)(2,1)S(1)} %broadcast_select_fusion.2), channel_id=1, source_target_pairs={{0,2},{4,6},{8,10},{12,14},{16,18},{20,22},{24,26},{28,30},{1,3},{... | collective-permute-start | bytes 49160 | tf_op jit(solution)/shard_map/ppermute | solution.py:427
  24.1 8.5 %collective-permute-start = (bf16[512,256]{1,0:T(8,128)(2,1)}, bf16[512,256]{1,0:T(8,128)(2,1)S(1)}, u32[]{:S(2)}, u32[]{:S(2)}) collective-permute-start(bf16[512,256]{1,0:T(8,128)(2,1)} %get-tuple-element.11.refs_0_), channel_id=1, source_target_pairs={{0,8},{2,10},{4,12},{6,14},{8,16},{10,18},{12,20},{14,22},{16,24},... | collective-permute-start | bytes 786440 | tf_op jit(solution)/shard_map/ppermute | solution.py:427
  26.7 8.8 %collective-permute-start.22 = (bf16[512,256]{1,0:T(8,128)(2,1)}, bf16[512,256]{1,0:T(8,128)(2,1)S(1)}, u32[]{:S(2)}, u32[]{:S(2)}) collective-permute-start(bf16[512,256]{1,0:T(8,128)(2,1)} %get-tuple-element.13.refs_0_), channel_id=1, source_target_pairs={{0,4},{2,6},{8,12},{10,14},{16,20},{18,22},{24,28},{26,30},{1,5},{... | collective-permute-start | bytes 786440 | tf_op jit(solution)/shard_map/ppermute | solution.py:427
  28.0 30.9 %copy-start.3 = (bf16[512,256]{1,0:T(8,128)(2,1)}, bf16[512,256]{1,0:T(8,128)(2,1)S(1)}, u32[]{:S(2)}) copy-start(bf16[512,256]{1,0:T(8,128)(2,1)S(1)} %collective-permute-done.7.refs_7_) | copy-start | bytes 786436
  28.0 7.5 %collective-permute-start.17 = (bf16[512,256]{1,0:T(8,128)(2,1)}, bf16[512,256]{1,0:T(8,128)(2,1)S(1)}, u32[]{:S(2)}, u32[]{:S(2)}) collective-permute-start(bf16[512,256]{1,0:T(8,128)(2,1)} %get-tuple-element.13.refs_0_), channel_id=1, source_target_pairs={{0,2},{4,6},{8,10},{12,14},{16,18},{20,22},{24,26},{28,30},{1,3},{... | collective-permute-start | bytes 786440 | tf_op jit(solution)/shard_map/ppermute | solution.py:427
  29.4 29.6 %copy-start.4 = (bf16[512,256]{1,0:T(8,128)(2,1)}, bf16[512,256]{1,0:T(8,128)(2,1)S(1)}, u32[]{:S(2)}) copy-start(bf16[512,256]{1,0:T(8,128)(2,1)S(1)} %collective-permute-done.2.refs_3_) | copy-start | bytes 786436
  29.4 8.8 %collective-permute-start.15 = (bf16[512,256]{1,0:T(8,128)(2,1)}, bf16[512,256]{1,0:T(8,128)(2,1)S(1)}, u32[]{:S(2)}, u32[]{:S(2)}) collective-permute-start(bf16[512,256]{1,0:T(8,128)(2,1)} %get-tuple-element.13.refs_0_), channel_id=1, source_target_pairs={{0,8},{2,10},{4,12},{6,14},{8,16},{10,18},{12,20},{14,22},{16,24},... | collective-permute-start | bytes 786440 | tf_op jit(solution)/shard_map/ppermute | solution.py:427
  32.6 11.1 %copy-start.8 = (bf16[512,256]{1,0:T(8,128)(2,1)}, bf16[512,256]{1,0:T(8,128)(2,1)S(1)}, u32[]{:S(2)}) copy-start(bf16[512,256]{1,0:T(8,128)(2,1)S(1)} %collective-permute-done.refs_1_) | copy-start | bytes 786436
  32.6 5.7 %collective-permute-start.9 = (bf16[512,256]{1,0:T(8,128)(2,1)S(1)}, bf16[512,256]{1,0:T(8,128)(2,1)S(1)}, u32[]{:S(2)}, u32[]{:S(2)}) collective-permute-start(bf16[512,256]{1,0:T(8,128)(2,1)S(1)} %collective-permute-done.7.refs_7_), channel_id=1, source_target_pairs={{4,6},{6,4},{12,14},{14,12},{20,22},{22,20},{28,30},{30,28},{5,7},... | collective-permute-start | bytes 786440 | tf_op jit(solution)/shard_map/ppermute | solution.py:427
  35.6 23.4 %copy-start.5 = (bf16[512,256]{1,0:T(8,128)(2,1)}, bf16[512,256]{1,0:T(8,128)(2,1)S(1)}, u32[]{:S(2)}) copy-start(bf16[512,256]{1,0:T(8,128)(2,1)S(1)} %collective-permute-done.22.refs_7_) | copy-start | bytes 786436
  35.6 7.8 %collective-permute-start.5 = (bf16[512,256]{1,0:T(8,128)(2,1)S(1)}, bf16[512,256]{1,0:T(8,128)(2,1)}, u32[]{:S(2)}, u32[]{:S(2)}) collective-permute-start(bf16[512,256]{1,0:T(8,128)(2,1)S(1)} %collective-permute-done.refs_1_), channel_id=1, source_target_pairs={{0,4},{2,6},{4,0},{6,2},{8,12},{10,14},{12,8},{14,10},{16,20},{18,... | collective-permute-start | bytes 786440 | tf_op jit(solution)/shard_map/ppermute | solution.py:427
  35.6 23.4 %copy-start.6 = (bf16[512,256]{1,0:T(8,128)(2,1)}, bf16[512,256]{1,0:T(8,128)(2,1)S(1)}, u32[]{:S(2)}) copy-start(bf16[512,256]{1,0:T(8,128)(2,1)S(1)} %collective-permute-done.17.refs_3_) | copy-start | bytes 786436
  35.6 9.7 %collective-permute-start.3 = (bf16[512,256]{1,0:T(8,128)(2,1)S(1)}, bf16[512,256]{1,0:T(8,128)(2,1)}, u32[]{:S(2)}, u32[]{:S(2)}) collective-permute-start(bf16[512,256]{1,0:T(8,128)(2,1)S(1)} %collective-permute-done.refs_1_), channel_id=1, source_target_pairs={{0,8},{2,10},{4,12},{6,14},{8,16},{10,18},{12,20},{14,22},{16,24},... | collective-permute-start | bytes 786440 | tf_op jit(solution)/shard_map/ppermute | solution.py:427
  38.2 34.0 %copy-start.7 = (bf16[512,256]{1,0:T(8,128)(2,1)}, bf16[512,256]{1,0:T(8,128)(2,1)S(1)}, u32[]{:S(2)}) copy-start(bf16[512,256]{1,0:T(8,128)(2,1)S(1)} %collective-permute-done.15.refs_1_) | copy-start | bytes 786436
  38.2 9.7 %collective-permute-start.1 = (bf16[512,256]{1,0:T(8,128)(2,1)S(1)}, bf16[512,256]{1,0:T(8,128)(2,1)S(1)}, u32[]{:S(2)}, u32[]{:S(2)}) collective-permute-start(bf16[512,256]{1,0:T(8,128)(2,1)S(1)} %collective-permute-done.refs_1_), channel_id=1, source_target_pairs={{0,2},{2,0},{4,6},{6,4},{8,10},{10,8},{12,14},{14,12},{16,18},{18,... | collective-permute-start | bytes 786440 | tf_op jit(solution)/shard_map/ppermute | solution.py:427
  38.3 9.6 %copy-start.10 = (bf16[512,256]{1,0:T(8,128)(2,1)}, bf16[512,256]{1,0:T(8,128)(2,1)S(1)}, u32[]{:S(2)}) copy-start(bf16[512,256]{1,0:T(8,128)(2,1)S(1)} %collective-permute-done.9.refs_9_) | copy-start | bytes 786436
  38.3 20.6 %collective-permute-start.24 = (bf16[512,256]{1,0:T(8,128)(2,1)S(1)}, bf16[512,256]{1,0:T(8,128)(2,1)S(1)}, u32[]{:S(2)}, u32[]{:S(2)}) collective-permute-start(bf16[512,256]{1,0:T(8,128)(2,1)S(1)} %collective-permute-done.22.refs_7_), channel_id=1, source_target_pairs={{4,6},{6,4},{12,14},{14,12},{20,22},{22,20},{28,30},{30,28},{5,7},... | collective-permute-start | bytes 786440 | tf_op jit(solution)/shard_map/ppermute | solution.py:427
  43.4 16.9 %collective-permute-start.20 = (bf16[512,256]{1,0:T(8,128)(2,1)S(1)}, bf16[512,256]{1,0:T(8,128)(2,1)S(1)}, u32[]{:S(2)}, u32[]{:S(2)}) collective-permute-start(bf16[512,256]{1,0:T(8,128)(2,1)S(1)} %collective-permute-done.15.refs_1_), channel_id=1, source_target_pairs={{0,4},{2,6},{4,0},{6,2},{8,12},{10,14},{12,8},{14,10},{16,20},{18,... | collective-permute-start | bytes 786440 | tf_op jit(solution)/shard_map/ppermute | solution.py:427
  45.3 16.2 %collective-permute-start.18 = (bf16[512,256]{1,0:T(8,128)(2,1)S(1)}, bf16[512,256]{1,0:T(8,128)(2,1)}, u32[]{:S(2)}, u32[]{:S(2)}) collective-permute-start(bf16[512,256]{1,0:T(8,128)(2,1)S(1)} %collective-permute-done.15.refs_1_), channel_id=1, source_target_pairs={{0,8},{2,10},{4,12},{6,14},{8,16},{10,18},{12,20},{14,22},{16,24},... | collective-permute-start | bytes 786440 | tf_op jit(solution)/shard_map/ppermute | solution.py:427
  47.9 11.0 %copy-start.13 = (bf16[512,256]{1,0:T(8,128)(2,1)}, bf16[512,256]{1,0:T(8,128)(2,1)S(1)}, u32[]{:S(2)}) copy-start(bf16[512,256]{1,0:T(8,128)(2,1)S(1)} %collective-permute-done.1.refs_2_) | copy-start | bytes 786436
  48.0 14.9 %collective-permute-start.8 = (bf16[512,256]{1,0:T(8,128)(2,1)}, bf16[512,256]{1,0:T(8,128)(2,1)}, u32[]{:S(2)}, u32[]{:S(2)}) collective-permute-start(bf16[512,256]{1,0:T(8,128)(2,1)} %collective-permute-done.3.refs_11_), channel_id=1, source_target_pairs={{4,0},{6,2},{12,8},{14,10},{20,16},{22,18},{28,24},{30,26},{5,1},{... | collective-permute-start | bytes 786440 | tf_op jit(solution)/shard_map/ppermute | solution.py:427
  59.0 2.5 %copy-start.9 = (bf16[512,256]{1,0:T(8,128)(2,1)}, bf16[512,256]{1,0:T(8,128)(2,1)S(1)}, u32[]{:S(2)}) copy-start(bf16[512,256]{1,0:T(8,128)(2,1)S(1)} %collective-permute-done.24.refs_9_) | copy-start | bytes 786436
  59.0 13.3 %collective-permute-start.4 = (bf16[512,256]{1,0:T(8,128)(2,1)}, bf16[512,256]{1,0:T(8,128)(2,1)S(1)}, u32[]{:S(2)}, u32[]{:S(2)}) collective-permute-start(bf16[512,256]{1,0:T(8,128)(2,1)} %collective-permute-done.3.refs_11_), channel_id=1, source_target_pairs={{2,0},{6,4},{10,8},{14,12},{18,16},{22,20},{26,24},{30,28},{3,1},{... | collective-permute-start | bytes 786440 | tf_op jit(solution)/shard_map/ppermute | solution.py:427
  60.3 2.5 %copy-start.11 = (bf16[512,256]{1,0:T(8,128)(2,1)}, bf16[512,256]{1,0:T(8,128)(2,1)S(1)}, u32[]{:S(2)}) copy-start(bf16[512,256]{1,0:T(8,128)(2,1)S(1)} %collective-permute-done.20.refs_5_) | copy-start | bytes 786436
  60.3 11.9 %collective-permute-start.6 = (bf16[512,256]{1,0:T(8,128)(2,1)}, bf16[512,256]{1,0:T(8,128)(2,1)}, u32[]{:S(2)}, u32[]{:S(2)}) collective-permute-start(bf16[512,256]{1,0:T(8,128)(2,1)} %collective-permute-done.5.refs_5_), channel_id=1, source_target_pairs={{0,2},{2,0},{4,6},{6,4},{8,10},{10,8},{12,14},{14,12},{16,18},{18,... | collective-permute-start | bytes 786440 | tf_op jit(solution)/shard_map/ppermute | solution.py:427
  61.5 12.1 %collective-permute-start.23 = (bf16[512,256]{1,0:T(8,128)(2,1)}, bf16[512,256]{1,0:T(8,128)(2,1)S(1)}, u32[]{:S(2)}, u32[]{:S(2)}) collective-permute-start(bf16[512,256]{1,0:T(8,128)(2,1)} %collective-permute-done.18.refs_11_), channel_id=1, source_target_pairs={{4,0},{6,2},{12,8},{14,10},{20,16},{22,18},{28,24},{30,26},{5,1},{... | collective-permute-start | bytes 786440 | tf_op jit(solution)/shard_map/ppermute | solution.py:427
  62.8 10.8 %copy-start.12 = (bf16[512,256]{1,0:T(8,128)(2,1)S(1)}, bf16[512,256]{1,0:T(8,128)(2,1)}, u32[]{:S(2)}) copy-start(bf16[512,256]{1,0:T(8,128)(2,1)} %copy-done.11) | copy-start | bytes 786436
  62.8 12.6 %collective-permute-start.10 = (bf16[512,256]{1,0:T(8,128)(2,1)}, bf16[512,256]{1,0:T(8,128)(2,1)}, u32[]{:S(2)}, u32[]{:S(2)}) collective-permute-start(bf16[512,256]{1,0:T(8,128)(2,1)} %collective-permute-done.8.refs_8_), channel_id=1, source_target_pairs={{0,2},{2,0},{8,10},{10,8},{16,18},{18,16},{24,26},{26,24},{1,3},{3... | collective-permute-start | bytes 786440 | tf_op jit(solution)/shard_map/ppermute | solution.py:427
  72.2 21.2 %collective-permute-start.16 = (bf16[512,256]{1,0:T(8,128)(2,1)S(1)}, bf16[512,256]{1,0:T(8,128)(2,1)}, u32[]{:S(2)}, u32[]{:S(2)}) collective-permute-start(bf16[512,256]{1,0:T(8,128)(2,1)S(1)} %collective-permute-done.15.refs_1_), channel_id=1, source_target_pairs={{0,2},{2,0},{4,6},{6,4},{8,10},{10,8},{12,14},{14,12},{16,18},{18,... | collective-permute-start | bytes 786440 | tf_op jit(solution)/shard_map/ppermute | solution.py:427
  72.3 4.5 %copy-start.15 = (bf16[512,256]{1,0:T(8,128)(2,1)}, bf16[512,256]{1,0:T(8,128)(2,1)S(1)}, u32[]{:S(2)}) copy-start(bf16[512,256]{1,0:T(8,128)(2,1)S(1)} %collective-permute-done.4.refs_4_) | copy-start | bytes 786436
  72.3 21.3 %collective-permute-start.19 = (bf16[512,256]{1,0:T(8,128)(2,1)}, bf16[512,256]{1,0:T(8,128)(2,1)}, u32[]{:S(2)}, u32[]{:S(2)}) collective-permute-start(bf16[512,256]{1,0:T(8,128)(2,1)} %collective-permute-done.18.refs_11_), channel_id=1, source_target_pairs={{2,0},{6,4},{10,8},{14,12},{18,16},{22,20},{26,24},{30,28},{3,1},{... | collective-permute-start | bytes 786440 | tf_op jit(solution)/shard_map/ppermute | solution.py:427
  73.6 19.8 %copy-start.14 = (bf16[512,256]{1,0:T(8,128)(2,1)}, bf16[512,256]{1,0:T(8,128)(2,1)S(1)}, u32[]{:S(2)}) copy-start(bf16[512,256]{1,0:T(8,128)(2,1)S(1)} %collective-permute-done.23.refs_8_) | copy-start | bytes 786436
  73.6 19.9 %collective-permute-start.21 = (bf16[512,256]{1,0:T(8,128)(2,1)S(1)}, bf16[512,256]{1,0:T(8,128)(2,1)}, u32[]{:S(2)}, u32[]{:S(2)}) collective-permute-start(bf16[512,256]{1,0:T(8,128)(2,1)S(1)} %copy-done.12), channel_id=1, source_target_pairs={{0,2},{2,0},{4,6},{6,4},{8,10},{10,8},{12,14},{14,12},{16,18},{18,... | collective-permute-start | bytes 786440 | tf_op jit(solution)/shard_map/ppermute | solution.py:427
  75.4 18.1 %collective-permute-start.25 = (bf16[512,256]{1,0:T(8,128)(2,1)S(1)}, bf16[512,256]{1,0:T(8,128)(2,1)}, u32[]{:S(2)}, u32[]{:S(2)}) collective-permute-start(bf16[512,256]{1,0:T(8,128)(2,1)S(1)} %collective-permute-done.23.refs_8_), channel_id=1, source_target_pairs={{0,2},{2,0},{8,10},{10,8},{16,18},{18,16},{24,26},{26,24},{1,3},{3... | collective-permute-start | bytes 786440 | tf_op jit(solution)/shard_map/ppermute | solution.py:427
  76.8 49.0 %collective-permute-start.29 = (bf16[1024,1024]{1,0:T(8,128)(2,1)S(1)}, bf16[1024,1024]{1,0:T(8,128)(2,1)}, u32[]{:S(2)}, u32[]{:S(2)}) collective-permute-start(bf16[1024,1024]{1,0:T(8,128)(2,1)S(1)} %collective-permute-done.28.wa_ref), channel_id=1, source_target_pairs={{0,2},{2,0},{4,6},{6,4},{8,10},{10,8},{12,14},{14,12},{16,18},{18,... | collective-permute-start | bytes 6291464 | tf_op jit(solution)/shard_map/ppermute | solution.py:427
  93.4 19.9 %copy-start.1 = (bf16[512,512]{1,0:T(8,128)(2,1)S(1)}, bf16[512,512]{1,0:T(8,128)(2,1)}, u32[]{:S(2)}) copy-start(bf16[512,512]{1,0:T(8,128)(2,1)} %attend.2.own0) | copy-start | bytes 1572868
  93.5 28.7 %collective-permute-start.26 = (bf16[512,512]{1,0:T(8,128)(2,1)}, bf16[512,512]{1,0:T(8,128)(2,1)S(1)}, u32[]{:S(2)}, u32[]{:S(2)}) collective-permute-start(bf16[512,512]{1,0:T(8,128)(2,1)} %attend.2.own0), channel_id=1, source_target_pairs={{0,1},{1,0},{2,3},{3,2},{4,5},{5,4},{6,7},{7,6},{8,9},{9,8},{10,11... | collective-permute-start | bytes 1572872 | tf_op jit(solution)/shard_map/ppermute | solution.py:427
  108.7 17.1 %collective-permute-start.27 = (bf16[512,512]{1,0:T(8,128)(2,1)}, bf16[512,512]{1,0:T(8,128)(2,1)S(1)}, u32[]{:S(2)}, u32[]{:S(2)}) collective-permute-start(bf16[512,512]{1,0:T(8,128)(2,1)} %attend.3.own1), channel_id=1, source_target_pairs={{0,1},{1,0},{2,3},{3,2},{4,5},{5,4},{6,7},{7,6},{8,9},{9,8},{10,11... | collective-permute-start | bytes 1572872 | tf_op jit(solution)/shard_map/ppermute | solution.py:427
  113.4 2.2 %copy-start = (bf16[512,4096]{1,0:T(8,128)(2,1)S(1)}, bf16[512,4096]{1,0:T(8,128)(2,1)}, u32[]{:S(2)}) copy-start(bf16[512,4096]{1,0:T(8,128)(2,1)} %tok_ref.7) | copy-start | bytes 12582916
  115.5 1.0 copy-start.2

commit v3 on v2

--- a/solution.py
+++ b/solution.py
@@ -208,6 +208,8 @@
         copy.wait()
 
     def queries_of(head):
+        if isinstance(head, int):
+            return q_ref[:, head * HEAD_DIM : (head + 1) * HEAD_DIM]
         return q_ref[:, pl.ds(pl.multiple_of(head * HEAD_DIM, HEAD_DIM), HEAD_DIM)]
 
     def scores_of(head, keys):
@@ -263,30 +265,41 @@
     lax.fori_loop(0, rest, single, 0)
     turns(whole_items, rest, whole // UNROLL, False)
 
-    def finish(head, carry):
-        reach = window[group * heads + head]
-
-        @pl.when(query_start + rows - 1 - reach >= 0)
-        def _():
-            base = group * PAIR
-            pad = jnp.zeros((HEAD_DIM - SINK_ROWS, HEAD_DIM), jnp.bfloat16)
-            keys = jnp.concatenate([sink_ref[:, base : base + HEAD_DIM], pad], axis=0)
-            values = jnp.concatenate([sink_ref[:, base + HEAD_DIM : base + PAIR], pad], axis=0)
-            vaug = jnp.concatenate([values, jnp.ones((HEAD_DIM, HEAD_DIM), jnp.bfloat16)], axis=1)
-            column = lax.broadcasted_iota(jnp.int32, (rows, HEAD_DIM), 1)
-            latest = lax.broadcasted_iota(jnp.int32, (rows, HEAD_DIM), 0) + (query_start - reach)
+    def finish(head):
+        out_ref[:, head * HEAD_DIM : (head + 1) * HEAD_DIM] = (
+            acc_ref[head, :, :HEAD_DIM] / acc_ref[head, :, HEAD_DIM:]
+        ).astype(jnp.bfloat16)
+
+    shortest = window[group * heads]
+    for head in range(1, heads):
+        shortest = jnp.minimum(shortest, window[group * heads + head])
+    any_open = query_start + rows - 1 - shortest >= 0
+
+    @pl.when(any_open)
+    def _():
+        base = group * PAIR
+        pad = jnp.zeros((HEAD_DIM - SINK_ROWS, HEAD_DIM), jnp.bfloat16)
+        keys = jnp.concatenate([sink_ref[:, base : base + HEAD_DIM], pad], axis=0)
+        values = jnp.concatenate([sink_ref[:, base + HEAD_DIM : base + PAIR], pad], axis=0)
+        vaug = jnp.concatenate([values, jnp.ones((HEAD_DIM, HEAD_DIM), jnp.bfloat16)], axis=1)
+        column = lax.broadcasted_iota(jnp.int32, (rows, HEAD_DIM), 1)
+        row = lax.broadcasted_iota(jnp.int32, (rows, HEAD_DIM), 0)
+        scored = []
+        for head in range(heads):
+            latest = row + (query_start - window[group * heads + head])
             count = jnp.minimum(sinks[group * heads + head], SINK)
             allowed = (column < count) & (column <= latest)
             scores = scores_of(head, keys) + bias[group * heads + head] * LOG2E
-            scores = jnp.where(allowed, scores, LOW)
-            fold(head, scores, scores, vaug)
-
-        out_ref[:, pl.ds(pl.multiple_of(head * HEAD_DIM, HEAD_DIM), HEAD_DIM)] = (
-            acc_ref[head, :, :HEAD_DIM] / acc_ref[head, :, HEAD_DIM:]
-        ).astype(jnp.bfloat16)
-        return carry
-
-    lax.fori_loop(0, heads, finish, 0)
+            scored.append(jnp.where(allowed, scores, LOW))
+        for head in range(heads):
+            fold(head, scored[head], scored[head], vaug)
+        for head in range(heads):
+            finish(head)
+
+    @pl.when(jnp.logical_not(any_open))
+    def _():
+        for head in range(heads):
+            finish(head)
 
 
 def attend(group, meta, window, sink_count, sink_bias, queries, blocks, sink_rows):
@@ -426,15 +439,9 @@
     def send(x, pairs, axis="seq"):
         return lax.ppermute(x, axis, pairs)
 
-    ahead = [(i, i + QUAD) for i in range(peers - QUAD)]
+    ahead = [(i, (i + QUAD) % peers) for i in everyone]
     core_swap = [(i, i ^ 1) for i in everyone]
-    core_up = [(i, i + 1) for i in everyone if i % 2 == 0]
-    core_down = [(i, i - 1) for i in everyone if i % 2 == 1]
     side_swap = [(i, i ^ 2) for i in everyone]
-    side_up = [(i, i + 2) for i in everyone if (i // 2) % 2 == 0]
-    side_down = [(i, i - 2) for i in everyone if (i // 2) % 2 == 1]
-    cross_up = [(i, i ^ 1) for i in everyone if (i // 2) % 2 == 1]
-    cross_down = [(i, i ^ 1) for i in everyone if (i // 2) % 2 == 0]
     head_swap = [(i, i ^ 1) for i in range(head_peers)]
 
     twin, across, mirror = me ^ 1, me ^ 2, me ^ 3
@@ -442,14 +449,14 @@
         me,
         me - 4,
         twin - 4,
-        jnp.where(core == 1, me - 1, -1),
-        jnp.where(core == 0, me - 7, -1),
+        jnp.where(core == 1, twin, -1),
+        jnp.where(core == 0, twin - 8, -1),
         across - 4,
         mirror - 4,
-        jnp.where(side == 1, me - 2, -1),
-        jnp.where(side == 0, me - 6, -1),
-        jnp.where(side == 1, twin - 2, -1),
-        jnp.where(side == 0, twin - 6, -1),
+        jnp.where(side == 1, across, -1),
+        jnp.where(side == 0, across - 8, -1),
+        jnp.where(side == 1, mirror, -1),
+        jnp.where(side == 0, mirror - 8, -1),
         me - 8,
     ]
     meta = jnp.stack([me] + index).astype(jnp.int32)
@@ -458,13 +465,13 @@
     *kv, sink_rows, scale, w_send = keys_values(place, tokens, gain, w_key, w_value, w_out, piece)
 
     back4 = [send(x, ahead) for x in kv]
-    near_side = [send(x, side_up) for x in kv]
-    near_core = [send(x, core_up) for x in kv]
+    near_side = [send(x, side_swap) for x in kv]
+    near_core = [send(x, core_swap) for x in kv]
     w_near = send(w_send, head_swap, "head")
 
     def spread(rows, have):
         step = have // 2
-        arrived = send(rows, [(i, i + step) for i in range(0, peers, have)])
+        arrived = send(rows, [(i, (i + step) % peers) for i in everyone])
         return jnp.where(me % have == step, arrived, rows), step
 
     have = peers
@@ -474,20 +481,20 @@
         b4, ns = back4[g], near_side[g]
         b8 = send(b4, ahead)
         across4 = send(b4, side_swap)
-        far_side = send(b8, side_down)
+        far_side = send(b8, side_swap)
         blocks.append(
             [
                 kv[g],
                 b4,
                 send(b4, core_swap),
                 near_core[g],
-                send(b8, core_down),
+                send(b8, core_swap),
                 across4,
                 send(across4, core_swap),
                 ns,
                 far_side,
-                send(ns, cross_up),
-                send(far_side, cross_down),
+                send(ns, core_swap),
+                send(far_side, core_swap),
                 b8,
             ]
         )

time: 133 us -> 122 us (0.917)
  starting transfers between devices: 44 us -> 26.4 us
  waiting for transfers between devices: 18.7 us -> 26.6 us
  Pallas kernels: 63.6 us -> 61.4 us
    ppermute x30, starting transfers between devices: 44 us -> 26.4 us  [send(): return lax.ppermute(x, axis, pairs)]
    ppermute x30, waiting for transfers between devices: 18.7 us -> 26.6 us  [send(): return lax.ppermute(x, axis, pairs)]
    pallas_call x2, Pallas kernels: 31.7 us -> 29.5 us  [attend(): pl.pallas_call(functools.partial(attend_kernel, group, slots), grid=(1,),...]
  transfers between devices with their start and end apart: 30 -> 30, of which waited for: 6 -> 9; matrix products, arithmetic and copies ran while one was open for 2% -> 2% of each run, Pallas kernels for 38% -> 40%
where the time goes in v3:
time: 122 us; the launch traced here: 120 us
  Pallas kernels  61.4 us (50%)
  waiting for transfers between devices  26.6 us (22%)
  starting transfers between devices  26.4 us (22%)
  local copies, waits for them, and re-layouts  4.03 us (3%)
  other arithmetic  1.41 us (1%)
    pallas_call x2, Pallas kernels, attend(): pl.pallas_call(functools.partial(attend_kernel, group, slots), grid=(1,),...  29.5 us
    ppermute x30, waiting for transfers between devices, send(): return lax.ppermute(x, axis, pairs)  26.6 us
    ppermute x30, starting transfers between devices, send(): return lax.ppermute(x, axis, pairs)  26.4 us
    pallas_call x2, Pallas kernels, query_group(): pl.pallas_call(query_kernel, grid=(width // chunk,), in_specs=[pl.BlockSp...  13.3 us
    pallas_call x1, Pallas kernels, keys_values(): pl.pallas_call(keys_values_kernel, grid_spec=pltpu.PrefetchScalarGridSpec...  6.62 us
    pallas_call x1, Pallas kernels, project_last(): pl.pallas_call(project_last_kernel, grid_spec=pltpu.PrefetchScalarGridSpe...  6.41 us
    pallas_call x1, Pallas kernels, project(): pl.pallas_call(project_kernel, grid_spec=pltpu.PrefetchScalarGridSpec(num...  5.58 us
    unnamed x32, local copies, waits for them, and re-layouts  3.41 us
  transfers between devices with their start and end apart: 30, of which 9 were waited for; matrix products, arithmetic and copies ran while one was open for 2% of the time, Pallas kernels for 40%

profile of v3, /device:TPU:18, one launch (start us, length us, event | category | flops | bytes accessed | tf_op | source)
XLA Modules:
  0.0 120.0 jit_solution(5392474789210016557)
XLA Ops:
  0.0 6.6 %keys_values.1 = (bf16[512,256]{1,0:T(8,128)(2,1)}, bf16[512,256]{1,0:T(8,128)(2,1)}, bf16[16,512]{1,0:T(8,128)(2,1)}, f32[512,128]{1,0:T(8,128)}, bf16[1024,1024]{1,0:T(8,128)(2,1)}) custom-call(s32[1]{0:T(128)} %bitcast.15.place, bf16[512,4096]{1,0:T(8,128)(2,1)} %tok_ref.7, f32[1,4096]{1,0:T(1,128)} %bitcast.16, bf16[4096,256]{1,0:T(8,128)(2,1)} %wk_ref.1, ...), custom_call_target="tpu_custom_call" | custom-call | flops 2147483648 | bytes 8388608 | tf_op jit(solution)/shard_map/keys_values/pallas_call | solution.py:77
  6.6 1.6 %collective-permute-start.28 = (bf16[1024,1024]{1,0:T(8,128)(2,1)}, bf16[1024,1024]{1,0:T(8,128)(2,1)S(1)}, u32[]{:S(2)}, u32[]{:S(2)}) collective-permute-start(bf16[1024,1024]{1,0:T(8,128)(2,1)} %get-tuple-element.14), channel_id=1, source_target_pairs={{0,1},{1,0},{2,3},{3,2},{4,5},{5,4},{6,7},{7,6},{8,9},{9,8},{10,11... | collective-permute-start | bytes 6291464 | tf_op jit(solution)/shard_map/ppermute | solution.py:440
  8.2 0.3 collective-permute-start.11
  8.6 4.5 %collective-permute-done.11 = bf16[16,512]{1,0:T(8,128)(2,1)S(1)} collective-permute-done((bf16[16,512]{1,0:T(8,128)(2,1)}, bf16[16,512]{1,0:T(8,128)(2,1)S(1)}, u32[]{:S(2)}, u32[]{:S(2)}) %collective-permute-start.11) | collective-permute-done | bytes 16416 | tf_op jit(solution)/shard_map/ppermute | solution.py:440
  13.1 0.7 broadcast_select_fusion
  13.8 1.6 %collective-permute-start.12 = (bf16[16,512]{1,0:T(8,128)(2,1)S(1)}, bf16[16,512]{1,0:T(8,128)(2,1)S(1)}, u32[]{:S(2)}, u32[]{:S(2)}) collective-permute-start(bf16[16,512]{1,0:T(8,128)(2,1)S(1)} %broadcast_select_fusion), channel_id=1, source_target_pairs={{0,8},{2,10},{4,12},{6,14},{8,16},{10,18},{12,20},{14,22},{16,24},... | collective-permute-start | bytes 49160 | tf_op jit(solution)/shard_map/ppermute | solution.py:440
  15.4 0.5 collective-permute-start.7
  16.0 1.6 %collective-permute-done.12 = bf16[16,512]{1,0:T(8,128)(2,1)S(1)} collective-permute-done((bf16[16,512]{1,0:T(8,128)(2,1)S(1)}, bf16[16,512]{1,0:T(8,128)(2,1)S(1)}, u32[]{:S(2)}, u32[]{:S(2)}) %collective-permute-start.12) | collective-permute-done | bytes 16416 | tf_op jit(solution)/shard_map/ppermute | solution.py:440
  17.5 1.6 %collective-permute-start.13 = (bf16[16,512]{1,0:T(8,128)(2,1)S(1)}, bf16[16,512]{1,0:T(8,128)(2,1)S(1)}, u32[]{:S(2)}, u32[]{:S(2)}) collective-permute-start(bf16[16,512]{1,0:T(8,128)(2,1)S(1)} %broadcast_select_fusion.1), channel_id=1, source_target_pairs={{0,4},{2,6},{4,8},{6,10},{8,12},{10,14},{12,16},{14,18},{16,20},{1... | collective-permute-start | bytes 49160 | tf_op jit(solution)/shard_map/ppermute | solution.py:440
  19.1 3.2 %collective-permute-done.13 = bf16[16,512]{1,0:T(8,128)(2,1)S(1)} collective-permute-done((bf16[16,512]{1,0:T(8,128)(2,1)S(1)}, bf16[16,512]{1,0:T(8,128)(2,1)S(1)}, u32[]{:S(2)}, u32[]{:S(2)}) %collective-permute-start.13) | collective-permute-done | bytes 16416 | tf_op jit(solution)/shard_map/ppermute | solution.py:440
  22.3 0.6 collective-permute-start
  23.0 2.5 %collective-permute-done.14 = bf16[16,512]{1,0:T(8,128)(2,1)S(1)} collective-permute-done((bf16[16,512]{1,0:T(8,128)(2,1)S(1)}, bf16[16,512]{1,0:T(8,128)(2,1)S(1)}, u32[]{:S(2)}, u32[]{:S(2)}) %collective-permute-start.14) | collective-permute-done | bytes 16416 | tf_op jit(solution)/shard_map/ppermute | solution.py:440
  25.5 0.7 collective-permute-start.22
  26.2 1.2 %collective-permute-start.17 = (bf16[512,256]{1,0:T(8,128)(2,1)}, bf16[512,256]{1,0:T(8,128)(2,1)S(1)}, u32[]{:S(2)}, u32[]{:S(2)}) collective-permute-start(bf16[512,256]{1,0:T(8,128)(2,1)} %get-tuple-element.13.refs_0_), channel_id=1, source_target_pairs={{0,2},{2,0},{4,6},{6,4},{8,10},{10,8},{12,14},{14,12},{16,18},{18,... | collective-permute-start | bytes 786440 | tf_op jit(solution)/shard_map/ppermute | solution.py:440
  27.5 1.2 collective-permute-start.15
  28.7 2.6 %collective-permute-done.refs_1_ = bf16[512,256]{1,0:T(8,128)(2,1)S(1)} collective-permute-done((bf16[512,256]{1,0:T(8,128)(2,1)}, bf16[512,256]{1,0:T(8,128)(2,1)S(1)}, u32[]{:S(2)}, u32[]{:S(2)}) %collective-permute-start) | collective-permute-done | bytes 262176 | tf_op jit(solution)/shard_map/ppermute | solution.py:440
  31.2 1.2 collective-permute-start.9
  32.4 1.5 %collective-permute-done.22.refs_7_ = bf16[512,256]{1,0:T(8,128)(2,1)S(1)} collective-permute-done((bf16[512,256]{1,0:T(8,128)(2,1)}, bf16[512,256]{1,0:T(8,128)(2,1)S(1)}, u32[]{:S(2)}, u32[]{:S(2)}) %collective-permute-start.22) | collective-permute-done | bytes 262176 | tf_op jit(solution)/shard_map/ppermute | solution.py:440
  34.0 1.2 collective-permute-start.5
  35.2 2.1 %collective-permute-start.3 = (bf16[512,256]{1,0:T(8,128)(2,1)S(1)}, bf16[512,256]{1,0:T(8,128)(2,1)}, u32[]{:S(2)}, u32[]{:S(2)}) collective-permute-start(bf16[512,256]{1,0:T(8,128)(2,1)S(1)} %collective-permute-done.refs_1_), channel_id=1, source_target_pairs={{0,8},{2,10},{4,12},{6,14},{8,16},{10,18},{12,20},{14,22},{16,24},... | collective-permute-start | bytes 786440 | tf_op jit(solution)/shard_map/ppermute | solution.py:440
  37.3 0.3 collective-permute-start.1
  37.5 0.2 collective-permute-start.24
  37.8 5.4 %collective-permute-done.5.refs_5_ = bf16[512,256]{1,0:T(8,128)(2,1)} collective-permute-done((bf16[512,256]{1,0:T(8,128)(2,1)S(1)}, bf16[512,256]{1,0:T(8,128)(2,1)}, u32[]{:S(2)}, u32[]{:S(2)}) %collective-permute-start.5) | collective-permute-done | bytes 262176 | tf_op jit(solution)/shard_map/ppermute | solution.py:440
  43.2 0.9 collective-permute-start.20
  44.1 2.2 %collective-permute-start.18 = (bf16[512,256]{1,0:T(8,128)(2,1)S(1)}, bf16[512,256]{1,0:T(8,128)(2,1)}, u32[]{:S(2)}, u32[]{:S(2)}) collective-permute-start(bf16[512,256]{1,0:T(8,128)(2,1)S(1)} %collective-permute-done.15.refs_1_), channel_id=1, source_target_pairs={{0,8},{2,10},{4,12},{6,14},{8,16},{10,18},{12,20},{14,22},{16,24},... | collective-permute-start | bytes 786440 | tf_op jit(solution)/shard_map/ppermute | solution.py:440
  46.2 0.3 collective-permute-start.8
  46.5 6.6 %query_group.3.q_ref = bf16[512,512]{1,0:T(8,128)(2,1)} custom-call(bf16[512,4096]{1,0:T(8,128)(2,1)} %tok_ref.7, f32[1,4096]{1,0:T(1,128)} %bitcast.17, bf16[4096,1024]{1,0:T(8,128)(2,1)} %w_ref.4, f32[512,128]{1,0:T(8,128)} %get-tuple-element.10.scale_ref), custom_call_target="tpu_custom_call" | custom-call | flops 2147483648 | bytes 8388608 | tf_op jit(solution)/shard_map/query_group/pallas_call | solution.py:138
  53.3 0.5 collective-permute-start.6
  53.8 0.1 copy-done.9
  53.9 1.8 %collective-permute-start.23 = (bf16[512,256]{1,0:T(8,128)(2,1)}, bf16[512,256]{1,0:T(8,128)(2,1)S(1)}, u32[]{:S(2)}, u32[]{:S(2)}) collective-permute-start(bf16[512,256]{1,0:T(8,128)(2,1)} %collective-permute-done.18.refs_11_), channel_id=1, source_target_pairs={{0,4},{2,6},{4,0},{6,2},{8,12},{10,14},{12,8},{14,10},{16,20},{18,... | collective-permute-start | bytes 786440 | tf_op jit(solution)/shard_map/ppermute | solution.py:440
  55.7 2.0 %collective-permute-done.8.refs_8_ = bf16[512,256]{1,0:T(8,128)(2,1)} collective-permute-done((bf16[512,256]{1,0:T(8,128)(2,1)}, bf16[512,256]{1,0:T(8,128)(2,1)}, u32[]{:S(2)}, u32[]{:S(2)}) %collective-permute-start.8) | collective-permute-done | bytes 262176 | tf_op jit(solution)/shard_map/ppermute | solution.py:440
  57.8 6.7 %query_group.2.q_ref = bf16[512,512]{1,0:T(8,128)(2,1)} custom-call(bf16[512,4096]{1,0:T(8,128)(2,1)} %tok_ref.7, f32[1,4096]{1,0:T(1,128)} %bitcast.18, bf16[4096,1024]{1,0:T(8,128)(2,1)} %w_ref.4, f32[512,128]{1,0:T(8,128)} %get-tuple-element.10.scale_ref), custom_call_target="tpu_custom_call" | custom-call | flops 2147483648 | bytes 8388608 | tf_op jit(solution)/shard_map/query_group/pallas_call | solution.py:138
  64.5 0.6 stack.64.meta
  65.1 0.6 broadcast_select_fusion.3.refs_12_
  65.7 0.5 collective-permute-start.16
  66.2 0.1 collective-permute-start.19
  66.3 0.5 collective-permute-start.21
  66.7 0.1 collective-permute-start.25
  66.8 0.4 collective-permute-start.29
  67.3 15.5 %attend.2.own0 = bf16[512,512]{1,0:T(8,128)(2,1)} custom-call(s32[13]{0:T(128)} %stack.64.meta, s32[8]{0:T(128)} %window.3, s32[8]{0:T(128)} %sinks.3, f32[8]{0:T(128)} %bias.3, bf16[512,512]{1,0:T(8,128)(2,1)} %query_group.2.q_ref, bf16[512,256]{1,0:T(8,128)(2,1)} %get-tuple-element.11.refs_0_, bf16[512,256]{1,0:T(8,128)(2,1)} %copy-done.8, ...), custom_call_target="tpu_custom_call" | custom-call | flops 9663676416 | bytes 3145728 | tf_op jit(solution)/shard_map/attend/pallas_call | solution.py:312
  82.9 14.0 %attend.3.own1 = bf16[512,512]{1,0:T(8,128)(2,1)} custom-call(s32[13]{0:T(128)} %stack.64.meta, s32[8]{0:T(128)} %window.3, s32[8]{0:T(128)} %sinks.3, f32[8]{0:T(128)} %bias.3, bf16[512,512]{1,0:T(8,128)(2,1)} %query_group.3.q_ref, bf16[512,256]{1,0:T(8,128)(2,1)} %get-tuple-element.13.refs_0_, bf16[512,256]{1,0:T(8,128)(2,1)} %copy-done.7, ...), custom_call_target="tpu_custom_call" | custom-call | flops 9663676416 | bytes 3145728 | tf_op jit(solution)/shard_map/attend/pallas_call | solution.py:312
  96.9 4.6 %collective-permute-start.27 = (bf16[512,512]{1,0:T(8,128)(2,1)}, bf16[512,512]{1,0:T(8,128)(2,1)S(1)}, u32[]{:S(2)}, u32[]{:S(2)}) collective-permute-start(bf16[512,512]{1,0:T(8,128)(2,1)} %attend.3.own1), channel_id=1, source_target_pairs={{0,1},{1,0},{2,3},{3,2},{4,5},{5,4},{6,7},{7,6},{8,9},{9,8},{10,11... | collective-permute-start | bytes 1572872 | tf_op jit(solution)/shard_map/ppermute | solution.py:440
  101.5 0.1 pad_add_fusion.where
  101.6 2.2 %copy-done = bf16[512,4096]{1,0:T(8,128)(2,1)S(1)} copy-done((bf16[512,4096]{1,0:T(8,128)(2,1)S(1)}, bf16[512,4096]{1,0:T(8,128)(2,1)}, u32[]{:S(2)}) %copy-start) | copy-done | bytes 4194328
  103.8 1.0 copy-done.2
  104.8 5.6 %project.1.part_ref = f32[512,2048]{1,0:T(8,128)S(1)} custom-call(s32[2]{0:T(128)S(1)} %pad_add_fusion.where, bf16[512,4096]{1,0:T(8,128)(2,1)S(1)} %copy-done, bf16[512,512]{1,0:T(8,128)(2,1)S(1)} %copy-done.1, bf16[512,512]{1,0:T(8,128)(2,1)S(1)} %copy-done.2, bf16[1024,4096]{1,0:T(8,128)(2,1)} %w_ref.5), custom_call_target="tpu_custom_call" | custom-call | flops 2147483648 | bytes 10485760 | tf_op jit(solution)/shard_map/project/pallas_call | solution.py:375
  110.4 3.2 %collective-permute-done.27.far1 = bf16[512,512]{1,0:T(8,128)(2,1)S(1)} collective-permute-done((bf16[512,512]{1,0:T(8,128)(2,1)}, bf16[512,512]{1,0:T(8,128)(2,1)S(1)}, u32[]{:S(2)}, u32[]{:S(2)}) %collective-permute-start.27) | collective-permute-done | bytes 524320 | tf_op jit(solution)/shard_map/ppermute | solution.py:440
  113.6 6.4 %project_last.1 = bf16[512,2048]{1,0:T(8,128)(2,1)} custom-call(s32[2]{0:T(128)S(1)} %pad_add_fusion.where, f32[512,2048]{1,0:T(8,128)S(1)} %project.1.part_ref, bf16[512,512]{1,0:T(8,128)(2,1)S(1)} %collective-permute-done.26.far0, bf16[512,512]{1,0:T(8,128)(2,1)S(1)} %collective-permute-done.27.far1, ...), custom_call_target="tpu_custom_call" | custom-call | flops 2147483648 | bytes 10485760 | tf_op jit(solution)/shard_map/project_last/pallas_call | solution.py:404
  (57 shorter events, 0.3 us)
Async XLA Ops:
  6.6 60.2 %collective-permute-start.28 = (bf16[1024,1024]{1,0:T(8,128)(2,1)}, bf16[1024,1024]{1,0:T(8,128)(2,1)S(1)}, u32[]{:S(2)}, u32[]{:S(2)}) collective-permute-start(bf16[1024,1024]{1,0:T(8,128)(2,1)} %get-tuple-element.14), channel_id=1, source_target_pairs={{0,1},{1,0},{2,3},{3,2},{4,5},{5,4},{6,7},{7,6},{8,9},{9,8},{10,11... | collective-permute-start | bytes 6291464 | tf_op jit(solution)/shard_map/ppermute | solution.py:440
  8.2 4.9 %collective-permute-start.11 = (bf16[16,512]{1,0:T(8,128)(2,1)}, bf16[16,512]{1,0:T(8,128)(2,1)S(1)}, u32[]{:S(2)}, u32[]{:S(2)}) collective-permute-start(bf16[16,512]{1,0:T(8,128)(2,1)} %get-tuple-element.12), channel_id=1, source_target_pairs={{0,16},{2,18},{4,20},{6,22},{8,24},{10,26},{12,28},{14,30},{16,0},... | collective-permute-start | bytes 49160 | tf_op jit(solution)/shard_map/ppermute | solution.py:440
  13.8 3.7 %collective-permute-start.12 = (bf16[16,512]{1,0:T(8,128)(2,1)S(1)}, bf16[16,512]{1,0:T(8,128)(2,1)S(1)}, u32[]{:S(2)}, u32[]{:S(2)}) collective-permute-start(bf16[16,512]{1,0:T(8,128)(2,1)S(1)} %broadcast_select_fusion), channel_id=1, source_target_pairs={{0,8},{2,10},{4,12},{6,14},{8,16},{10,18},{12,20},{14,22},{16,24},... | collective-permute-start | bytes 49160 | tf_op jit(solution)/shard_map/ppermute | solution.py:440
  15.4 10.8 %collective-permute-start.7 = (bf16[512,256]{1,0:T(8,128)(2,1)}, bf16[512,256]{1,0:T(8,128)(2,1)S(1)}, u32[]{:S(2)}, u32[]{:S(2)}) collective-permute-start(bf16[512,256]{1,0:T(8,128)(2,1)} %get-tuple-element.11.refs_0_), channel_id=1, source_target_pairs={{0,4},{2,6},{4,0},{6,2},{8,12},{10,14},{12,8},{14,10},{16,20},{18,... | collective-permute-start | bytes 786440 | tf_op jit(solution)/shard_map/ppermute | solution.py:440
  16.0 11.5 %collective-permute-start.2 = (bf16[512,256]{1,0:T(8,128)(2,1)}, bf16[512,256]{1,0:T(8,128)(2,1)S(1)}, u32[]{:S(2)}, u32[]{:S(2)}) collective-permute-start(bf16[512,256]{1,0:T(8,128)(2,1)} %get-tuple-element.11.refs_0_), channel_id=1, source_target_pairs={{0,2},{2,0},{4,6},{6,4},{8,10},{10,8},{12,14},{14,12},{16,18},{18,... | collective-permute-start | bytes 786440 | tf_op jit(solution)/shard_map/ppermute | solution.py:440
  17.5 4.8 %collective-permute-start.13 = (bf16[16,512]{1,0:T(8,128)(2,1)S(1)}, bf16[16,512]{1,0:T(8,128)(2,1)S(1)}, u32[]{:S(2)}, u32[]{:S(2)}) collective-permute-start(bf16[16,512]{1,0:T(8,128)(2,1)S(1)} %broadcast_select_fusion.1), channel_id=1, source_target_pairs={{0,4},{2,6},{4,8},{6,10},{8,12},{10,14},{12,16},{14,18},{16,20},{1... | collective-permute-start | bytes 49160 | tf_op jit(solution)/shard_map/ppermute | solution.py:440
  22.3 3.2 %collective-permute-start.14 = (bf16[16,512]{1,0:T(8,128)(2,1)S(1)}, bf16[16,512]{1,0:T(8,128)(2,1)S(1)}, u32[]{:S(2)}, u32[]{:S(2)}) collective-permute-start(bf16[16,512]{1,0:T(8,128)(2,1)S(1)} %broadcast_select_fusion.2), channel_id=1, source_target_pairs={{0,2},{2,4},{4,6},{6,8},{8,10},{10,12},{12,14},{14,16},{16,18},{18... | collective-permute-start | bytes 49160 | tf_op jit(solution)/shard_map/ppermute | solution.py:440
  22.3 8.9 %collective-permute-start = (bf16[512,256]{1,0:T(8,128)(2,1)}, bf16[512,256]{1,0:T(8,128)(2,1)S(1)}, u32[]{:S(2)}, u32[]{:S(2)}) collective-permute-start(bf16[512,256]{1,0:T(8,128)(2,1)} %get-tuple-element.11.refs_0_), channel_id=1, source_target_pairs={{0,8},{2,10},{4,12},{6,14},{8,16},{10,18},{12,20},{14,22},{16,24},... | collective-permute-start | bytes 786440 | tf_op jit(solution)/shard_map/ppermute | solution.py:440
  25.5 8.5 %collective-permute-start.22 = (bf16[512,256]{1,0:T(8,128)(2,1)}, bf16[512,256]{1,0:T(8,128)(2,1)S(1)}, u32[]{:S(2)}, u32[]{:S(2)}) collective-permute-start(bf16[512,256]{1,0:T(8,128)(2,1)} %get-tuple-element.13.refs_0_), channel_id=1, source_target_pairs={{0,4},{2,6},{4,0},{6,2},{8,12},{10,14},{12,8},{14,10},{16,20},{18,... | collective-permute-start | bytes 786440 | tf_op jit(solution)/shard_map/ppermute | solution.py:440
  26.2 26.9 %copy-start.3 = (bf16[512,256]{1,0:T(8,128)(2,1)}, bf16[512,256]{1,0:T(8,128)(2,1)S(1)}, u32[]{:S(2)}) copy-start(bf16[512,256]{1,0:T(8,128)(2,1)S(1)} %collective-permute-done.7.refs_7_) | copy-start | bytes 786436
  26.2 8.9 %collective-permute-start.17 = (bf16[512,256]{1,0:T(8,128)(2,1)}, bf16[512,256]{1,0:T(8,128)(2,1)S(1)}, u32[]{:S(2)}, u32[]{:S(2)}) collective-permute-start(bf16[512,256]{1,0:T(8,128)(2,1)} %get-tuple-element.13.refs_0_), channel_id=1, source_target_pairs={{0,2},{2,0},{4,6},{6,4},{8,10},{10,8},{12,14},{14,12},{16,18},{18,... | collective-permute-start | bytes 786440 | tf_op jit(solution)/shard_map/ppermute | solution.py:440
  27.5 25.7 %copy-start.4 = (bf16[512,256]{1,0:T(8,128)(2,1)}, bf16[512,256]{1,0:T(8,128)(2,1)S(1)}, u32[]{:S(2)}) copy-start(bf16[512,256]{1,0:T(8,128)(2,1)S(1)} %collective-permute-done.2.refs_3_) | copy-start | bytes 786436
  27.5 9.8 %collective-permute-start.15 = (bf16[512,256]{1,0:T(8,128)(2,1)}, bf16[512,256]{1,0:T(8,128)(2,1)S(1)}, u32[]{:S(2)}, u32[]{:S(2)}) collective-permute-start(bf16[512,256]{1,0:T(8,128)(2,1)} %get-tuple-element.13.refs_0_), channel_id=1, source_target_pairs={{0,8},{2,10},{4,12},{6,14},{8,16},{10,18},{12,20},{14,22},{16,24},... | collective-permute-start | bytes 786440 | tf_op jit(solution)/shard_map/ppermute | solution.py:440
  31.2 12.8 %copy-start.8 = (bf16[512,256]{1,0:T(8,128)(2,1)}, bf16[512,256]{1,0:T(8,128)(2,1)S(1)}, u32[]{:S(2)}) copy-start(bf16[512,256]{1,0:T(8,128)(2,1)S(1)} %collective-permute-done.refs_1_) | copy-start | bytes 786436
  31.2 6.3 %collective-permute-start.9 = (bf16[512,256]{1,0:T(8,128)(2,1)S(1)}, bf16[512,256]{1,0:T(8,128)(2,1)S(1)}, u32[]{:S(2)}, u32[]{:S(2)}) collective-permute-start(bf16[512,256]{1,0:T(8,128)(2,1)S(1)} %collective-permute-done.7.refs_7_), channel_id=1, source_target_pairs={{0,2},{2,0},{4,6},{6,4},{8,10},{10,8},{12,14},{14,12},{16,18},{18,... | collective-permute-start | bytes 786440 | tf_op jit(solution)/shard_map/ppermute | solution.py:440
  34.0 19.2 %copy-start.5 = (bf16[512,256]{1,0:T(8,128)(2,1)}, bf16[512,256]{1,0:T(8,128)(2,1)S(1)}, u32[]{:S(2)}) copy-start(bf16[512,256]{1,0:T(8,128)(2,1)S(1)} %collective-permute-done.22.refs_7_) | copy-start | bytes 786436
  34.0 9.2 %collective-permute-start.5 = (bf16[512,256]{1,0:T(8,128)(2,1)S(1)}, bf16[512,256]{1,0:T(8,128)(2,1)}, u32[]{:S(2)}, u32[]{:S(2)}) collective-permute-start(bf16[512,256]{1,0:T(8,128)(2,1)S(1)} %collective-permute-done.refs_1_), channel_id=1, source_target_pairs={{0,4},{2,6},{4,0},{6,2},{8,12},{10,14},{12,8},{14,10},{16,20},{18,... | collective-permute-start | bytes 786440 | tf_op jit(solution)/shard_map/ppermute | solution.py:440
  35.2 18.0 %copy-start.6 = (bf16[512,256]{1,0:T(8,128)(2,1)}, bf16[512,256]{1,0:T(8,128)(2,1)S(1)}, u32[]{:S(2)}) copy-start(bf16[512,256]{1,0:T(8,128)(2,1)S(1)} %collective-permute-done.17.refs_3_) | copy-start | bytes 786436
  35.2 8.9 %collective-permute-start.3 = (bf16[512,256]{1,0:T(8,128)(2,1)S(1)}, bf16[512,256]{1,0:T(8,128)(2,1)}, u32[]{:S(2)}, u32[]{:S(2)}) collective-permute-start(bf16[512,256]{1,0:T(8,128)(2,1)S(1)} %collective-permute-done.refs_1_), channel_id=1, source_target_pairs={{0,8},{2,10},{4,12},{6,14},{8,16},{10,18},{12,20},{14,22},{16,24},... | collective-permute-start | bytes 786440 | tf_op jit(solution)/shard_map/ppermute | solution.py:440
  37.2 28.4 %copy-start.7 = (bf16[512,256]{1,0:T(8,128)(2,1)}, bf16[512,256]{1,0:T(8,128)(2,1)S(1)}, u32[]{:S(2)}) copy-start(bf16[512,256]{1,0:T(8,128)(2,1)S(1)} %collective-permute-done.15.refs_1_) | copy-start | bytes 786436
  37.3 9.0 %collective-permute-start.1 = (bf16[512,256]{1,0:T(8,128)(2,1)S(1)}, bf16[512,256]{1,0:T(8,128)(2,1)S(1)}, u32[]{:S(2)}, u32[]{:S(2)}) collective-permute-start(bf16[512,256]{1,0:T(8,128)(2,1)S(1)} %collective-permute-done.refs_1_), channel_id=1, source_target_pairs={{0,2},{2,0},{4,6},{6,4},{8,10},{10,8},{12,14},{14,12},{16,18},{18,... | collective-permute-start | bytes 786440 | tf_op jit(solution)/shard_map/ppermute | solution.py:440
  37.5 8.7 %copy-start.10 = (bf16[512,256]{1,0:T(8,128)(2,1)}, bf16[512,256]{1,0:T(8,128)(2,1)S(1)}, u32[]{:S(2)}) copy-start(bf16[512,256]{1,0:T(8,128)(2,1)S(1)} %collective-permute-done.9.refs_9_) | copy-start | bytes 786436
  37.5 15.6 %collective-permute-start.24 = (bf16[512,256]{1,0:T(8,128)(2,1)S(1)}, bf16[512,256]{1,0:T(8,128)(2,1)S(1)}, u32[]{:S(2)}, u32[]{:S(2)}) collective-permute-start(bf16[512,256]{1,0:T(8,128)(2,1)S(1)} %collective-permute-done.22.refs_7_), channel_id=1, source_target_pairs={{0,2},{2,0},{4,6},{6,4},{8,10},{10,8},{12,14},{14,12},{16,18},{18,... | collective-permute-start | bytes 786440 | tf_op jit(solution)/shard_map/ppermute | solution.py:440
  43.2 10.1 %collective-permute-start.20 = (bf16[512,256]{1,0:T(8,128)(2,1)S(1)}, bf16[512,256]{1,0:T(8,128)(2,1)S(1)}, u32[]{:S(2)}, u32[]{:S(2)}) collective-permute-start(bf16[512,256]{1,0:T(8,128)(2,1)S(1)} %collective-permute-done.15.refs_1_), channel_id=1, source_target_pairs={{0,4},{2,6},{4,0},{6,2},{8,12},{10,14},{12,8},{14,10},{16,20},{18,... | collective-permute-start | bytes 786440 | tf_op jit(solution)/shard_map/ppermute | solution.py:440
  44.1 9.7 %collective-permute-start.18 = (bf16[512,256]{1,0:T(8,128)(2,1)S(1)}, bf16[512,256]{1,0:T(8,128)(2,1)}, u32[]{:S(2)}, u32[]{:S(2)}) collective-permute-start(bf16[512,256]{1,0:T(8,128)(2,1)S(1)} %collective-permute-done.15.refs_1_), channel_id=1, source_target_pairs={{0,8},{2,10},{4,12},{6,14},{8,16},{10,18},{12,20},{14,22},{16,24},... | collective-permute-start | bytes 786440 | tf_op jit(solution)/shard_map/ppermute | solution.py:440
  46.2 6.9 %copy-start.13 = (bf16[512,256]{1,0:T(8,128)(2,1)}, bf16[512,256]{1,0:T(8,128)(2,1)S(1)}, u32[]{:S(2)}) copy-start(bf16[512,256]{1,0:T(8,128)(2,1)S(1)} %collective-permute-done.1.refs_2_) | copy-start | bytes 786436
  46.2 11.5 %collective-permute-start.8 = (bf16[512,256]{1,0:T(8,128)(2,1)}, bf16[512,256]{1,0:T(8,128)(2,1)}, u32[]{:S(2)}, u32[]{:S(2)}) collective-permute-start(bf16[512,256]{1,0:T(8,128)(2,1)} %collective-permute-done.3.refs_11_), channel_id=1, source_target_pairs={{0,4},{2,6},{4,0},{6,2},{8,12},{10,14},{12,8},{14,10},{16,20},{18,... | collective-permute-start | bytes 786440 | tf_op jit(solution)/shard_map/ppermute | solution.py:440
  53.2 0.7 copy-start.9
  53.2 13.0 %collective-permute-start.4 = (bf16[512,256]{1,0:T(8,128)(2,1)}, bf16[512,256]{1,0:T(8,128)(2,1)S(1)}, u32[]{:S(2)}, u32[]{:S(2)}) collective-permute-start(bf16[512,256]{1,0:T(8,128)(2,1)} %collective-permute-done.3.refs_11_), channel_id=1, source_target_pairs={{0,2},{2,0},{4,6},{6,4},{8,10},{10,8},{12,14},{14,12},{16,18},{18,... | collective-permute-start | bytes 786440 | tf_op jit(solution)/shard_map/ppermute | solution.py:440
  53.3 2.4 %copy-start.11 = (bf16[512,256]{1,0:T(8,128)(2,1)}, bf16[512,256]{1,0:T(8,128)(2,1)S(1)}, u32[]{:S(2)}) copy-start(bf16[512,256]{1,0:T(8,128)(2,1)S(1)} %collective-permute-done.20.refs_5_) | copy-start | bytes 786436
  53.3 12.4 %collective-permute-start.6 = (bf16[512,256]{1,0:T(8,128)(2,1)}, bf16[512,256]{1,0:T(8,128)(2,1)}, u32[]{:S(2)}, u32[]{:S(2)}) collective-permute-start(bf16[512,256]{1,0:T(8,128)(2,1)} %collective-permute-done.5.refs_5_), channel_id=1, source_target_pairs={{0,2},{2,0},{4,6},{6,4},{8,10},{10,8},{12,14},{14,12},{16,18},{18,... | collective-permute-start | bytes 786440 | tf_op jit(solution)/shard_map/ppermute | solution.py:440
  53.9 12.3 %collective-permute-start.23 = (bf16[512,256]{1,0:T(8,128)(2,1)}, bf16[512,256]{1,0:T(8,128)(2,1)S(1)}, u32[]{:S(2)}, u32[]{:S(2)}) collective-permute-start(bf16[512,256]{1,0:T(8,128)(2,1)} %collective-permute-done.18.refs_11_), channel_id=1, source_target_pairs={{0,4},{2,6},{4,0},{6,2},{8,12},{10,14},{12,8},{14,10},{16,20},{18,... | collective-permute-start | bytes 786440 | tf_op jit(solution)/shard_map/ppermute | solution.py:440
  57.8 8.5 %copy-start.12 = (bf16[512,256]{1,0:T(8,128)(2,1)S(1)}, bf16[512,256]{1,0:T(8,128)(2,1)}, u32[]{:S(2)}) copy-start(bf16[512,256]{1,0:T(8,128)(2,1)} %copy-done.11) | copy-start | bytes 786436
  57.8 9.0 %collective-permute-start.10 = (bf16[512,256]{1,0:T(8,128)(2,1)}, bf16[512,256]{1,0:T(8,128)(2,1)}, u32[]{:S(2)}, u32[]{:S(2)}) collective-permute-start(bf16[512,256]{1,0:T(8,128)(2,1)} %collective-permute-done.8.refs_8_), channel_id=1, source_target_pairs={{0,2},{2,0},{4,6},{6,4},{8,10},{10,8},{12,14},{14,12},{16,18},{18,... | collective-permute-start | bytes 786440 | tf_op jit(solution)/shard_map/ppermute | solution.py:440
  65.7 17.1 %collective-permute-start.16 = (bf16[512,256]{1,0:T(8,128)(2,1)S(1)}, bf16[512,256]{1,0:T(8,128)(2,1)}, u32[]{:S(2)}, u32[]{:S(2)}) collective-permute-start(bf16[512,256]{1,0:T(8,128)(2,1)S(1)} %collective-permute-done.15.refs_1_), channel_id=1, source_target_pairs={{0,2},{2,0},{4,6},{6,4},{8,10},{10,8},{12,14},{14,12},{16,18},{18,... | collective-permute-start | bytes 786440 | tf_op jit(solution)/shard_map/ppermute | solution.py:440
  66.2 1.1 copy-start.15
  66.2 16.7 %collective-permute-start.19 = (bf16[512,256]{1,0:T(8,128)(2,1)}, bf16[512,256]{1,0:T(8,128)(2,1)}, u32[]{:S(2)}, u32[]{:S(2)}) collective-permute-start(bf16[512,256]{1,0:T(8,128)(2,1)} %collective-permute-done.18.refs_11_), channel_id=1, source_target_pairs={{0,2},{2,0},{4,6},{6,4},{8,10},{10,8},{12,14},{14,12},{16,18},{18,... | collective-permute-start | bytes 786440 | tf_op jit(solution)/shard_map/ppermute | solution.py:440
  66.3 16.5 %copy-start.14 = (bf16[512,256]{1,0:T(8,128)(2,1)}, bf16[512,256]{1,0:T(8,128)(2,1)S(1)}, u32[]{:S(2)}) copy-start(bf16[512,256]{1,0:T(8,128)(2,1)S(1)} %collective-permute-done.23.refs_8_) | copy-start | bytes 786436
  66.3 16.6 %collective-permute-start.21 = (bf16[512,256]{1,0:T(8,128)(2,1)S(1)}, bf16[512,256]{1,0:T(8,128)(2,1)}, u32[]{:S(2)}, u32[]{:S(2)}) collective-permute-start(bf16[512,256]{1,0:T(8,128)(2,1)S(1)} %copy-done.12), channel_id=1, source_target_pairs={{0,2},{2,0},{4,6},{6,4},{8,10},{10,8},{12,14},{14,12},{16,18},{18,... | collective-permute-start | bytes 786440 | tf_op jit(solution)/shard_map/ppermute | solution.py:440
  66.7 16.1 %collective-permute-start.25 = (bf16[512,256]{1,0:T(8,128)(2,1)S(1)}, bf16[512,256]{1,0:T(8,128)(2,1)}, u32[]{:S(2)}, u32[]{:S(2)}) collective-permute-start(bf16[512,256]{1,0:T(8,128)(2,1)S(1)} %collective-permute-done.23.refs_8_), channel_id=1, source_target_pairs={{0,2},{2,0},{4,6},{6,4},{8,10},{10,8},{12,14},{14,12},{16,18},{18,... | collective-permute-start | bytes 786440 | tf_op jit(solution)/shard_map/ppermute | solution.py:440
  66.8 46.8 %collective-permute-start.29 = (bf16[1024,1024]{1,0:T(8,128)(2,1)S(1)}, bf16[1024,1024]{1,0:T(8,128)(2,1)}, u32[]{:S(2)}, u32[]{:S(2)}) collective-permute-start(bf16[1024,1024]{1,0:T(8,128)(2,1)S(1)} %collective-permute-done.28.wa_ref), channel_id=1, source_target_pairs={{0,2},{2,0},{4,6},{6,4},{8,10},{10,8},{12,14},{14,12},{16,18},{18,... | collective-permute-start | bytes 6291464 | tf_op jit(solution)/shard_map/ppermute | solution.py:440
  82.8 18.8 %copy-start.1 = (bf16[512,512]{1,0:T(8,128)(2,1)S(1)}, bf16[512,512]{1,0:T(8,128)(2,1)}, u32[]{:S(2)}) copy-start(bf16[512,512]{1,0:T(8,128)(2,1)} %attend.2.own0) | copy-start | bytes 1572868
  82.8 27.6 %collective-permute-start.26 = (bf16[512,512]{1,0:T(8,128)(2,1)}, bf16[512,512]{1,0:T(8,128)(2,1)S(1)}, u32[]{:S(2)}, u32[]{:S(2)}) collective-permute-start(bf16[512,512]{1,0:T(8,128)(2,1)} %attend.2.own0), channel_id=1, source_target_pairs={{0,1},{1,0},{2,3},{3,2},{4,5},{5,4},{6,7},{7,6},{8,9},{9,8},{10,11... | collective-permute-start | bytes 1572872 | tf_op jit(solution)/shard_map/ppermute | solution.py:440
  96.9 16.7 %collective-permute-start.27 = (bf16[512,512]{1,0:T(8,128)(2,1)}, bf16[512,512]{1,0:T(8,128)(2,1)S(1)}, u32[]{:S(2)}, u32[]{:S(2)}) collective-permute-start(bf16[512,512]{1,0:T(8,128)(2,1)} %attend.3.own1), channel_id=1, source_target_pairs={{0,1},{1,0},{2,3},{3,2},{4,5},{5,4},{6,7},{7,6},{8,9},{9,8},{10,11... | collective-permute-start | bytes 1572872 | tf_op jit(solution)/shard_map/ppermute | solution.py:440
  101.6 2.2 %copy-start = (bf16[512,4096]{1,0:T(8,128)(2,1)S(1)}, bf16[512,4096]{1,0:T(8,128)(2,1)}, u32[]{:S(2)}) copy-start(bf16[512,4096]{1,0:T(8,128)(2,1)} %tok_ref.7) | copy-start | bytes 12582916
  103.8 1.0 copy-start.2

commit v4 on v3

v4 whole, which is shorter than its diff:
```python
import functools

import jax
import jax.numpy as jnp
from jax import lax
from jax.experimental import pallas as pl
from jax.experimental.pallas import tpu as pltpu
from jax.sharding import PartitionSpec as P


HEAD_DIM = 128
PAIR = 2 * HEAD_DIM
SINK = 4
SINK_ROWS = 16
SPAN = 9
QUAD = (SPAN - 1) // 2
EPSILON = 1e-05
LOG2E = 1.4426950408889634
LOW = -1e30
UNROLL = 2
NOWHERE = 1 << 20
MIB = 1024 * 1024
ALL_VMEM = 67043328 - 128 * 1024
ANY = pl.BlockSpec(memory_space=pltpu.HBM)
SMEM = pl.BlockSpec(memory_space=pltpu.SMEM)


def keys_values_kernel(place, tok_ref, gain_ref, wk_ref, wv_ref, w_hbm, *refs):
    groups = wk_ref.shape[1] // HEAD_DIM
    kv_ref, scale_ref, send_hbm, k_acc, v_acc, squares, w_vmem, sem_in, sem_out = refs
    step, steps = pl.program_id(0), pl.num_programs(0)
    piece = send_hbm.shape[1]
    columns = pl.ds(pl.multiple_of(place[0], HEAD_DIM), piece)
    fetch = pltpu.make_async_copy(w_hbm.at[:, columns], w_vmem, sem_in)
    store = pltpu.make_async_copy(w_vmem, send_hbm, sem_out)

    @pl.when(step == 0)
    def _():
        fetch.start()
        k_acc[...] = jnp.zeros(k_acc.shape, jnp.float32)
        v_acc[...] = jnp.zeros(v_acc.shape, jnp.float32)
        squares[...] = jnp.zeros(squares.shape, jnp.float32)

    @pl.when(step == steps // 2)
    def _():
        fetch.wait()
        store.start()

    widened = tok_ref[...].astype(jnp.float32)
    scaled = (widened * gain_ref[...]).astype(jnp.bfloat16)
    k_acc[...] += jnp.dot(scaled, wk_ref[...], preferred_element_type=jnp.float32)
    v_acc[...] += jnp.dot(scaled, wv_ref[...], preferred_element_type=jnp.float32)
    square = widened * widened
    total = square[:, :HEAD_DIM]
    for lo in range(HEAD_DIM, square.shape[1], HEAD_DIM):
        total += square[:, lo : lo + HEAD_DIM]
    squares[...] += total

    @pl.when(step == steps - 1)
    def _():
        mean = jnp.sum(squares[...], axis=1, keepdims=True) / (steps * tok_ref.shape[1])
        scale = jnp.broadcast_to(lax.rsqrt(mean + EPSILON), scale_ref.shape)
        scale_ref[...] = scale
        for g in range(groups):
            at = slice(g * HEAD_DIM, (g + 1) * HEAD_DIM)
            pair = jnp.concatenate([k_acc[:, at] * scale, v_acc[:, at] * scale], axis=1).astype(jnp.bfloat16)
            kv_ref[:, g * PAIR : (g + 1) * PAIR] = pair
        store.wait()


def keys_values(place, tokens, gain, w_key, w_value, w_out, piece):
    rows, width = tokens.shape
    narrow = w_key.shape[1]
    groups = narrow // HEAD_DIM
    chunk = width // 4
    fixed = lambda shape: pl.BlockSpec(shape, lambda i, place: (0, 0))
    return pl.pallas_call(
        keys_values_kernel,
        grid_spec=pltpu.PrefetchScalarGridSpec(
            num_scalar_prefetch=1,
            grid=(width // chunk,),
            in_specs=[
                pl.BlockSpec((rows, chunk), lambda i, place: (0, i)),
                pl.BlockSpec((1, chunk), lambda i, place: (0, i)),
                pl.BlockSpec((chunk, narrow), lambda i, place: (i, 0)),
                pl.BlockSpec((chunk, narrow), lambda i, place: (i, 0)),
                ANY,
            ],
            out_specs=[fixed((rows, groups * PAIR))]
            + [fixed((rows, HEAD_DIM)), ANY],
            scratch_shapes=[
                pltpu.VMEM((rows, narrow), jnp.float32),
                pltpu.VMEM((rows, narrow), jnp.float32),
                pltpu.VMEM((rows, HEAD_DIM), jnp.float32),
                pltpu.VMEM((w_out.shape[0], piece), jnp.bfloat16),
                pltpu.SemaphoreType.DMA,
                pltpu.SemaphoreType.DMA,
            ],
        ),
        out_shape=[jax.ShapeDtypeStruct((rows, groups * PAIR), jnp.bfloat16)]
        + [
            jax.ShapeDtypeStruct((rows, HEAD_DIM), jnp.float32),
            jax.ShapeDtypeStruct((w_out.shape[0], piece), jnp.bfloat16),
        ],
        compiler_params=pltpu.CompilerParams(vmem_limit_bytes=60 * MIB),
        cost_estimate=pl.CostEstimate(
            flops=4 * rows * width * narrow, bytes_accessed=2 * width * (rows + 2 * narrow), transcendentals=rows
        ),
        name="keys_values",
    )(place, tokens, gain, w_key, w_value, w_out)


def query_kernel(tok_ref, gain_ref, w_ref, scale_ref, q_ref, acc):
    step = pl.program_id(0)
    scaled = (tok_ref[...].astype(jnp.float32) * gain_ref[...]).astype(jnp.bfloat16)
    add = jnp.dot(scaled, w_ref[...], preferred_element_type=jnp.float32)

    @pl.when(step == 0)
    def _():
        acc[...] = add

    @pl.when(step > 0)
    def _():
        acc[...] += add

    @pl.when(step == pl.num_programs(0) - 1)
    def _():
        scale = scale_ref[...] * (HEAD_DIM**-0.5 * LOG2E)
        scale = jnp.concatenate([scale] * (acc.shape[1] // HEAD_DIM), axis=1)
        q_ref[...] = (acc[...] * scale).astype(jnp.bfloat16)


def project_queries(tokens, gain, w_query, scale):
    rows, width = tokens.shape
    share = w_query.shape[1]
    chunk = width // 4
    return pl.pallas_call(
        query_kernel,
        grid=(width // chunk,),
        in_specs=[
            pl.BlockSpec((rows, chunk), lambda i: (0, i)),
            pl.BlockSpec((1, chunk), lambda i: (0, i)),
            pl.BlockSpec((chunk, share), lambda i: (i, 0)),
            pl.BlockSpec(scale.shape, lambda i: (0, 0)),
        ],
        out_specs=pl.BlockSpec((rows, share), lambda i: (0, 0)),
        out_shape=jax.ShapeDtypeStruct((rows, share), jnp.bfloat16),
        scratch_shapes=[pltpu.VMEM((rows, share), jnp.float32)],
        compiler_params=pltpu.CompilerParams(vmem_limit_bytes=58 * MIB),
        cost_estimate=pl.CostEstimate(
            flops=2 * rows * width * share, bytes_accessed=2 * width * (rows + share), transcendentals=0
        ),
        name="queries",
    )(tokens, gain, w_query, scale)


def early_blocks(me):
    twin, core = me ^ 1, me % 2
    return [me, me - 4, jnp.where(core == 0, twin - 4, -1), jnp.where(core == 1, twin, -1)]


def late_blocks(me):
    twin, across, mirror = me ^ 1, me ^ 2, me ^ 3
    core, side = me % 2, (me // 2) % 2
    return [
        me - 8,
        across - 4,
        mirror - 4,
        jnp.where(core == 0, twin - 8, -1),
        jnp.where(side == 1, across, -1),
        jnp.where(side == 1, mirror, -1),
        jnp.where(core == 1, twin - 4, -1),
        jnp.where(side == 0, across - 8, -1),
        jnp.where(side == 0, mirror - 8, -1),
    ]


def attend_kernel(groups, per_group, sources, start, *refs):
    window, sinks, bias, q_hbm = refs[:4]
    sent = 1 + max(ref for slot in sources for ref, _ in slot)
    kv_refs, refs = refs[4 : 4 + sent], refs[4 + sent :]
    if start:
        acc_hbm, packed_hbm = refs[:2]
        refs = refs[2:]
    else:
        sink_old, sink_new, acc_hbm, packed_hbm, out_hbm, sink_ref, out_ref = refs[:5] + refs[-2:]
        refs = refs[5:-2]
    q_ref, kvbuf, sems, items, s_even, s_odd, x_even, x_odd, m_ref, acc_ref, packed_ref = refs
    bufs = ((s_even, x_even), (s_odd, x_odd))
    rows, key_rows = q_ref.shape[0], kvbuf.shape[1]
    share, buffers = len(groups), kvbuf.shape[0]
    heads = share * per_group
    base_head = groups[0] * per_group
    all_heads = acc_hbm.shape[0]
    lanes = key_rows // HEAD_DIM
    own = lax.axis_index("seq")
    query_start = own * rows
    table = early_blocks(own) if start else late_blocks(own)
    acc_vmem = acc_ref.at[:, :, pl.ds(0, HEAD_DIM)]
    copies = [
        pltpu.make_async_copy(
            q_hbm.at[:, pl.ds(base_head * HEAD_DIM, heads * HEAD_DIM)], q_ref, sems.at[buffers]
        )
    ]
    if not start:
        copies += [
            pltpu.make_async_copy(acc_hbm.at[pl.ds(base_head, heads)], acc_vmem, sems.at[buffers + 1]),
            pltpu.make_async_copy(packed_hbm, packed_ref, sems.at[buffers + 2]),
            pltpu.make_async_copy(sink_old, sink_ref.at[0], sems.at[buffers + 3]),
            pltpu.make_async_copy(sink_new, sink_ref.at[1], sems.at[buffers + 4]),
        ]
    longest = [window[base_head + g * per_group] for g in range(share)]
    for g in range(share):
        for head in range(1, per_group):
            longest[g] = jnp.maximum(longest[g], window[base_head + g * per_group + head])
    wanted = []
    for s, slot in enumerate(sources):
        for g, (ref, column) in enumerate(slot):
            need = (table[s] >= 0) & ((own - table[s]) * rows - (rows - 1) < longest[g])
            copy = pltpu.make_async_copy(
                kv_refs[ref].at[:, pl.ds(column, PAIR)],
                kvbuf.at[s * share + g, :, pl.ds(0, PAIR)],
                sems.at[s * share + g],
            )
            wanted.append((need, copy))
            pl.when(need)(copy.start)
    for copy in copies:
        copy.start()
    kvbuf[:, :, PAIR:] = jnp.ones((buffers, key_rows, HEAD_DIM), jnp.bfloat16)
    if start:
        m_ref[...] = jnp.full(m_ref.shape, LOW, jnp.float32)
        acc_ref[...] = jnp.zeros(acc_ref.shape, jnp.float32)

    def put(n, head, kv, gap):
        items[0, n] = head
        items[1, n] = kv
        items[2, n] = gap

    def scan(s, block, n, want_whole):
        gap = (own - block) * rows

        def add(head, n):
            reach = window[base_head + head]
            put(n, head, s * share + head // per_group, gap)
            some = gap - (rows - 1) < reach
            whole = (gap > 0) & (gap + rows - 1 < reach)
            return n + (whole if want_whole else some & jnp.logical_not(whole)).astype(jnp.int32)

        return lax.fori_loop(0, jnp.where(block >= 0, heads, 0), add, n)

    n = jnp.int32(0)
    for s, block in enumerate(table):
        n = scan(s, block, n, False)
    masked = n
    for s, block in enumerate(table):
        n = scan(s, block, n, True)
    odd = lax.rem(n, UNROLL)

    @pl.when(odd > 0)
    def _():
        loaded = items[1, 0]

        def shift(k, carry):
            for row in range(3):
                items[row, n - k] = items[row, n - k - 1]
            return carry

        lax.fori_loop(0, n - masked, shift, 0)
        put(masked, 0, loaded, NOWHERE)

    masked_turns = (masked + odd + UNROLL - 1) // UNROLL
    all_turns = (n + odd) // UNROLL
    put(n + odd, 0, 0, NOWHERE)
    diff = lax.broadcasted_iota(jnp.int32, (rows, key_rows), 0) - lax.broadcasted_iota(
        jnp.int32, (rows, key_rows), 1
    )
    for copy in copies:
        copy.wait()
    for need, copy in wanted:
        pl.when(need)(copy.wait)
    if not start:
        for head in range(heads):
            top = packed_ref[:, base_head + head : base_head + head + 1]
            total = packed_ref[:, all_heads + base_head + head : all_heads + base_head + head + 1]
            m_ref[head] = jnp.broadcast_to(top, (rows, HEAD_DIM))
            acc_ref[head, :, HEAD_DIM:] = jnp.broadcast_to(total, (rows, HEAD_DIM))

    def scores_of(head, keys):
        if isinstance(head, int):
            at = slice(head * HEAD_DIM, (head + 1) * HEAD_DIM)
        else:
            at = pl.ds(pl.multiple_of(head * HEAD_DIM, HEAD_DIM), HEAD_DIM)
        return lax.dot_general(
            q_ref[:, at], keys, (((1,), (1,)), ((), ())), preferred_element_type=jnp.float32
        )

    def score(i, buf, mask):
        head = items[0, i]
        scores = scores_of(head, kvbuf[items[1, i], :, :HEAD_DIM])
        if mask:
            high = window[base_head + head] - items[2, i]
            seen = diff < high
            if start:
                seen = seen & (diff >= -items[2, i])
            scores = jnp.where(seen, scores, LOW)
        buf[0][...] = scores
        top = scores[:, :HEAD_DIM]
        for part in range(1, lanes):
            top = jnp.maximum(top, scores[:, part * HEAD_DIM : (part + 1) * HEAD_DIM])
        buf[1][...] = top

    def fold(head, scores, top, vaug):
        m_prev = m_ref[head]
        m_new = jnp.maximum(m_prev, jnp.max(top, axis=1, keepdims=True))
        alpha = jnp.exp2(m_prev - m_new)
        m_ref[head] = m_new
        shift = jnp.concatenate([m_new] * (scores.shape[1] // HEAD_DIM), axis=1)
        weights = jnp.exp2(scores - shift).astype(jnp.bfloat16)
        add = jnp.dot(weights, vaug, preferred_element_type=jnp.float32)
        acc_ref[head] = acc_ref[head] * jnp.concatenate([alpha, alpha], axis=1) + add

    def turns(first, last, mask):
        def turn(j, carry):
            for u in range(UNROLL):
                i = UNROLL * j + u
                score(i + 1, bufs[(u + 1) % 2], mask)
                held, top = bufs[u % 2]
                fold(items[0, i], held[...], top[...], kvbuf[items[1, i], :, HEAD_DIM:])
            return carry

        lax.fori_loop(first, last, turn, 0)

    score(0, bufs[0], True)
    turns(0, masked_turns, True)
    turns(masked_turns, all_turns, False)
    if start:
        store = pltpu.make_async_copy(acc_vmem, acc_hbm, sems.at[buffers + 1])
        store.start()
        lane = lax.broadcasted_iota(jnp.int32, (rows, HEAD_DIM), 1)
        packed = jnp.zeros((rows, HEAD_DIM), jnp.float32)
        for head in range(heads):
            packed = jnp.where(lane == head, m_ref[head], packed)
            packed = jnp.where(lane == all_heads + head, acc_ref[head, :, HEAD_DIM:], packed)
        packed_ref[...] = packed
        second = pltpu.make_async_copy(packed_ref, packed_hbm, sems.at[buffers + 2])
        second.start()
        store.wait()
        second.wait()
        return

    def give(head):
        at = pl.ds(head * HEAD_DIM, HEAD_DIM)
        return pltpu.make_async_copy(out_ref.at[:, at], out_hbm.at[:, at], sems.at[head])

    def finish(head):
        out_ref[:, head * HEAD_DIM : (head + 1) * HEAD_DIM] = (
            acc_ref[head, :, :HEAD_DIM] / acc_ref[head, :, HEAD_DIM:]
        ).astype(jnp.bfloat16)
        give(head).start()

    shortest = window[base_head]
    for head in range(1, heads):
        shortest = jnp.minimum(shortest, window[base_head + head])
    any_open = query_start + rows - 1 - shortest >= 0

    @pl.when(any_open)
    def _():
        column = lax.broadcasted_iota(jnp.int32, (rows, HEAD_DIM), 1)
        row = lax.broadcasted_iota(jnp.int32, (rows, HEAD_DIM), 0)
        pad = jnp.zeros((HEAD_DIM - SINK_ROWS, HEAD_DIM), jnp.bfloat16)
        scored, valued = [], []
        fresh = (own // QUAD) % 2 == 1
        for head in range(heads):
            base = groups[head // per_group] * PAIR
            pair = jnp.where(fresh, sink_ref[1, :, base : base + PAIR], sink_ref[0, :, base : base + PAIR])
            keys = jnp.concatenate([pair[:, :HEAD_DIM], pad], axis=0)
            values = jnp.concatenate([pair[:, HEAD_DIM:], pad], axis=0)
            valued.append(jnp.concatenate([values, jnp.ones((HEAD_DIM, HEAD_DIM), jnp.bfloat16)], axis=1))
            latest = row + (query_start - window[base_head + head])
            count = jnp.minimum(sinks[base_head + head], SINK)
            allowed = (column < count) & (column <= latest)
            scores = scores_of(head, keys) + bias[base_head + head] * LOG2E
            scored.append(jnp.where(allowed, scores, LOW))
        for head in range(heads):
            fold(head, scored[head], scored[head], valued[head])
        for head in range(heads):
            finish(head)

    @pl.when(jnp.logical_not(any_open))
    def _():
        for head in range(heads):
            finish(head)

    for head in range(heads):
        give(head).wait()


def attend(groups, all_groups, scalars, queries, arrays, sources, sinks=None, state=None):
    rows = queries.shape[0]
    key_rows = arrays[0].shape[0]
    per_group = queries.shape[1] // HEAD_DIM // all_groups
    heads = per_group * len(groups)
    buffers = len(sources) * len(groups)
    items = heads * len(sources) + 2 * UNROLL
    f32 = jnp.float32
    scratch = [
        pltpu.VMEM((rows, heads * HEAD_DIM), jnp.bfloat16),
        pltpu.VMEM((buffers, key_rows, 3 * HEAD_DIM), jnp.bfloat16),
        pltpu.SemaphoreType.DMA((buffers + 5,)),
        pltpu.SMEM((3, items), jnp.int32),
        pltpu.VMEM((rows, key_rows), f32),
        pltpu.VMEM((rows, key_rows), f32),
        pltpu.VMEM((rows, HEAD_DIM), f32),
        pltpu.VMEM((rows, HEAD_DIM), f32),
        pltpu.VMEM((heads, rows, HEAD_DIM), f32),
        pltpu.VMEM((heads, rows, PAIR), f32),
        pltpu.VMEM((rows, HEAD_DIM), f32),
    ]
    in_specs = [SMEM] * 3 + [ANY] * (1 + len(arrays))
    operands = [*scalars, queries, *arrays]
    if state is None:
        out_specs = [ANY, ANY]
        out_shape = [
            jax.ShapeDtypeStruct((heads, rows, HEAD_DIM), f32),
            jax.ShapeDtypeStruct((rows, HEAD_DIM), f32),
        ]
    else:
        in_specs += [ANY] * 4
        operands += [*sinks, *state]
        out_specs = ANY
        out_shape = jax.ShapeDtypeStruct((rows, heads * HEAD_DIM), jnp.bfloat16)
        scratch += [
            pltpu.VMEM((2, *sinks[0].shape), jnp.bfloat16),
            pltpu.VMEM((rows, heads * HEAD_DIM), jnp.bfloat16),
        ]
    return pl.pallas_call(
        functools.partial(attend_kernel, groups, per_group, sources, state is None),
        in_specs=in_specs,
        out_specs=out_specs,
        out_shape=out_shape,
        scratch_shapes=scratch,
        compiler_params=pltpu.CompilerParams(vmem_limit_bytes=ALL_VMEM),
        cost_estimate=pl.CostEstimate(
            flops=8 * rows * buffers * key_rows * per_group * HEAD_DIM,
            bytes_accessed=2 * buffers * key_rows * PAIR,
            transcendentals=rows * buffers * key_rows * per_group,
        ),
        name="attend",
    )(*operands)


def project_kernel(where, tok_ref, own0, own1, far_ref, w_ref, wa_ref, wb_ref, out_ref):
    half = own0.shape[1]
    total = jnp.dot(own0[...], w_ref[:half, :], preferred_element_type=jnp.float32)
    total += jnp.dot(own1[...], w_ref[half:, :], preferred_element_type=jnp.float32)
    total += tok_ref[...].astype(jnp.float32)
    far_dot(far_ref, wa_ref, wb_ref, out_ref, total)


def project_last_kernel(where, part_ref, far_ref, wa_ref, wb_ref, out_ref):
    far_dot(far_ref, wa_ref, wb_ref, out_ref, part_ref[...])


def far_dot(far_ref, wa_ref, wb_ref, out_ref, total):
    step, turn = pl.program_id(0), pl.num_programs(0) // 2

    @pl.when(step < turn)
    def _():
        more = jnp.dot(far_ref[...], wa_ref[...], preferred_element_type=jnp.float32)
        out_ref[...] = (total + more).astype(out_ref.dtype)

    @pl.when(step >= turn)
    def _():
        more = jnp.dot(far_ref[...], wb_ref[...], preferred_element_type=jnp.float32)
        out_ref[...] = (total + more).astype(out_ref.dtype)


def project(where, rows, share, row, own_side, far, w_near, w_swap):
    depth, _ = w_near.shape
    tile = 512
    steps = share // tile
    part = steps // 2
    half = far.shape[1]

    def column(j, where):
        return jnp.where(where[1] == 0, j, lax.rem(j + part, steps))

    here = pl.BlockSpec((rows, tile), lambda j, where: (0, column(j, where)))
    shifted = lambda height: pl.BlockSpec((height, tile), lambda j, where: (0, where[0] * steps + column(j, where)))
    fixed = lambda a: pl.BlockSpec(a.shape, lambda j, where: (0, 0))
    far_specs = [
        fixed(far),
        pl.BlockSpec((half, tile), lambda j, where: (row, jnp.minimum(j, part - 1))),
        pl.BlockSpec((half, tile), lambda j, where: (row, jnp.maximum(j - part, 0))),
    ]
    if len(own_side) > 1:
        tokens, own0, own1, w_out = own_side
        kernel, dtype = project_kernel, jnp.float32
        specs = [shifted(rows), fixed(own0), fixed(own1), far_specs[0], shifted(w_out.shape[0]), *far_specs[1:]]
        operands = [tokens, own0, own1, far, w_out, w_near, w_swap]
    else:
        kernel, dtype = project_last_kernel, jnp.bfloat16
        specs = [here, *far_specs]
        operands = [own_side[0], far, w_near, w_swap]
    return pl.pallas_call(
        kernel,
        grid_spec=pltpu.PrefetchScalarGridSpec(
            num_scalar_prefetch=1, grid=(steps,), in_specs=specs, out_specs=here
        ),
        out_shape=jax.ShapeDtypeStruct((rows, share), dtype),
        compiler_params=pltpu.CompilerParams(vmem_limit_bytes=40 * MIB),
        cost_estimate=pl.CostEstimate(
            flops=len(operands) * rows * half * share, bytes_accessed=4 * depth * share, transcendentals=0
        ),
        name="project",
    )(where, *operands)


def local(tokens, norm_gain, w_query, w_key, w_value, w_out, window, sink_count, sink_bias):
    peers = lax.axis_size("seq")
    head_peers = lax.axis_size("head")
    me = lax.axis_index("seq")
    my_head = lax.axis_index("head")
    core, side = me % 2, (me // 2) % 2
    groups = w_key.shape[1] // HEAD_DIM
    share = w_out.shape[1] // head_peers
    piece = share // 2
    gain = norm_gain.reshape(1, -1)
    everyone = range(peers)

    def send(x, pairs, axis="seq"):
        return lax.ppermute(x, axis, pairs)

    ahead = [(i, (i + QUAD) % peers) for i in everyone]
    core_swap = [(i, i ^ 1) for i in everyone]
    side_swap = [(i, i ^ 2) for i in everyone]
    head_swap = [(i, i ^ 1) for i in range(head_peers)]

    scalars = (window, sink_count, sink_bias)
    place = ((1 - my_head) * share + core * piece).astype(jnp.int32).reshape(1)

    kv, scale, w_send = keys_values(place, tokens, gain, w_key, w_value, w_out, piece)
    queries = project_queries(tokens, gain, w_query, scale)

    back4 = send(kv, ahead)
    near_side = send(kv, side_swap)
    w_near = send(w_send, head_swap, "head")
    near_core = send(kv, core_swap)
    back8 = send(back4, ahead)
    across4 = send(back4, side_swap)
    core4 = send(back4, core_swap)
    cross_near = send(near_side, core_swap)
    core8 = send(back8, core_swap)
    cross4 = send(across4, core_swap)
    far, cross_far = [], []
    for g in range(groups):
        at = slice(g * PAIR, (g + 1) * PAIR)
        part = (back8 if g % 2 == 0 else across4)[:, at]
        far.append(send(part, side_swap if g % 2 == 0 else ahead))
        cross_far.append(send(far[g], core_swap))

    top = lambda x: x[:SINK_ROWS]
    left = jnp.where(core == 0, top(kv), top(near_core))
    right = jnp.where(core == 0, top(near_side), top(cross_near))
    arrived = old = jnp.where(side == 0, left, right)
    have = peers
    while have > QUAD:
        old = arrived if have == peers else jnp.where(me % (2 * have) >= have, arrived, old)
        step = have // 2
        arrived = send(old, [(i, (i + step) % peers) for i in everyone])
        have = step
    sinks = (old, arrived)
    w_swap = send(w_near, core_swap)

    every = tuple(range(groups))
    state = attend(
        every,
        groups,
        scalars,
        queries,
        [kv, back4, core4, near_core],
        [[(a, g * PAIR) for g in every] for a in range(4)],
    )
    own, other = [], []
    for g in every:
        att = attend(
            (g,),
            groups,
            scalars,
            queries,
            [back8, across4, cross4, core8, near_side, cross_near, core4, far[g], cross_far[g]],
            [[(a, g * PAIR)] for a in range(7)] + [[(7, 0)], [(8, 0)]],
            sinks,
            state,
        )
        own.append(att)
        other.append(send(att, head_swap, "head"))
    where = jnp.stack([my_head, core]).astype(jnp.int32)
    rows = tokens.shape[0]
    partial = project(where, rows, share, 0, (tokens, *own, w_out), other[0], w_near, w_swap)
    return project(where, rows, share, 1, (partial,), other[1], w_near, w_swap)


def solution(mesh):
    in_specs = (
        P("seq", None),
        P(),
        P(None, "head"),
        P(None, "head"),
        P(None, "head"),
        P("head", None),
        P("head"),
        P("head"),
        P("head"),
    )
    out_specs = P("seq", "head")
    return jax.shard_map(local, mesh=mesh, in_specs=in_specs, out_specs=out_specs, check_vma=False)
```

time: 122 us -> 111 us (0.910); the launches traced: 120 us -> 111 us
  starting transfers between devices: 26.4 us -> 18.1 us
  waiting for transfers between devices: 26.6 us -> 22.5 us
  local copies, waits for them, and re-layouts: 4.03 us -> 7.29 us
    ppermute x30 -> x19, starting transfers between devices: 26.4 us -> 18.1 us  [send(): return lax.ppermute(x, axis, pairs)]
    ppermute x30 -> x19, waiting for transfers between devices: 26.6 us -> 22.5 us  [send(): return lax.ppermute(x, axis, pairs)]
    slice x0 -> x2, local copies, waits for them, and re-layouts: none -> 2.63 us  [local(): part = (back8 if g % 2 == 0 else across4)[:, at]]
    unnamed x32 -> x20, local copies, waits for them, and re-layouts: 3.41 us -> 4.66 us
  transfers between devices with their start and end apart: 30 -> 19, of which waited for: 9 -> 5; matrix products, arithmetic and copies ran while one was open for 2% -> 3% of each run, Pallas kernels for 40% -> 45%
where the time goes in v4:
time: 111 us
  Pallas kernels  61.9 us (56%)
  waiting for transfers between devices  22.5 us (20%)
  starting transfers between devices  18.1 us (16%)
  local copies, waits for them, and re-layouts  7.29 us (7%)
    pallas_call x3, Pallas kernels, attend(): pl.pallas_call(functools.partial(attend_kernel, groups, per_group, source...  32.7 us
    ppermute x19, waiting for transfers between devices, send(): return lax.ppermute(x, axis, pairs)  22.5 us
    ppermute x19, starting transfers between devices, send(): return lax.ppermute(x, axis, pairs)  18.1 us
    pallas_call x2, Pallas kernels, project(): pl.pallas_call(kernel, grid_spec=pltpu.PrefetchScalarGridSpec(num_scalar_...  13.2 us
    pallas_call x1, Pallas kernels, project_queries(): pl.pallas_call(query_kernel, grid=(width // chunk,), in_specs=[pl.BlockSp...  9.42 us
    pallas_call x1, Pallas kernels, keys_values(): pl.pallas_call(keys_values_kernel, grid_spec=pltpu.PrefetchScalarGridSpec...  6.6 us
    unnamed x20, local copies, waits for them, and re-layouts  4.66 us
    slice x2, local copies, waits for them, and re-layouts, local(): part = (back8 if g % 2 == 0 else across4)[:, at]  2.63 us
  transfers between devices with their start and end apart: 19, of which 5 were waited for; matrix products, arithmetic and copies ran while one was open for 3% of the time, Pallas kernels for 45%

profile of v4, /device:TPU:18, one launch (start us, length us, event | category | flops | bytes accessed | tf_op | source)
XLA Modules:
  0.0 110.7 jit_solution(9181251713845602477)
XLA Ops:
  0.0 6.6 %keys_values.1 = (bf16[512,512]{1,0:T(8,128)(2,1)}, f32[512,128]{1,0:T(8,128)}, bf16[1024,1024]{1,0:T(8,128)(2,1)}) custom-call(s32[1]{0:T(128)} %bitcast.3.place, bf16[512,4096]{1,0:T(8,128)(2,1)} %tok_ref.5, f32[1,4096]{1,0:T(1,128)} %bitcast.4, bf16[4096,256]{1,0:T(8,128)(2,1)} %wk_ref.1, bf16[4096,256]{1,0:T(8,128)(2,1)} %wv_ref.1, bf16[1024,4096]{1,0:T(8,128)(2,1)} %w_ref.3), custom_call_target="tpu_custom_call" | custom-call | flops 2147483648 | bytes 8388608 | tf_op jit(solution)/shard_map/keys_values/pallas_call | solution.py:77
  6.6 1.6 %collective-permute-start.16 = (bf16[1024,1024]{1,0:T(8,128)(2,1)}, bf16[1024,1024]{1,0:T(8,128)(2,1)}, u32[]{:S(2)}, u32[]{:S(2)}) collective-permute-start(bf16[1024,1024]{1,0:T(8,128)(2,1)} %get-tuple-element.14), channel_id=1, source_target_pairs={{0,1},{1,0},{2,3},{3,2},{4,5},{5,4},{6,7},{7,6},{8,9},{9,8},{10,11... | collective-permute-start | bytes 6291464 | tf_op jit(solution)/shard_map/ppermute | solution.py:532
  8.2 0.5 collective-permute-start.5
  8.7 1.6 %collective-permute-start = (bf16[512,512]{1,0:T(8,128)(2,1)}, bf16[512,512]{1,0:T(8,128)(2,1)S(1)}, u32[]{:S(2)}, u32[]{:S(2)}) collective-permute-start(bf16[512,512]{1,0:T(8,128)(2,1)} %get-tuple-element.11.refs_4_), channel_id=1, source_target_pairs={{0,8},{2,10},{4,12},{6,14},{8,16},{10,18},{12,20},{14,22},{16,24},... | collective-permute-start | bytes 1572872 | tf_op jit(solution)/shard_map/ppermute | solution.py:532
  10.3 0.0 collective-permute-start.10
  10.3 11.5 %collective-permute-done.5.refs_8_ = bf16[512,512]{1,0:T(8,128)(2,1)S(1)} collective-permute-done((bf16[512,512]{1,0:T(8,128)(2,1)}, bf16[512,512]{1,0:T(8,128)(2,1)S(1)}, u32[]{:S(2)}, u32[]{:S(2)}) %collective-permute-start.5) | collective-permute-done | bytes 524320 | tf_op jit(solution)/shard_map/ppermute | solution.py:532
  21.8 0.0 collective-permute-start.6
  21.8 0.2 collective-permute-done.refs_5_
  22.0 1.6 %collective-permute-start.1 = (bf16[512,512]{1,0:T(8,128)(2,1)S(1)}, bf16[512,512]{1,0:T(8,128)(2,1)}, u32[]{:S(2)}, u32[]{:S(2)}) collective-permute-start(bf16[512,512]{1,0:T(8,128)(2,1)S(1)} %collective-permute-done.refs_5_), channel_id=1, source_target_pairs={{0,8},{2,10},{4,12},{6,14},{8,16},{10,18},{12,20},{14,22},{16,24},... | collective-permute-start | bytes 1572872 | tf_op jit(solution)/shard_map/ppermute | solution.py:532
  23.6 0.0 collective-permute-done.10.refs_7_
  23.6 0.1 collective-permute-done.6.refs_9_
  23.7 0.7 fusion
  24.5 0.6 collective-permute-start.11
  25.1 0.0 collective-permute-start.7
  25.1 1.5 %collective-permute-start.2 = (bf16[512,512]{1,0:T(8,128)(2,1)S(1)}, bf16[512,512]{1,0:T(8,128)(2,1)}, u32[]{:S(2)}, u32[]{:S(2)}) collective-permute-start(bf16[512,512]{1,0:T(8,128)(2,1)S(1)} %collective-permute-done.refs_5_), channel_id=1, source_target_pairs={{0,4},{2,6},{4,0},{6,2},{8,12},{10,14},{12,8},{14,10},{16,20},{18,... | collective-permute-start | bytes 1572872 | tf_op jit(solution)/shard_map/ppermute | solution.py:532
  26.6 10.2 %collective-permute-done.1.refs_4_ = bf16[512,512]{1,0:T(8,128)(2,1)} collective-permute-done((bf16[512,512]{1,0:T(8,128)(2,1)S(1)}, bf16[512,512]{1,0:T(8,128)(2,1)}, u32[]{:S(2)}, u32[]{:S(2)}) %collective-permute-start.1) | collective-permute-done | bytes 524320 | tf_op jit(solution)/shard_map/ppermute | solution.py:532
  36.8 1.0 slice.24
  37.7 0.6 collective-permute-start.8
  38.3 0.0 collective-permute-done.11
  38.4 1.3 %collective-permute-start.12 = (bf16[16,512]{1,0:T(8,128)(2,1)S(1)}, bf16[16,512]{1,0:T(8,128)(2,1)S(1)}, u32[]{:S(2)}, u32[]{:S(2)}) collective-permute-start(bf16[16,512]{1,0:T(8,128)(2,1)S(1)} %broadcast_select_fusion.refs_13_), channel_id=1, source_target_pairs={{0,8},{2,10},{4,12},{6,14},{8,16},{10,18},{12,20},{14,22},{16,24},... | collective-permute-start | bytes 49160 | tf_op jit(solution)/shard_map/ppermute | solution.py:532
  39.6 9.4 %queries.1.refs_3_ = bf16[512,1024]{1,0:T(8,128)(2,1)} custom-call(bf16[512,4096]{1,0:T(8,128)(2,1)} %tok_ref.5, f32[1,4096]{1,0:T(1,128)} %bitcast.5, bf16[4096,1024]{1,0:T(8,128)(2,1)} %w_ref.2, f32[512,128]{1,0:T(8,128)} %get-tuple-element.10.scale_ref), custom_call_target="tpu_custom_call" | custom-call | flops 4294967296 | bytes 12582912 | tf_op jit(solution)/shard_map/queries/pallas_call | solution.py:137
  49.1 0.0 collective-permute-done.2.refs_5_
  49.1 1.7 %slice.28 = bf16[512,256]{1,0:T(8,128)(2,1)} slice(bf16[512,512]{1,0:T(8,128)(2,1)} %collective-permute-done.2.refs_5_), slice={[0:512], [256:512]} | slice | bytes 524288 | tf_op jit(solution)/shard_map/slice | solution.py:558
  50.8 3.2 %collective-permute-start.13 = (bf16[512,256]{1,0:T(8,128)(2,1)}, bf16[512,256]{1,0:T(8,128)(2,1)}, u32[]{:S(2)}, u32[]{:S(2)}) collective-permute-start(bf16[512,256]{1,0:T(8,128)(2,1)} %slice.28), channel_id=1, source_target_pairs={{0,8},{2,10},{4,12},{6,14},{8,16},{10,18},{12,20},{14,22},{16,24},... | collective-permute-start | bytes 786440 | tf_op jit(solution)/shard_map/ppermute | solution.py:532
  54.0 0.0 collective-permute-done.7.refs_6_.refs_10_
  54.0 0.0 collective-permute-start.3
  54.0 0.0 collective-permute-done.12.refs_14_
  54.0 0.5 collective-permute-start.4
  54.5 0.0 collective-permute-done.8.refs_11_
  54.5 0.4 copy-done.8
  54.9 0.5 collective-permute-start.17
  55.4 12.8 %attend.3 = (f32[8,512,128]{2,1,0:T(8,128)}, f32[512,128]{1,0:T(8,128)}) custom-call(s32[8]{0:T(128)} %refs_0_.5, s32[8]{0:T(128)} %refs_1_.5, f32[8]{0:T(128)} %refs_2_.5, bf16[512,1024]{1,0:T(8,128)(2,1)} %queries.1.refs_3_, bf16[512,512]{1,0:T(8,128)(2,1)} %get-tuple-element.11.refs_4_, bf16[512,512]{1,0:T(8,128)(2,1)} %copy-done.7, ...), custom_call_target="tpu_custom_call" | custom-call | flops 8589934592 | bytes 2097152 | tf_op jit(solution)/shard_map/attend/pallas_call | solution.py:436
  68.2 0.0 collective-permute-done.13.refs_11_
  68.2 0.8 collective-permute-start.14
  69.0 0.0 collective-permute-done.3.refs_6_
  69.0 0.0 collective-permute-done.4.refs_7_
  69.0 9.9 %attend.4.own0 = bf16[512,512]{1,0:T(8,128)(2,1)} custom-call(s32[8]{0:T(128)} %refs_0_.5, s32[8]{0:T(128)} %refs_1_.5, f32[8]{0:T(128)} %refs_2_.5, bf16[512,1024]{1,0:T(8,128)(2,1)} %queries.1.refs_3_, bf16[512,512]{1,0:T(8,128)(2,1)} %collective-permute-done.1.refs_4_, bf16[512,512]{1,0:T(8,128)(2,1)} %collective-permute-done.2.refs_5_, ...), custom_call_target="tpu_custom_call" | custom-call | flops 9663676416 | bytes 2359296 | tf_op jit(solution)/shard_map/attend/pallas_call | solution.py:436
  79.0 0.1 collective-permute-start.15
  79.1 9.9 %attend.5.own1 = bf16[512,512]{1,0:T(8,128)(2,1)} custom-call(s32[8]{0:T(128)} %refs_0_.5, s32[8]{0:T(128)} %refs_1_.5, f32[8]{0:T(128)} %refs_2_.5, bf16[512,1024]{1,0:T(8,128)(2,1)} %queries.1.refs_3_, bf16[512,512]{1,0:T(8,128)(2,1)} %collective-permute-done.1.refs_4_, bf16[512,512]{1,0:T(8,128)(2,1)} %collective-permute-done.2.refs_5_, ...), custom_call_target="tpu_custom_call" | custom-call | flops 9663676416 | bytes 2359296 | tf_op jit(solution)/shard_map/attend/pallas_call | solution.py:436
  89.0 3.7 %collective-permute-start.18 = (bf16[512,512]{1,0:T(8,128)(2,1)}, bf16[512,512]{1,0:T(8,128)(2,1)S(1)}, u32[]{:S(2)}, u32[]{:S(2)}) collective-permute-start(bf16[512,512]{1,0:T(8,128)(2,1)} %attend.5.own1), channel_id=1, source_target_pairs={{0,1},{1,0},{2,3},{3,2},{4,5},{5,4},{6,7},{7,6},{8,9},{9,8},{10,11... | collective-permute-start | bytes 1572872 | tf_op jit(solution)/shard_map/ppermute | solution.py:532
  92.7 0.1 pad_add_fusion.where
  92.8 0.5 collective-permute-done.15.far_ref
  93.3 0.0 collective-permute-done.17.wb_ref
  93.3 2.2 %copy-done = bf16[512,4096]{1,0:T(8,128)(2,1)S(1)} copy-done((bf16[512,4096]{1,0:T(8,128)(2,1)S(1)}, bf16[512,4096]{1,0:T(8,128)(2,1)}, u32[]{:S(2)}) %copy-start) | copy-done | bytes 4194328
  95.5 1.0 copy-done.1
  96.5 1.0 copy-done.2
  97.5 7.6 %project.2.part_ref = f32[512,2048]{1,0:T(8,128)S(1)} custom-call(s32[2]{0:T(128)S(1)} %pad_add_fusion.where, bf16[512,4096]{1,0:T(8,128)(2,1)S(1)} %copy-done, bf16[512,512]{1,0:T(8,128)(2,1)S(1)} %copy-done.1, bf16[512,512]{1,0:T(8,128)(2,1)S(1)} %copy-done.2, bf16[512,512]{1,0:T(8,128)(2,1)} %collective-permute-done.15.far_ref, bf16[1024,4096]{1,0:T(8,128)(2,1)} %w_ref.3, ...), custom_call_target="tpu_custom_call" | custom-call | flops 3758096384 | bytes 8388608 | tf_op jit(solution)/shard_map/project/pallas_call | solution.py:505
  105.2 5.6 %project.3 = bf16[512,2048]{1,0:T(8,128)(2,1)} custom-call(s32[2]{0:T(128)S(1)} %pad_add_fusion.where, f32[512,2048]{1,0:T(8,128)S(1)} %project.2.part_ref, bf16[512,512]{1,0:T(8,128)(2,1)S(1)} %collective-permute-done.18.far_ref, bf16[1024,1024]{1,0:T(8,128)(2,1)} %collective-permute-done.16.wa_ref, bf16[1024,1024]{1,0:T(8,128)(2,1)} %collective-permute-done.17.wb_ref), custom_call_target="tpu_custom_call" | custom-call | flops 2147483648 | bytes 8388608 | tf_op jit(solution)/shard_map/project/pallas_call | solution.py:505
  (22 shorter events, 0.0 us)
Async XLA Ops:
  6.6 48.3 %collective-permute-start.16 = (bf16[1024,1024]{1,0:T(8,128)(2,1)}, bf16[1024,1024]{1,0:T(8,128)(2,1)}, u32[]{:S(2)}, u32[]{:S(2)}) collective-permute-start(bf16[1024,1024]{1,0:T(8,128)(2,1)} %get-tuple-element.14), channel_id=1, source_target_pairs={{0,1},{1,0},{2,3},{3,2},{4,5},{5,4},{6,7},{7,6},{8,9},{9,8},{10,11... | collective-permute-start | bytes 6291464 | tf_op jit(solution)/shard_map/ppermute | solution.py:532
  8.2 13.6 %collective-permute-start.5 = (bf16[512,512]{1,0:T(8,128)(2,1)}, bf16[512,512]{1,0:T(8,128)(2,1)S(1)}, u32[]{:S(2)}, u32[]{:S(2)}) collective-permute-start(bf16[512,512]{1,0:T(8,128)(2,1)} %get-tuple-element.11.refs_4_), channel_id=1, source_target_pairs={{0,4},{2,6},{4,0},{6,2},{8,12},{10,14},{12,8},{14,10},{16,20},{18,... | collective-permute-start | bytes 1572872 | tf_op jit(solution)/shard_map/ppermute | solution.py:532
  8.7 13.3 %collective-permute-start = (bf16[512,512]{1,0:T(8,128)(2,1)}, bf16[512,512]{1,0:T(8,128)(2,1)S(1)}, u32[]{:S(2)}, u32[]{:S(2)}) collective-permute-start(bf16[512,512]{1,0:T(8,128)(2,1)} %get-tuple-element.11.refs_4_), channel_id=1, source_target_pairs={{0,8},{2,10},{4,12},{6,14},{8,16},{10,18},{12,20},{14,22},{16,24},... | collective-permute-start | bytes 1572872 | tf_op jit(solution)/shard_map/ppermute | solution.py:532
  10.3 13.3 %collective-permute-start.10 = (bf16[512,512]{1,0:T(8,128)(2,1)}, bf16[512,512]{1,0:T(8,128)(2,1)S(1)}, u32[]{:S(2)}, u32[]{:S(2)}) collective-permute-start(bf16[512,512]{1,0:T(8,128)(2,1)} %get-tuple-element.11.refs_4_), channel_id=1, source_target_pairs={{0,2},{2,0},{4,6},{6,4},{8,10},{10,8},{12,14},{14,12},{16,18},{18,... | collective-permute-start | bytes 1572872 | tf_op jit(solution)/shard_map/ppermute | solution.py:532
  21.8 1.9 %copy-start.4 = (bf16[512,512]{1,0:T(8,128)(2,1)}, bf16[512,512]{1,0:T(8,128)(2,1)S(1)}, u32[]{:S(2)}) copy-start(bf16[512,512]{1,0:T(8,128)(2,1)S(1)} %collective-permute-done.5.refs_8_) | copy-start | bytes 1572868
  21.8 1.9 %collective-permute-start.6 = (bf16[512,512]{1,0:T(8,128)(2,1)S(1)}, bf16[512,512]{1,0:T(8,128)(2,1)S(1)}, u32[]{:S(2)}, u32[]{:S(2)}) collective-permute-start(bf16[512,512]{1,0:T(8,128)(2,1)S(1)} %collective-permute-done.5.refs_8_), channel_id=1, source_target_pairs={{0,2},{2,0},{4,6},{6,4},{8,10},{10,8},{12,14},{14,12},{16,18},{18,... | collective-permute-start | bytes 1572872 | tf_op jit(solution)/shard_map/ppermute | solution.py:532
  22.0 27.0 %copy-start.7 = (bf16[512,512]{1,0:T(8,128)(2,1)}, bf16[512,512]{1,0:T(8,128)(2,1)S(1)}, u32[]{:S(2)}) copy-start(bf16[512,512]{1,0:T(8,128)(2,1)S(1)} %collective-permute-done.refs_5_) | copy-start | bytes 1572868
  22.0 14.7 %collective-permute-start.1 = (bf16[512,512]{1,0:T(8,128)(2,1)S(1)}, bf16[512,512]{1,0:T(8,128)(2,1)}, u32[]{:S(2)}, u32[]{:S(2)}) collective-permute-start(bf16[512,512]{1,0:T(8,128)(2,1)S(1)} %collective-permute-done.refs_5_), channel_id=1, source_target_pairs={{0,8},{2,10},{4,12},{6,14},{8,16},{10,18},{12,20},{14,22},{16,24},... | collective-permute-start | bytes 1572872 | tf_op jit(solution)/shard_map/ppermute | solution.py:532
  23.6 25.4 %copy-start.6 = (bf16[512,512]{1,0:T(8,128)(2,1)}, bf16[512,512]{1,0:T(8,128)(2,1)S(1)}, u32[]{:S(2)}) copy-start(bf16[512,512]{1,0:T(8,128)(2,1)S(1)} %collective-permute-done.10.refs_7_) | copy-start | bytes 1572868
  23.7 25.4 %copy-start.5 = (bf16[512,512]{1,0:T(8,128)(2,1)}, bf16[512,512]{1,0:T(8,128)(2,1)S(1)}, u32[]{:S(2)}) copy-start(bf16[512,512]{1,0:T(8,128)(2,1)S(1)} %collective-permute-done.6.refs_9_) | copy-start | bytes 1572868
  24.5 13.9 %collective-permute-start.11 = (bf16[16,512]{1,0:T(8,128)(2,1)S(1)}, bf16[16,512]{1,0:T(8,128)(2,1)S(1)}, u32[]{:S(2)}, u32[]{:S(2)}) collective-permute-start(bf16[16,512]{1,0:T(8,128)(2,1)S(1)} %fusion), channel_id=1, source_target_pairs={{0,16},{2,18},{4,20},{6,22},{8,24},{10,26},{12,28},{14,30},{16,0},... | collective-permute-start | bytes 49160 | tf_op jit(solution)/shard_map/ppermute | solution.py:532
  25.1 28.9 %collective-permute-start.7 = (bf16[512,512]{1,0:T(8,128)(2,1)S(1)}, bf16[512,512]{1,0:T(8,128)(2,1)S(1)}, u32[]{:S(2)}, u32[]{:S(2)}) collective-permute-start(bf16[512,512]{1,0:T(8,128)(2,1)S(1)} %collective-permute-done.refs_5_), channel_id=1, source_target_pairs={{0,2},{2,0},{4,6},{6,4},{8,10},{10,8},{12,14},{14,12},{16,18},{18,... | collective-permute-start | bytes 1572872 | tf_op jit(solution)/shard_map/ppermute | solution.py:532
  25.1 24.0 %collective-permute-start.2 = (bf16[512,512]{1,0:T(8,128)(2,1)S(1)}, bf16[512,512]{1,0:T(8,128)(2,1)}, u32[]{:S(2)}, u32[]{:S(2)}) collective-permute-start(bf16[512,512]{1,0:T(8,128)(2,1)S(1)} %collective-permute-done.refs_5_), channel_id=1, source_target_pairs={{0,4},{2,6},{4,0},{6,2},{8,12},{10,14},{12,8},{14,10},{16,20},{18,... | collective-permute-start | bytes 1572872 | tf_op jit(solution)/shard_map/ppermute | solution.py:532
  37.7 16.8 %collective-permute-start.8 = (bf16[512,256]{1,0:T(8,128)(2,1)S(1)}, bf16[512,256]{1,0:T(8,128)(2,1)}, u32[]{:S(2)}, u32[]{:S(2)}) collective-permute-start(bf16[512,256]{1,0:T(8,128)(2,1)S(1)} %slice.24), channel_id=1, source_target_pairs={{0,4},{2,6},{4,0},{6,2},{8,12},{10,14},{12,8},{14,10},{16,20},{18,... | collective-permute-start | bytes 786440 | tf_op jit(solution)/shard_map/ppermute | solution.py:532
  38.4 10.7 %copy-start.3 = (bf16[16,512]{1,0:T(8,128)(2,1)}, bf16[16,512]{1,0:T(8,128)(2,1)S(1)}, u32[]{:S(2)}) copy-start(bf16[16,512]{1,0:T(8,128)(2,1)S(1)} %broadcast_select_fusion.refs_13_) | copy-start | bytes 49156
  38.4 15.6 %collective-permute-start.12 = (bf16[16,512]{1,0:T(8,128)(2,1)S(1)}, bf16[16,512]{1,0:T(8,128)(2,1)S(1)}, u32[]{:S(2)}, u32[]{:S(2)}) collective-permute-start(bf16[16,512]{1,0:T(8,128)(2,1)S(1)} %broadcast_select_fusion.refs_13_), channel_id=1, source_target_pairs={{0,8},{2,10},{4,12},{6,14},{8,16},{10,18},{12,20},{14,22},{16,24},... | collective-permute-start | bytes 49160 | tf_op jit(solution)/shard_map/ppermute | solution.py:532
  50.8 17.5 %collective-permute-start.13 = (bf16[512,256]{1,0:T(8,128)(2,1)}, bf16[512,256]{1,0:T(8,128)(2,1)}, u32[]{:S(2)}, u32[]{:S(2)}) collective-permute-start(bf16[512,256]{1,0:T(8,128)(2,1)} %slice.28), channel_id=1, source_target_pairs={{0,8},{2,10},{4,12},{6,14},{8,16},{10,18},{12,20},{14,22},{16,24},... | collective-permute-start | bytes 786440 | tf_op jit(solution)/shard_map/ppermute | solution.py:532
  54.0 0.9 copy-start.8
  54.0 15.0 %collective-permute-start.3 = (bf16[512,512]{1,0:T(8,128)(2,1)}, bf16[512,512]{1,0:T(8,128)(2,1)}, u32[]{:S(2)}, u32[]{:S(2)}) collective-permute-start(bf16[512,512]{1,0:T(8,128)(2,1)} %collective-permute-done.2.refs_5_), channel_id=1, source_target_pairs={{0,2},{2,0},{4,6},{6,4},{8,10},{10,8},{12,14},{14,12},{16,18},{18,... | collective-permute-start | bytes 1572872 | tf_op jit(solution)/shard_map/ppermute | solution.py:532
  54.0 14.2 %copy-start.9 = (bf16[16,512]{1,0:T(8,128)(2,1)}, bf16[16,512]{1,0:T(8,128)(2,1)S(1)}, u32[]{:S(2)}) copy-start(bf16[16,512]{1,0:T(8,128)(2,1)S(1)} %collective-permute-done.12.refs_14_) | copy-start | bytes 49156
  54.0 15.0 %collective-permute-start.4 = (bf16[512,512]{1,0:T(8,128)(2,1)}, bf16[512,512]{1,0:T(8,128)(2,1)}, u32[]{:S(2)}, u32[]{:S(2)}) collective-permute-start(bf16[512,512]{1,0:T(8,128)(2,1)} %collective-permute-done.1.refs_4_), channel_id=1, source_target_pairs={{0,2},{2,0},{4,6},{6,4},{8,10},{10,8},{12,14},{14,12},{16,18},{18,... | collective-permute-start | bytes 1572872 | tf_op jit(solution)/shard_map/ppermute | solution.py:532
  54.9 14.2 %collective-permute-start.9 = (bf16[512,256]{1,0:T(8,128)(2,1)}, bf16[512,256]{1,0:T(8,128)(2,1)}, u32[]{:S(2)}, u32[]{:S(2)}) collective-permute-start(bf16[512,256]{1,0:T(8,128)(2,1)} %collective-permute-done.8.refs_11_), channel_id=1, source_target_pairs={{0,2},{2,0},{4,6},{6,4},{8,10},{10,8},{12,14},{14,12},{16,18},{18,... | collective-permute-start | bytes 786440 | tf_op jit(solution)/shard_map/ppermute | solution.py:532
  54.9 38.4 %collective-permute-start.17 = (bf16[1024,1024]{1,0:T(8,128)(2,1)}, bf16[1024,1024]{1,0:T(8,128)(2,1)}, u32[]{:S(2)}, u32[]{:S(2)}) collective-permute-start(bf16[1024,1024]{1,0:T(8,128)(2,1)} %collective-permute-done.16.wa_ref), channel_id=1, source_target_pairs={{0,2},{2,0},{4,6},{6,4},{8,10},{10,8},{12,14},{14,12},{16,18},{18,... | collective-permute-start | bytes 6291464 | tf_op jit(solution)/shard_map/ppermute | solution.py:532
  68.2 10.8 %collective-permute-start.14 = (bf16[512,256]{1,0:T(8,128)(2,1)}, bf16[512,256]{1,0:T(8,128)(2,1)}, u32[]{:S(2)}, u32[]{:S(2)}) collective-permute-start(bf16[512,256]{1,0:T(8,128)(2,1)} %collective-permute-done.13.refs_11_), channel_id=1, source_target_pairs={{0,2},{2,0},{4,6},{6,4},{8,10},{10,8},{12,14},{14,12},{16,18},{18,... | collective-permute-start | bytes 786440 | tf_op jit(solution)/shard_map/ppermute | solution.py:532
  79.0 14.3 %collective-permute-start.15 = (bf16[512,512]{1,0:T(8,128)(2,1)}, bf16[512,512]{1,0:T(8,128)(2,1)}, u32[]{:S(2)}, u32[]{:S(2)}) collective-permute-start(bf16[512,512]{1,0:T(8,128)(2,1)} %attend.4.own0), channel_id=1, source_target_pairs={{0,1},{1,0},{2,3},{3,2},{4,5},{5,4},{6,7},{7,6},{8,9},{9,8},{10,11... | collective-permute-start | bytes 1572872 | tf_op jit(solution)/shard_map/ppermute | solution.py:532
  89.0 16.2 %collective-permute-start.18 = (bf16[512,512]{1,0:T(8,128)(2,1)}, bf16[512,512]{1,0:T(8,128)(2,1)S(1)}, u32[]{:S(2)}, u32[]{:S(2)}) collective-permute-start(bf16[512,512]{1,0:T(8,128)(2,1)} %attend.5.own1), channel_id=1, source_target_pairs={{0,1},{1,0},{2,3},{3,2},{4,5},{5,4},{6,7},{7,6},{8,9},{9,8},{10,11... | collective-permute-start | bytes 1572872 | tf_op jit(solution)/shard_map/ppermute | solution.py:532
  93.3 2.2 %copy-start = (bf16[512,4096]{1,0:T(8,128)(2,1)S(1)}, bf16[512,4096]{1,0:T(8,128)(2,1)}, u32[]{:S(2)}) copy-start(bf16[512,4096]{1,0:T(8,128)(2,1)} %tok_ref.5) | copy-start | bytes 12582916
  95.5 1.0 copy-start.1
  96.5 1.0 copy-start.2

commit v5 on v4

--- a/solution.py
+++ b/solution.py
@@ -23,6 +23,7 @@
 ALL_VMEM = 67043328 - 128 * 1024
 ANY = pl.BlockSpec(memory_space=pltpu.HBM)
 SMEM = pl.BlockSpec(memory_space=pltpu.SMEM)
+VMEM = pl.BlockSpec(memory_space=pltpu.VMEM)
 
 
 def keys_values_kernel(place, tok_ref, gain_ref, wk_ref, wv_ref, w_hbm, *refs):
@@ -154,6 +155,10 @@
     )(tokens, gain, w_query, scale)
 
 
+def stay(*arrays):
+    return [pltpu.with_memory_space_constraint(a, pltpu.HBM) for a in arrays]
+
+
 def early_blocks(me):
     twin, core = me ^ 1, me % 2
     return [me, me - 4, jnp.where(core == 0, twin - 4, -1), jnp.where(core == 1, twin, -1)]
@@ -175,7 +180,7 @@
     ]
 
 
-def attend_kernel(groups, per_group, sources, start, *refs):
+def attend_kernel(groups, per_group, base_head, sources, start, extra, *refs):
     window, sinks, bias, q_hbm = refs[:4]
     sent = 1 + max(ref for slot in sources for ref, _ in slot)
     kv_refs, refs = refs[4 : 4 + sent], refs[4 + sent :]
@@ -183,14 +188,16 @@
         acc_hbm, packed_hbm = refs[:2]
         refs = refs[2:]
     else:
-        sink_old, sink_new, acc_hbm, packed_hbm, out_hbm, sink_ref, out_ref = refs[:5] + refs[-2:]
-        refs = refs[5:-2]
+        sink_old, sink_new, acc_hbm, packed_hbm = refs[:4]
+        sources_ahead, out_hbm = refs[4 : 4 + extra], refs[4 + extra]
+        targets_ahead, refs = refs[5 + extra : 5 + 2 * extra], refs[5 + 2 * extra :]
+        sink_ref, out_ref = refs[-2:]
+        refs = refs[:-2]
     q_ref, kvbuf, sems, items, s_even, s_odd, x_even, x_odd, m_ref, acc_ref, packed_ref = refs
     bufs = ((s_even, x_even), (s_odd, x_odd))
     rows, key_rows = q_ref.shape[0], kvbuf.shape[1]
     share, buffers = len(groups), kvbuf.shape[0]
     heads = share * per_group
-    base_head = groups[0] * per_group
     all_heads = acc_hbm.shape[0]
     lanes = key_rows // HEAD_DIM
     own = lax.axis_index("seq")
@@ -226,6 +233,13 @@
             pl.when(need)(copy.start)
     for copy in copies:
         copy.start()
+    ahead = []
+    if not start and extra:
+        for i, (source, target) in enumerate(zip(sources_ahead, targets_ahead)):
+            width = target.shape[1]
+            columns = pl.ds(pl.multiple_of(lax.axis_index("head") * width, width), width)
+            ahead.append(pltpu.make_async_copy(source.at[:, columns], target, sems.at[buffers + 5 + i]))
+            ahead[-1].start()
     kvbuf[:, :, PAIR:] = jnp.ones((buffers, key_rows, HEAD_DIM), jnp.bfloat16)
     if start:
         m_ref[...] = jnp.full(m_ref.shape, LOW, jnp.float32)
@@ -393,12 +407,13 @@
 
     for head in range(heads):
         give(head).wait()
-
-
-def attend(groups, all_groups, scalars, queries, arrays, sources, sinks=None, state=None):
+    for copy in ahead:
+        copy.wait()
+
+
+def attend(groups, per_group, base_head, scalars, queries, arrays, sources, sinks=None, state=None, ahead=(), share=0):
     rows = queries.shape[0]
     key_rows = arrays[0].shape[0]
-    per_group = queries.shape[1] // HEAD_DIM // all_groups
     heads = per_group * len(groups)
     buffers = len(sources) * len(groups)
     items = heads * len(sources) + 2 * UNROLL
@@ -406,7 +421,7 @@
     scratch = [
         pltpu.VMEM((rows, heads * HEAD_DIM), jnp.bfloat16),
         pltpu.VMEM((buffers, key_rows, 3 * HEAD_DIM), jnp.bfloat16),
-        pltpu.SemaphoreType.DMA((buffers + 5,)),
+        pltpu.SemaphoreType.DMA((buffers + 5 + len(ahead),)),
         pltpu.SMEM((3, items), jnp.int32),
         pltpu.VMEM((rows, key_rows), f32),
         pltpu.VMEM((rows, key_rows), f32),
@@ -417,7 +432,7 @@
         pltpu.VMEM((rows, HEAD_DIM), f32),
     ]
     in_specs = [SMEM] * 3 + [ANY] * (1 + len(arrays))
-    operands = [*scalars, queries, *arrays]
+    operands = [*scalars, *stay(queries, *arrays)]
     if state is None:
         out_specs = [ANY, ANY]
         out_shape = [
@@ -425,21 +440,22 @@
             jax.ShapeDtypeStruct((rows, HEAD_DIM), f32),
         ]
     else:
-        in_specs += [ANY] * 4
-        operands += [*sinks, *state]
-        out_specs = ANY
-        out_shape = jax.ShapeDtypeStruct((rows, heads * HEAD_DIM), jnp.bfloat16)
+        in_specs += [ANY] * (4 + len(ahead))
+        operands += stay(*sinks, *state, *ahead)
+        out_specs = [ANY] + [VMEM] * len(ahead)
+        out_shape = [jax.ShapeDtypeStruct((rows, heads * HEAD_DIM), jnp.bfloat16)]
+        out_shape += [jax.ShapeDtypeStruct((a.shape[0], share), a.dtype) for a in ahead]
         scratch += [
             pltpu.VMEM((2, *sinks[0].shape), jnp.bfloat16),
             pltpu.VMEM((rows, heads * HEAD_DIM), jnp.bfloat16),
         ]
     return pl.pallas_call(
-        functools.partial(attend_kernel, groups, per_group, sources, state is None),
+        functools.partial(attend_kernel, groups, per_group, base_head, sources, state is None, len(ahead)),
         in_specs=in_specs,
         out_specs=out_specs,
         out_shape=out_shape,
         scratch_shapes=scratch,
-        compiler_params=pltpu.CompilerParams(vmem_limit_bytes=ALL_VMEM),
+        compiler_params=pltpu.CompilerParams(vmem_limit_bytes=40 * MIB if ahead else ALL_VMEM),
         cost_estimate=pl.CostEstimate(
             flops=8 * rows * buffers * key_rows * per_group * HEAD_DIM,
             bytes_accessed=2 * buffers * key_rows * PAIR,
@@ -449,71 +465,114 @@
     )(*operands)
 
 
-def project_kernel(where, tok_ref, own0, own1, far_ref, w_ref, wa_ref, wb_ref, out_ref):
-    half = own0.shape[1]
-    total = jnp.dot(own0[...], w_ref[:half, :], preferred_element_type=jnp.float32)
-    total += jnp.dot(own1[...], w_ref[half:, :], preferred_element_type=jnp.float32)
-    total += tok_ref[...].astype(jnp.float32)
-    far_dot(far_ref, wa_ref, wb_ref, out_ref, total)
-
-
-def project_last_kernel(where, part_ref, far_ref, wa_ref, wb_ref, out_ref):
-    far_dot(far_ref, wa_ref, wb_ref, out_ref, part_ref[...])
-
-
-def far_dot(far_ref, wa_ref, wb_ref, out_ref, total):
-    step, turn = pl.program_id(0), pl.num_programs(0) // 2
-
-    @pl.when(step < turn)
-    def _():
-        more = jnp.dot(far_ref[...], wa_ref[...], preferred_element_type=jnp.float32)
-        out_ref[...] = (total + more).astype(out_ref.dtype)
-
-    @pl.when(step >= turn)
-    def _():
-        more = jnp.dot(far_ref[...], wb_ref[...], preferred_element_type=jnp.float32)
-        out_ref[...] = (total + more).astype(out_ref.dtype)
-
-
-def project(where, rows, share, row, own_side, far, w_near, w_swap):
-    depth, _ = w_near.shape
-    tile = 512
-    steps = share // tile
-    part = steps // 2
-    half = far.shape[1]
-
-    def column(j, where):
-        return jnp.where(where[1] == 0, j, lax.rem(j + part, steps))
-
-    here = pl.BlockSpec((rows, tile), lambda j, where: (0, column(j, where)))
-    shifted = lambda height: pl.BlockSpec((height, tile), lambda j, where: (0, where[0] * steps + column(j, where)))
-    fixed = lambda a: pl.BlockSpec(a.shape, lambda j, where: (0, 0))
-    far_specs = [
-        fixed(far),
-        pl.BlockSpec((half, tile), lambda j, where: (row, jnp.minimum(j, part - 1))),
-        pl.BlockSpec((half, tile), lambda j, where: (row, jnp.maximum(j - part, 0))),
+TILE = 512
+
+
+def wide_copies(w_near, w_swap, row, w_buf, sems):
+    piece, depth = w_near.shape[1], w_buf.shape[0]
+    core = lax.axis_index("seq") % 2
+    places = [pl.multiple_of(core * piece, piece), pl.multiple_of((1 - core) * piece, piece)]
+    return [
+        pltpu.make_async_copy(
+            w.at[pl.ds(row, depth), :], w_buf.at[:, pl.ds(place, piece)], sems.at[i]
+        )
+        for i, (w, place) in enumerate(zip((w_near, w_swap), places))
     ]
-    if len(own_side) > 1:
-        tokens, own0, own1, w_out = own_side
-        kernel, dtype = project_kernel, jnp.float32
-        specs = [shifted(rows), fixed(own0), fixed(own1), far_specs[0], shifted(w_out.shape[0]), *far_specs[1:]]
-        operands = [tokens, own0, own1, far, w_out, w_near, w_swap]
-    else:
-        kernel, dtype = project_last_kernel, jnp.bfloat16
-        specs = [here, *far_specs]
-        operands = [own_side[0], far, w_near, w_swap]
+
+
+def project_kernel(counts, tok, w_own, *refs):
+    own, refs = refs[: counts[0]], refs[counts[0] :]
+    far, refs = refs[: counts[1]], refs[counts[1] :]
+    w_near, w_swap, part, w_last, lhs, far_buf, w_far, sems, near_sems, last_sems = refs
+    tiles = part.shape[1] // TILE
+    loads, at = [], 0
+    for i, ref in enumerate(own):
+        loads.append(pltpu.make_async_copy(ref, lhs.at[:, pl.ds(at, ref.shape[1])], sems.at[i]))
+        at += ref.shape[1]
+    late, at = [], 0
+    for i, ref in enumerate(far):
+        late.append(
+            pltpu.make_async_copy(ref, far_buf.at[:, pl.ds(at, ref.shape[1])], sems.at[len(own) + i])
+        )
+        at += ref.shape[1]
+    late += wide_copies(w_near, w_swap, 0, w_far, near_sems)
+    last = wide_copies(w_near, w_swap, at, w_last, last_sems)
+    for copy in loads + late + last:
+        copy.start()
+    for copy in loads:
+        copy.wait()
+    for t in range(tiles):
+        here = slice(t * TILE, (t + 1) * TILE)
+        total = jnp.dot(lhs[...], w_own[:, here], preferred_element_type=jnp.float32)
+        part[:, here] = tok[:, here].astype(jnp.float32) + total
+    for copy in late:
+        copy.wait()
+    for t in range(tiles):
+        here = slice(t * TILE, (t + 1) * TILE)
+        part[:, here] += jnp.dot(far_buf[...], w_far[:, here], preferred_element_type=jnp.float32)
+    for copy in last:
+        copy.wait()
+
+
+def project_last_kernel(part, far, w_last, out, out_buf, sems):
+    stores = []
+    for t in range(out.shape[1] // TILE):
+        here = slice(t * TILE, (t + 1) * TILE)
+        more = jnp.dot(far[...], w_last[:, here], preferred_element_type=jnp.float32)
+        out_buf[:, here] = (part[:, here] + more).astype(jnp.bfloat16)
+        at = pl.ds(t * TILE, TILE)
+        stores.append(pltpu.make_async_copy(out_buf.at[:, at], out.at[:, at], sems.at[t]))
+        stores[-1].start()
+    for store in stores:
+        store.wait()
+
+
+def project(tokens, w_own, own, far, w_near, w_swap):
+    rows, share = tokens.shape
+    depth = w_own.shape[0]
+    known = sum(x.shape[1] for x in far)
+    bf16 = jnp.bfloat16
     return pl.pallas_call(
-        kernel,
-        grid_spec=pltpu.PrefetchScalarGridSpec(
-            num_scalar_prefetch=1, grid=(steps,), in_specs=specs, out_specs=here
-        ),
-        out_shape=jax.ShapeDtypeStruct((rows, share), dtype),
+        functools.partial(project_kernel, (len(own), len(far))),
+        in_specs=[VMEM] * 2 + [ANY] * (2 + len(own) + len(far)),
+        out_specs=[VMEM, VMEM],
+        out_shape=[
+            jax.ShapeDtypeStruct((rows, share), jnp.float32),
+            jax.ShapeDtypeStruct((w_near.shape[0] - known, share), bf16),
+        ],
+        scratch_shapes=[
+            pltpu.VMEM((rows, depth), bf16),
+            pltpu.VMEM((rows, known), bf16),
+            pltpu.VMEM((known, share), bf16),
+            pltpu.SemaphoreType.DMA((len(own) + len(far),)),
+            pltpu.SemaphoreType.DMA((2,)),
+            pltpu.SemaphoreType.DMA((2,)),
+        ],
         compiler_params=pltpu.CompilerParams(vmem_limit_bytes=40 * MIB),
         cost_estimate=pl.CostEstimate(
-            flops=len(operands) * rows * half * share, bytes_accessed=4 * depth * share, transcendentals=0
+            flops=2 * rows * (depth + known) * share, bytes_accessed=2 * known * share, transcendentals=0
         ),
         name="project",
-    )(where, *operands)
+    )(tokens, w_own, *stay(*own, *far, w_near, w_swap))
+
+
+def project_last(partial, far, w_last):
+    rows, share = partial.shape
+    return pl.pallas_call(
+        project_last_kernel,
+        in_specs=[VMEM] * 3,
+        out_specs=ANY,
+        out_shape=jax.ShapeDtypeStruct((rows, share), jnp.bfloat16),
+        scratch_shapes=[
+            pltpu.VMEM((rows, share), jnp.bfloat16),
+            pltpu.SemaphoreType.DMA((share // TILE,)),
+        ],
+        compiler_params=pltpu.CompilerParams(vmem_limit_bytes=24 * MIB),
+        cost_estimate=pl.CostEstimate(
+            flops=2 * rows * far.shape[1] * share, bytes_accessed=2 * rows * share, transcendentals=0
+        ),
+        name="project_last",
+    )(partial, far, w_last)
 
 
 def local(tokens, norm_gain, w_query, w_key, w_value, w_out, window, sink_count, sink_bias):
@@ -573,32 +632,39 @@
     w_swap = send(w_near, core_swap)
 
     every = tuple(range(groups))
+    per_group = queries.shape[1] // HEAD_DIM // groups
     state = attend(
         every,
-        groups,
+        per_group,
+        0,
         scalars,
         queries,
         [kv, back4, core4, near_core],
         [[(a, g * PAIR) for g in every] for a in range(4)],
     )
+    chunks = [(g, g * per_group, per_group) for g in every[:-1]]
+    g, half = every[-1], per_group // 2
+    chunks += [(g, g * per_group, half), (g, g * per_group + half, half)]
     own, other = [], []
-    for g in every:
+    for c, (g, base_head, count) in enumerate(chunks):
         att = attend(
             (g,),
-            groups,
+            count,
+            base_head,
             scalars,
             queries,
             [back8, across4, cross4, core8, near_side, cross_near, core4, far[g], cross_far[g]],
             [[(a, g * PAIR)] for a in range(7)] + [[(7, 0)], [(8, 0)]],
             sinks,
             state,
+            (tokens, w_out) if c == len(chunks) - 1 else (),
+            share,
         )
+        att, early = att[0], att[1:]
         own.append(att)
         other.append(send(att, head_swap, "head"))
-    where = jnp.stack([my_head, core]).astype(jnp.int32)
-    rows = tokens.shape[0]
-    partial = project(where, rows, share, 0, (tokens, *own, w_out), other[0], w_near, w_swap)
-    return project(where, rows, share, 1, (partial,), other[1], w_near, w_swap)
+    partial, w_last = project(*early, own, other[:-1], w_near, w_swap)
+    return project_last(partial, other[-1], w_last)
 
 
 def solution(mesh):

time: 111 us -> 108 us (0.973)
  local copies, waits for them, and re-layouts: 7.29 us -> 4.1 us
  Pallas kernels: 61.9 us -> 59 us
  waiting for transfers between devices: 22.5 us -> 24.6 us
    unnamed x20 -> x22, local copies, waits for them, and re-layouts: 4.66 us -> 1.46 us
    pallas_call x5 -> x6, Pallas kernels: 45.8 us -> 42.9 us  [the longest x4 35.8 us: attend(): pl.pallas_call(functools.partial(attend_kernel, groups, per_group, base_h...]
    ppermute x19 -> x20, waiting for transfers between devices: 22.5 us -> 24.6 us  [send(): return lax.ppermute(x, axis, pairs)]
    ppermute x19 -> x20, starting transfers between devices: 18.1 us -> 18.7 us  [send(): return lax.ppermute(x, axis, pairs)]
  transfers between devices with their start and end apart: 19 -> 20, of which waited for: 5 -> 5; matrix products, arithmetic and copies ran while one was open for 3% -> 3% of each run, Pallas kernels for 45% -> 47%
where the time goes in v5:
time: 108 us; the launch traced here: 107 us
  Pallas kernels  59 us (55%)
  waiting for transfers between devices  24.6 us (23%)
  starting transfers between devices  18.7 us (17%)
  local copies, waits for them, and re-layouts  4.1 us (4%)
    pallas_call x4, Pallas kernels, attend(): pl.pallas_call(functools.partial(attend_kernel, groups, per_group, base_h...  35.8 us
    ppermute x20, waiting for transfers between devices, send(): return lax.ppermute(x, axis, pairs)  24.6 us
    ppermute x20, starting transfers between devices, send(): return lax.ppermute(x, axis, pairs)  18.7 us
    pallas_call x1, Pallas kernels, project_queries(): pl.pallas_call(query_kernel, grid=(width // chunk,), in_specs=[pl.BlockSp...  9.46 us
    pallas_call x1, Pallas kernels, keys_values(): pl.pallas_call(keys_values_kernel, grid_spec=pltpu.PrefetchScalarGridSpec...  6.64 us
    pallas_call x1, Pallas kernels, project(): pl.pallas_call(functools.partial(project_kernel, (len(own), len(far))), i...  5.41 us
    slice x2, local copies, waits for them, and re-layouts, local(): part = (back8 if g % 2 == 0 else across4)[:, at]  2.64 us
  transfers between devices with their start and end apart: 20, of which 5 were waited for; matrix products, arithmetic and copies ran while one was open for 3% of the time, Pallas kernels for 47%

profile of v5, /device:TPU:18, one launch (start us, length us, event | category | flops | bytes accessed | tf_op | source)
XLA Modules:
  0.0 107.5 jit_solution(14209992546065538657)
XLA Ops:
  0.0 6.6 %keys_values.1 = (bf16[512,512]{1,0:T(8,128)(2,1)}, f32[512,128]{1,0:T(8,128)}, bf16[1024,1024]{1,0:T(8,128)(2,1)}) custom-call(s32[1]{0:T(128)} %bitcast.1.place, bf16[512,4096]{1,0:T(8,128)(2,1)} %refs_17_.1, f32[1,4096]{1,0:T(1,128)} %bitcast.2, bf16[4096,256]{1,0:T(8,128)(2,1)} %wk_ref.1, bf16[4096,256]{1,0:T(8,128)(2,1)} %wv_ref.1, ...), custom_call_target="tpu_custom_call" | custom-call | flops 2147483648 | bytes 8388608 | tf_op jit(solution)/shard_map/keys_values/pallas_call | solution.py:78
  6.6 1.6 %collective-permute-start.17 = (bf16[1024,1024]{1,0:T(8,128)(2,1)}, bf16[1024,1024]{1,0:T(8,128)(2,1)}, u32[]{:S(2)}, u32[]{:S(2)}) collective-permute-start(bf16[1024,1024]{1,0:T(8,128)(2,1)} %get-tuple-element.22), channel_id=1, source_target_pairs={{0,1},{1,0},{2,3},{3,2},{4,5},{5,4},{6,7},{7,6},{8,9},{9,8},{10,11... | collective-permute-start | bytes 6291464 | tf_op jit(solution)/shard_map/ppermute | solution.py:591
  8.2 0.5 collective-permute-start.5
  8.8 1.6 %collective-permute-start = (bf16[512,512]{1,0:T(8,128)(2,1)}, bf16[512,512]{1,0:T(8,128)(2,1)S(1)}, u32[]{:S(2)}, u32[]{:S(2)}) collective-permute-start(bf16[512,512]{1,0:T(8,128)(2,1)} %get-tuple-element.16.refs_4_), channel_id=1, source_target_pairs={{0,8},{2,10},{4,12},{6,14},{8,16},{10,18},{12,20},{14,22},{16,24},... | collective-permute-start | bytes 1572872 | tf_op jit(solution)/shard_map/ppermute | solution.py:591
  10.3 0.0 collective-permute-start.10
  10.3 11.5 %collective-permute-done.5.refs_8_ = bf16[512,512]{1,0:T(8,128)(2,1)S(1)} collective-permute-done((bf16[512,512]{1,0:T(8,128)(2,1)}, bf16[512,512]{1,0:T(8,128)(2,1)S(1)}, u32[]{:S(2)}, u32[]{:S(2)}) %collective-permute-start.5) | collective-permute-done | bytes 524320 | tf_op jit(solution)/shard_map/ppermute | solution.py:591
  21.8 0.0 collective-permute-start.6
  21.8 0.2 collective-permute-done.refs_5_
  22.1 1.6 %collective-permute-start.1 = (bf16[512,512]{1,0:T(8,128)(2,1)S(1)}, bf16[512,512]{1,0:T(8,128)(2,1)}, u32[]{:S(2)}, u32[]{:S(2)}) collective-permute-start(bf16[512,512]{1,0:T(8,128)(2,1)S(1)} %collective-permute-done.refs_5_), channel_id=1, source_target_pairs={{0,8},{2,10},{4,12},{6,14},{8,16},{10,18},{12,20},{14,22},{16,24},... | collective-permute-start | bytes 1572872 | tf_op jit(solution)/shard_map/ppermute | solution.py:591
  23.7 0.0 collective-permute-done.10.refs_7_
  23.7 0.1 collective-permute-done.6.refs_9_
  23.7 0.7 copy-done.8
  24.5 0.7 fusion
  25.2 0.7 collective-permute-start.11
  25.9 1.5 %collective-permute-start.2 = (bf16[512,512]{1,0:T(8,128)(2,1)S(1)}, bf16[512,512]{1,0:T(8,128)(2,1)}, u32[]{:S(2)}, u32[]{:S(2)}) collective-permute-start(bf16[512,512]{1,0:T(8,128)(2,1)S(1)} %collective-permute-done.refs_5_), channel_id=1, source_target_pairs={{0,4},{2,6},{4,0},{6,2},{8,12},{10,14},{12,8},{14,10},{16,20},{18,... | collective-permute-start | bytes 1572872 | tf_op jit(solution)/shard_map/ppermute | solution.py:591
  27.4 0.0 collective-permute-start.7
  27.4 9.4 %collective-permute-done.1.refs_4_ = bf16[512,512]{1,0:T(8,128)(2,1)} collective-permute-done((bf16[512,512]{1,0:T(8,128)(2,1)S(1)}, bf16[512,512]{1,0:T(8,128)(2,1)}, u32[]{:S(2)}, u32[]{:S(2)}) %collective-permute-start.1) | collective-permute-done | bytes 524320 | tf_op jit(solution)/shard_map/ppermute | solution.py:591
  36.8 1.0 slice.28
  37.8 0.6 collective-permute-start.13
  38.4 0.0 collective-permute-done.11
  38.4 1.3 %collective-permute-start.12 = (bf16[16,512]{1,0:T(8,128)(2,1)S(1)}, bf16[16,512]{1,0:T(8,128)(2,1)S(1)}, u32[]{:S(2)}, u32[]{:S(2)}) collective-permute-start(bf16[16,512]{1,0:T(8,128)(2,1)S(1)} %broadcast_select_fusion.refs_13_), channel_id=1, source_target_pairs={{0,8},{2,10},{4,12},{6,14},{8,16},{10,18},{12,20},{14,22},{16,24},... | collective-permute-start | bytes 49160 | tf_op jit(solution)/shard_map/ppermute | solution.py:591
  39.7 9.5 %queries.1.refs_3_ = bf16[512,1024]{1,0:T(8,128)(2,1)} custom-call(bf16[512,4096]{1,0:T(8,128)(2,1)} %refs_17_.1, f32[1,4096]{1,0:T(1,128)} %bitcast.3, bf16[4096,1024]{1,0:T(8,128)(2,1)} %w_ref.1, f32[512,128]{1,0:T(8,128)} %get-tuple-element.15.scale_ref), custom_call_target="tpu_custom_call" | custom-call | flops 4294967296 | bytes 12582912 | tf_op jit(solution)/shard_map/queries/pallas_call | solution.py:138
  49.1 0.0 collective-permute-done.2.refs_5_
  49.2 1.7 %slice.24 = bf16[512,256]{1,0:T(8,128)(2,1)} slice(bf16[512,512]{1,0:T(8,128)(2,1)} %collective-permute-done.2.refs_5_), slice={[0:512], [256:512]} | slice | bytes 524288 | tf_op jit(solution)/shard_map/slice | solution.py:617
  50.8 3.2 %collective-permute-start.8 = (bf16[512,256]{1,0:T(8,128)(2,1)}, bf16[512,256]{1,0:T(8,128)(2,1)}, u32[]{:S(2)}, u32[]{:S(2)}) collective-permute-start(bf16[512,256]{1,0:T(8,128)(2,1)} %slice.24), channel_id=1, source_target_pairs={{0,8},{2,10},{4,12},{6,14},{8,16},{10,18},{12,20},{14,22},{16,24},... | collective-permute-start | bytes 786440 | tf_op jit(solution)/shard_map/ppermute | solution.py:591
  54.1 0.0 collective-permute-done.7.refs_6_.refs_10_
  54.1 0.0 collective-permute-start.3
  54.1 0.5 collective-permute-start.4
  54.6 0.0 collective-permute-done.13.refs_11_
  54.6 0.1 collective-permute-start.14
  54.7 0.0 collective-permute-done.17.refs_5_
  54.7 0.4 collective-permute-start.18
  55.1 12.8 %attend.4 = (f32[8,512,128]{2,1,0:T(8,128)}, f32[512,128]{1,0:T(8,128)}) custom-call(s32[8]{0:T(128)} %refs_0_.7, s32[8]{0:T(128)} %refs_1_.7, f32[8]{0:T(128)} %refs_2_.7, bf16[512,1024]{1,0:T(8,128)(2,1)} %queries.1.refs_3_, bf16[512,512]{1,0:T(8,128)(2,1)} %get-tuple-element.16.refs_4_, bf16[512,512]{1,0:T(8,128)(2,1)} %copy-done.9, ...), custom_call_target="tpu_custom_call" | custom-call | flops 8589934592 | bytes 2097152 | tf_op jit(solution)/shard_map/attend/pallas_call | solution.py:452
  67.9 0.9 collective-permute-start.9
  68.8 10.0 %attend.6.refs_0_ = bf16[512,512]{1,0:T(8,128)(2,1)} custom-call(s32[8]{0:T(128)} %refs_0_.7, s32[8]{0:T(128)} %refs_1_.7, f32[8]{0:T(128)} %refs_2_.7, bf16[512,1024]{1,0:T(8,128)(2,1)} %queries.1.refs_3_, bf16[512,512]{1,0:T(8,128)(2,1)} %collective-permute-done.1.refs_4_, bf16[512,512]{1,0:T(8,128)(2,1)} %collective-permute-done.2.refs_5_, ...), custom_call_target="tpu_custom_call" | custom-call | flops 9663676416 | bytes 2359296 | tf_op jit(solution)/shard_map/attend/pallas_call | solution.py:452
  78.8 0.0 copy-start
  78.8 0.0 copy-start.1
  78.8 0.0 copy-start.2
  78.8 0.2 collective-permute-start.15
  79.1 8.3 %attend.7.refs_1_ = bf16[512,256]{1,0:T(8,128)(2,1)} custom-call(s32[8]{0:T(128)} %refs_0_.7, s32[8]{0:T(128)} %refs_1_.7, f32[8]{0:T(128)} %refs_2_.7, bf16[512,1024]{1,0:T(8,128)(2,1)} %queries.1.refs_3_, bf16[512,512]{1,0:T(8,128)(2,1)} %collective-permute-done.1.refs_4_, bf16[512,512]{1,0:T(8,128)(2,1)} %collective-permute-done.2.refs_5_, ...), custom_call_target="tpu_custom_call" | custom-call | flops 4831838208 | bytes 2359296 | tf_op jit(solution)/shard_map/attend/pallas_call | solution.py:452
  87.4 1.1 collective-permute-start.16
  88.5 4.8 %attend.5 = (bf16[512,256]{1,0:T(8,128)(2,1)S(1)}, bf16[512,2048]{1,0:T(8,128)(2,1)S(1)}, bf16[1024,2048]{1,0:T(8,128)(2,1)S(1)}) custom-call(s32[8]{0:T(128)S(1)} %copy-done, s32[8]{0:T(128)S(1)} %copy-done.1, f32[8]{0:T(128)S(1)} %copy-done.2, bf16[512,1024]{1,0:T(8,128)(2,1)} %queries.1.refs_3_, bf16[512,512]{1,0:T(8,128)(2,1)} %collective-permute-done.1.refs_4_, ...), custom_call_target="tpu_custom_call" | custom-call | flops 4831838208 | bytes 2359296 | tf_op jit(solution)/shard_map/attend/pallas_call | solution.py:452
  93.2 0.0 copy-start.3
  93.2 3.0 %collective-permute-start.19 = (bf16[512,256]{1,0:T(8,128)(2,1)S(1)}, bf16[512,256]{1,0:T(8,128)(2,1)S(1)}, u32[]{:S(2)}, u32[]{:S(2)}) collective-permute-start(bf16[512,256]{1,0:T(8,128)(2,1)S(1)} %get-tuple-element.21.refs_2_), channel_id=1, source_target_pairs={{0,1},{1,0},{2,3},{3,2},{4,5},{5,4},{6,7},{7,6},{8,9},{9,8},{10,11... | collective-permute-start | bytes 786440 | tf_op jit(solution)/shard_map/ppermute | solution.py:591
  96.2 3.3 %collective-permute-done.16.refs_4_ = bf16[512,256]{1,0:T(8,128)(2,1)S(1)} collective-permute-done((bf16[512,256]{1,0:T(8,128)(2,1)}, bf16[512,256]{1,0:T(8,128)(2,1)S(1)}, u32[]{:S(2)}, u32[]{:S(2)}) %collective-permute-start.16) | collective-permute-done | bytes 262176 | tf_op jit(solution)/shard_map/ppermute | solution.py:591
  99.6 0.7 copy-done.10
  100.2 5.4 %project.1 = (f32[512,2048]{1,0:T(8,128)S(1)}, bf16[256,2048]{1,0:T(8,128)(2,1)S(1)}) custom-call(bf16[512,2048]{1,0:T(8,128)(2,1)S(1)} %get-tuple-element.19.tok, bf16[1024,2048]{1,0:T(8,128)(2,1)S(1)} %get-tuple-element.20.w_own, bf16[512,512]{1,0:T(8,128)(2,1)} %attend.6.refs_0_, bf16[512,256]{1,0:T(8,128)(2,1)} %attend.7.refs_1_, ...), custom_call_target="tpu_custom_call" | custom-call | flops 3758096384 | bytes 3145728 | tf_op jit(solution)/shard_map/project/pallas_call | solution.py:535
  105.7 1.7 %project_last.1 = bf16[512,2048]{1,0:T(8,128)(2,1)} custom-call(f32[512,2048]{1,0:T(8,128)S(1)} %get-tuple-element.23.part, bf16[512,256]{1,0:T(8,128)(2,1)S(1)} %collective-permute-done.19.far, bf16[256,2048]{1,0:T(8,128)(2,1)S(1)} %get-tuple-element.24.w_last), custom_call_target="tpu_custom_call" | custom-call | flops 536870912 | bytes 2097152 | tf_op jit(solution)/shard_map/project_last/pallas_call | solution.py:561
  (26 shorter events, 0.1 us)
Async XLA Ops:
  6.6 48.0 %collective-permute-start.17 = (bf16[1024,1024]{1,0:T(8,128)(2,1)}, bf16[1024,1024]{1,0:T(8,128)(2,1)}, u32[]{:S(2)}, u32[]{:S(2)}) collective-permute-start(bf16[1024,1024]{1,0:T(8,128)(2,1)} %get-tuple-element.22), channel_id=1, source_target_pairs={{0,1},{1,0},{2,3},{3,2},{4,5},{5,4},{6,7},{7,6},{8,9},{9,8},{10,11... | collective-permute-start | bytes 6291464 | tf_op jit(solution)/shard_map/ppermute | solution.py:591
  8.2 13.6 %collective-permute-start.5 = (bf16[512,512]{1,0:T(8,128)(2,1)}, bf16[512,512]{1,0:T(8,128)(2,1)S(1)}, u32[]{:S(2)}, u32[]{:S(2)}) collective-permute-start(bf16[512,512]{1,0:T(8,128)(2,1)} %get-tuple-element.16.refs_4_), channel_id=1, source_target_pairs={{0,4},{2,6},{4,0},{6,2},{8,12},{10,14},{12,8},{14,10},{16,20},{18,... | collective-permute-start | bytes 1572872 | tf_op jit(solution)/shard_map/ppermute | solution.py:591
  8.8 13.3 %collective-permute-start = (bf16[512,512]{1,0:T(8,128)(2,1)}, bf16[512,512]{1,0:T(8,128)(2,1)S(1)}, u32[]{:S(2)}, u32[]{:S(2)}) collective-permute-start(bf16[512,512]{1,0:T(8,128)(2,1)} %get-tuple-element.16.refs_4_), channel_id=1, source_target_pairs={{0,8},{2,10},{4,12},{6,14},{8,16},{10,18},{12,20},{14,22},{16,24},... | collective-permute-start | bytes 1572872 | tf_op jit(solution)/shard_map/ppermute | solution.py:591
  10.3 13.3 %collective-permute-start.10 = (bf16[512,512]{1,0:T(8,128)(2,1)}, bf16[512,512]{1,0:T(8,128)(2,1)S(1)}, u32[]{:S(2)}, u32[]{:S(2)}) collective-permute-start(bf16[512,512]{1,0:T(8,128)(2,1)} %get-tuple-element.16.refs_4_), channel_id=1, source_target_pairs={{0,2},{2,0},{4,6},{6,4},{8,10},{10,8},{12,14},{14,12},{16,18},{18,... | collective-permute-start | bytes 1572872 | tf_op jit(solution)/shard_map/ppermute | solution.py:591
  21.8 27.3 %copy-start.4 = (bf16[512,512]{1,0:T(8,128)(2,1)}, bf16[512,512]{1,0:T(8,128)(2,1)S(1)}, u32[]{:S(2)}) copy-start(bf16[512,512]{1,0:T(8,128)(2,1)S(1)} %collective-permute-done.5.refs_8_) | copy-start | bytes 1572868
  21.8 1.9 %collective-permute-start.6 = (bf16[512,512]{1,0:T(8,128)(2,1)S(1)}, bf16[512,512]{1,0:T(8,128)(2,1)S(1)}, u32[]{:S(2)}, u32[]{:S(2)}) collective-permute-start(bf16[512,512]{1,0:T(8,128)(2,1)S(1)} %collective-permute-done.5.refs_8_), channel_id=1, source_target_pairs={{0,2},{2,0},{4,6},{6,4},{8,10},{10,8},{12,14},{14,12},{16,18},{18,... | collective-permute-start | bytes 1572872 | tf_op jit(solution)/shard_map/ppermute | solution.py:591
  22.1 27.1 %copy-start.9 = (bf16[512,512]{1,0:T(8,128)(2,1)}, bf16[512,512]{1,0:T(8,128)(2,1)S(1)}, u32[]{:S(2)}) copy-start(bf16[512,512]{1,0:T(8,128)(2,1)S(1)} %collective-permute-done.refs_5_) | copy-start | bytes 1572868
  22.1 14.7 %collective-permute-start.1 = (bf16[512,512]{1,0:T(8,128)(2,1)S(1)}, bf16[512,512]{1,0:T(8,128)(2,1)}, u32[]{:S(2)}, u32[]{:S(2)}) collective-permute-start(bf16[512,512]{1,0:T(8,128)(2,1)S(1)} %collective-permute-done.refs_5_), channel_id=1, source_target_pairs={{0,8},{2,10},{4,12},{6,14},{8,16},{10,18},{12,20},{14,22},{16,24},... | collective-permute-start | bytes 1572872 | tf_op jit(solution)/shard_map/ppermute | solution.py:591
  23.7 0.8 copy-start.8
  24.5 24.7 %copy-start.5 = (bf16[512,512]{1,0:T(8,128)(2,1)}, bf16[512,512]{1,0:T(8,128)(2,1)S(1)}, u32[]{:S(2)}) copy-start(bf16[512,512]{1,0:T(8,128)(2,1)S(1)} %collective-permute-done.6.refs_9_) | copy-start | bytes 1572868
  25.2 13.2 %collective-permute-start.11 = (bf16[16,512]{1,0:T(8,128)(2,1)S(1)}, bf16[16,512]{1,0:T(8,128)(2,1)S(1)}, u32[]{:S(2)}, u32[]{:S(2)}) collective-permute-start(bf16[16,512]{1,0:T(8,128)(2,1)S(1)} %fusion), channel_id=1, source_target_pairs={{0,16},{2,18},{4,20},{6,22},{8,24},{10,26},{12,28},{14,30},{16,0},... | collective-permute-start | bytes 49160 | tf_op jit(solution)/shard_map/ppermute | solution.py:591
  25.9 23.2 %collective-permute-start.2 = (bf16[512,512]{1,0:T(8,128)(2,1)S(1)}, bf16[512,512]{1,0:T(8,128)(2,1)}, u32[]{:S(2)}, u32[]{:S(2)}) collective-permute-start(bf16[512,512]{1,0:T(8,128)(2,1)S(1)} %collective-permute-done.refs_5_), channel_id=1, source_target_pairs={{0,4},{2,6},{4,0},{6,2},{8,12},{10,14},{12,8},{14,10},{16,20},{18,... | collective-permute-start | bytes 1572872 | tf_op jit(solution)/shard_map/ppermute | solution.py:591
  27.4 26.7 %collective-permute-start.7 = (bf16[512,512]{1,0:T(8,128)(2,1)S(1)}, bf16[512,512]{1,0:T(8,128)(2,1)}, u32[]{:S(2)}, u32[]{:S(2)}) collective-permute-start(bf16[512,512]{1,0:T(8,128)(2,1)S(1)} %collective-permute-done.refs_5_), channel_id=1, source_target_pairs={{0,2},{2,0},{4,6},{6,4},{8,10},{10,8},{12,14},{14,12},{16,18},{18,... | collective-permute-start | bytes 1572872 | tf_op jit(solution)/shard_map/ppermute | solution.py:591
  37.8 16.8 %collective-permute-start.13 = (bf16[512,256]{1,0:T(8,128)(2,1)S(1)}, bf16[512,256]{1,0:T(8,128)(2,1)}, u32[]{:S(2)}, u32[]{:S(2)}) collective-permute-start(bf16[512,256]{1,0:T(8,128)(2,1)S(1)} %slice.28), channel_id=1, source_target_pairs={{0,4},{2,6},{4,0},{6,2},{8,12},{10,14},{12,8},{14,10},{16,20},{18,... | collective-permute-start | bytes 786440 | tf_op jit(solution)/shard_map/ppermute | solution.py:591
  38.4 10.8 %copy-start.6 = (bf16[16,512]{1,0:T(8,128)(2,1)}, bf16[16,512]{1,0:T(8,128)(2,1)S(1)}, u32[]{:S(2)}) copy-start(bf16[16,512]{1,0:T(8,128)(2,1)S(1)} %broadcast_select_fusion.refs_13_) | copy-start | bytes 49156
  38.4 15.7 %collective-permute-start.12 = (bf16[16,512]{1,0:T(8,128)(2,1)S(1)}, bf16[16,512]{1,0:T(8,128)(2,1)S(1)}, u32[]{:S(2)}, u32[]{:S(2)}) collective-permute-start(bf16[16,512]{1,0:T(8,128)(2,1)S(1)} %broadcast_select_fusion.refs_13_), channel_id=1, source_target_pairs={{0,8},{2,10},{4,12},{6,14},{8,16},{10,18},{12,20},{14,22},{16,24},... | collective-permute-start | bytes 49160 | tf_op jit(solution)/shard_map/ppermute | solution.py:591
  50.8 17.1 %collective-permute-start.8 = (bf16[512,256]{1,0:T(8,128)(2,1)}, bf16[512,256]{1,0:T(8,128)(2,1)}, u32[]{:S(2)}, u32[]{:S(2)}) collective-permute-start(bf16[512,256]{1,0:T(8,128)(2,1)} %slice.24), channel_id=1, source_target_pairs={{0,8},{2,10},{4,12},{6,14},{8,16},{10,18},{12,20},{14,22},{16,24},... | collective-permute-start | bytes 786440 | tf_op jit(solution)/shard_map/ppermute | solution.py:591
  54.1 14.8 %collective-permute-start.3 = (bf16[512,512]{1,0:T(8,128)(2,1)}, bf16[512,512]{1,0:T(8,128)(2,1)}, u32[]{:S(2)}, u32[]{:S(2)}) collective-permute-start(bf16[512,512]{1,0:T(8,128)(2,1)} %collective-permute-done.2.refs_5_), channel_id=1, source_target_pairs={{0,2},{2,0},{4,6},{6,4},{8,10},{10,8},{12,14},{14,12},{16,18},{18,... | collective-permute-start | bytes 1572872 | tf_op jit(solution)/shard_map/ppermute | solution.py:591
  54.1 13.8 %copy-start.7 = (bf16[16,512]{1,0:T(8,128)(2,1)}, bf16[16,512]{1,0:T(8,128)(2,1)S(1)}, u32[]{:S(2)}) copy-start(bf16[16,512]{1,0:T(8,128)(2,1)S(1)} %collective-permute-done.12.refs_14_) | copy-start | bytes 49156
  54.1 14.7 %collective-permute-start.4 = (bf16[512,512]{1,0:T(8,128)(2,1)}, bf16[512,512]{1,0:T(8,128)(2,1)}, u32[]{:S(2)}, u32[]{:S(2)}) collective-permute-start(bf16[512,512]{1,0:T(8,128)(2,1)} %collective-permute-done.1.refs_4_), channel_id=1, source_target_pairs={{0,2},{2,0},{4,6},{6,4},{8,10},{10,8},{12,14},{14,12},{16,18},{18,... | collective-permute-start | bytes 1572872 | tf_op jit(solution)/shard_map/ppermute | solution.py:591
  54.6 14.2 %collective-permute-start.14 = (bf16[512,256]{1,0:T(8,128)(2,1)}, bf16[512,256]{1,0:T(8,128)(2,1)}, u32[]{:S(2)}, u32[]{:S(2)}) collective-permute-start(bf16[512,256]{1,0:T(8,128)(2,1)} %collective-permute-done.13.refs_11_), channel_id=1, source_target_pairs={{0,2},{2,0},{4,6},{6,4},{8,10},{10,8},{12,14},{14,12},{16,18},{18,... | collective-permute-start | bytes 786440 | tf_op jit(solution)/shard_map/ppermute | solution.py:591
  54.7 44.9 %collective-permute-start.18 = (bf16[1024,1024]{1,0:T(8,128)(2,1)}, bf16[1024,1024]{1,0:T(8,128)(2,1)}, u32[]{:S(2)}, u32[]{:S(2)}) collective-permute-start(bf16[1024,1024]{1,0:T(8,128)(2,1)} %collective-permute-done.17.refs_5_), channel_id=1, source_target_pairs={{0,2},{2,0},{4,6},{6,4},{8,10},{10,8},{12,14},{14,12},{16,18},{18,... | collective-permute-start | bytes 6291464 | tf_op jit(solution)/shard_map/ppermute | solution.py:591
  67.9 11.2 %collective-permute-start.9 = (bf16[512,256]{1,0:T(8,128)(2,1)}, bf16[512,256]{1,0:T(8,128)(2,1)}, u32[]{:S(2)}, u32[]{:S(2)}) collective-permute-start(bf16[512,256]{1,0:T(8,128)(2,1)} %collective-permute-done.8.refs_11_), channel_id=1, source_target_pairs={{0,2},{2,0},{4,6},{6,4},{8,10},{10,8},{12,14},{14,12},{16,18},{18,... | collective-permute-start | bytes 786440 | tf_op jit(solution)/shard_map/ppermute | solution.py:591
  78.8 9.6 %copy-start = (s32[8]{0:T(128)S(1)}, s32[8]{0:T(128)}, u32[]{:S(2)}) copy-start(s32[8]{0:T(128)} %refs_0_.7) | copy-start | bytes 100
  78.8 9.6 %copy-start.1 = (s32[8]{0:T(128)S(1)}, s32[8]{0:T(128)}, u32[]{:S(2)}) copy-start(s32[8]{0:T(128)} %refs_1_.7) | copy-start | bytes 100
  78.8 9.6 %copy-start.2 = (f32[8]{0:T(128)S(1)}, f32[8]{0:T(128)}, u32[]{:S(2)}) copy-start(f32[8]{0:T(128)} %refs_2_.7) | copy-start | bytes 100
  78.8 20.7 %collective-permute-start.15 = (bf16[512,512]{1,0:T(8,128)(2,1)}, bf16[512,512]{1,0:T(8,128)(2,1)}, u32[]{:S(2)}, u32[]{:S(2)}) collective-permute-start(bf16[512,512]{1,0:T(8,128)(2,1)} %attend.6.refs_0_), channel_id=1, source_target_pairs={{0,1},{1,0},{2,3},{3,2},{4,5},{5,4},{6,7},{7,6},{8,9},{9,8},{10,11... | collective-permute-start | bytes 1572872 | tf_op jit(solution)/shard_map/ppermute | solution.py:591
  87.4 12.1 %collective-permute-start.16 = (bf16[512,256]{1,0:T(8,128)(2,1)}, bf16[512,256]{1,0:T(8,128)(2,1)S(1)}, u32[]{:S(2)}, u32[]{:S(2)}) collective-permute-start(bf16[512,256]{1,0:T(8,128)(2,1)} %attend.7.refs_1_), channel_id=1, source_target_pairs={{0,1},{1,0},{2,3},{3,2},{4,5},{5,4},{6,7},{7,6},{8,9},{9,8},{10,11... | collective-permute-start | bytes 786440 | tf_op jit(solution)/shard_map/ppermute | solution.py:591
  93.2 6.3 %copy-start.3 = (bf16[512,256]{1,0:T(8,128)(2,1)}, bf16[512,256]{1,0:T(8,128)(2,1)S(1)}, u32[]{:S(2)}) copy-start(bf16[512,256]{1,0:T(8,128)(2,1)S(1)} %get-tuple-element.21.refs_2_) | copy-start | bytes 786436
  93.2 12.4 %collective-permute-start.19 = (bf16[512,256]{1,0:T(8,128)(2,1)S(1)}, bf16[512,256]{1,0:T(8,128)(2,1)S(1)}, u32[]{:S(2)}, u32[]{:S(2)}) collective-permute-start(bf16[512,256]{1,0:T(8,128)(2,1)S(1)} %get-tuple-element.21.refs_2_), channel_id=1, source_target_pairs={{0,1},{1,0},{2,3},{3,2},{4,5},{5,4},{6,7},{7,6},{8,9},{9,8},{10,11... | collective-permute-start | bytes 786440 | tf_op jit(solution)/shard_map/ppermute | solution.py:591
  99.5 0.7 copy-start.10
